TPU v7x, 32 devices: a whole 2x2x4 slice. The times are simulated.
32 devices in a mesh: dp: 4 (over y, x), tensor: 8 (over z, core).
Axes of the slice: x: 2, y: 2, z: 4, core: 2. Of those that a mesh axis runs over, the one named last changes fastest.
Arguments:
- tokens: bfloat16 [512, 8192], P('dp', 'tensor'), may hold values from -6 to 6
- cotangent: bfloat16 [512, 8192], P('dp', 'tensor'), may hold values from -6 to 6
- up_blocks: bfloat16 [64, 6, 256, 256], P('tensor'), may hold values from -0.15625 to 0.15625
- down_blocks: bfloat16 [64, 6, 256, 256], P('tensor'), may hold values from -0.109375 to 0.109375
- up_left: bfloat16 [8192, 256], P('tensor'), may hold values from -0.0625 to 0.0625
- up_right: bfloat16 [256, 16384], P(None, 'tensor'), may hold values from -0.375 to 0.375
- down_left: bfloat16 [16384, 256], P('tensor'), may hold values from -0.046875 to 0.046875
- down_right: bfloat16 [256, 8192], P(None, 'tensor'), may hold values from -0.375 to 0.375
Outputs:
- layer_out: bfloat16 [512, 8192], P('dp', 'tensor')
- token_grads: bfloat16 [512, 8192], P('dp', 'tensor')
- grad_up_blocks: bfloat16 [64, 6, 256, 256], P('tensor', None, 'dp')
- grad_down_blocks: bfloat16 [64, 6, 256, 256], P('tensor', None, 'dp')
- grad_up_left: bfloat16 [8192, 256], P('tensor', 'dp')
- grad_up_right: bfloat16 [256, 16384], P('dp', 'tensor')
- grad_down_left: bfloat16 [16384, 256], P('tensor', 'dp')
- grad_down_right: bfloat16 [256, 8192], P('dp', 'tensor')
All inputs are finite; a program needn't handle non-finite values.
Results may differ from a plain program's by a relative error of at most 0.018.
Values may be sent and summed in bfloat16 or wider, within the bound.
No kernel may reach another device: no remote copies, remote signals or barrier semaphores. Data moves between devices by JAX's collectives and lax.ppermute only.
A program may use at most 128 MiB of HBM per device.

v0:
```python
import math

import jax
import jax.numpy as jnp
from jax import lax
from jax.sharding import PartitionSpec as P

BLK = 256


butterfly_strides = (0, 1, 2, 4, 8, 16)
root_coef = math.sqrt(2.0 / math.pi)
cubic_coef = 0.044715


def swapped(x, axis, bit):
    return lax.ppermute(x, axis, [(i, i ^ 1 << bit) for i in range(lax.axis_size(axis))])


def gelu_value(value):
    inner = root_coef * (value + cubic_coef * value * value * value)
    return 0.5 * value * (1.0 + jnp.tanh(inner))


def gelu_slope(value):
    tanh_val = jnp.tanh(root_coef * (value + cubic_coef * value * value * value))
    return 0.5 * (1.0 + tanh_val) + 0.5 * value * (1.0 - tanh_val * tanh_val) * root_coef * (
        1.0 + 3.0 * cubic_coef * value * value
    )


def flip_local(local, stride):
    rows, blocks, width = local.shape
    split = local.reshape(rows, blocks // (2 * stride), 2, stride, width)
    return split[:, :, ::-1].reshape(rows, blocks, width)


def hop_paired(local, stride):
    blocks = local.shape[1]
    if stride == 0:
        return local
    if stride < blocks:
        return flip_local(local, stride)
    bit_pos = (stride // blocks).bit_length() - 1
    return swapped(local, "tensor", bit_pos)


def hop_partial(local, stride):
    blocks = local.shape[1]
    if stride == 0:
        return local
    if stride < blocks:
        return flip_local(local, stride)
    bit_pos = (stride // blocks).bit_length() - 1
    return swapped(local, "tensor", bit_pos)


def paired_stack(local):
    return jnp.stack([hop_paired(local, stride) for stride in butterfly_strides], axis=2)


def partner_total(parts):
    total = None
    for factor, stride in enumerate(butterfly_strides):
        piece = hop_partial(parts[:, :, factor], stride)
        total = piece if total is None else total + piece
    return total


def shards(tokens, cotangent, up_blocks, down_blocks, up_left, up_right, down_left, down_right):
    f32 = jnp.float32
    bf16 = jnp.bfloat16
    rows, local_width = tokens.shape
    blocks = local_width // BLK
    hidden_local = up_blocks.shape[0]
    ratio = hidden_local // blocks
    factors = len(butterfly_strides)
    scale = 1.0 / math.sqrt(rows * lax.axis_size("dp"))
    up_w = up_blocks.reshape(blocks, ratio, factors, BLK, BLK)
    down_w = down_blocks.reshape(blocks, ratio, factors, BLK, BLK)
    joined = jnp.concatenate((tokens, cotangent), axis=0).reshape(2 * rows, blocks, BLK)
    both_blocks = paired_stack(joined)
    tok_blocks = both_blocks[:rows]
    cot_blocks = both_blocks[rows:]
    up_part = jnp.dot(tokens, up_left, preferred_element_type=f32)
    lat_sum = lax.psum(up_part, "tensor")
    lat_up = lat_sum.astype(bf16)
    pre_act = jnp.einsum("tijb,irjbc->tirc", tok_blocks, up_w, preferred_element_type=f32)
    pre_act = pre_act.reshape(rows, hidden_local * BLK) + jnp.dot(
        lat_up, up_right, preferred_element_type=f32
    )
    act_out = gelu_value(pre_act).astype(bf16)
    lat_down = lax.psum(jnp.dot(act_out, down_left, preferred_element_type=f32), "tensor").astype(
        bf16
    )
    act_four = act_out.reshape(rows, blocks, ratio, BLK)
    parts = jnp.einsum("tirc,irjcb->tijb", act_four, down_w, preferred_element_type=f32)
    out_sum = partner_total(parts).reshape(rows, local_width)
    layer_out = (out_sum + jnp.dot(lat_down, down_right, preferred_element_type=f32)).astype(bf16)
    cot_part = jnp.einsum("td,rd->tr", cotangent, down_right, preferred_element_type=f32)
    lat_cot = lax.psum(cot_part, "tensor").astype(bf16)
    act_grad = jnp.einsum("tijb,irjcb->tirc", cot_blocks, down_w, preferred_element_type=f32)
    act_grad = act_grad.reshape(rows, hidden_local * BLK) + jnp.einsum(
        "tr,fr->tf", lat_cot, down_left, preferred_element_type=f32
    )
    pre_grad = (act_grad * gelu_slope(pre_act)).astype(bf16)
    grad_down = jnp.einsum("tirc,tijb->irjcb", act_four, cot_blocks, preferred_element_type=f32)
    grad_down = grad_down.reshape(hidden_local, factors, BLK, BLK) * scale
    grad_dl = jnp.einsum("tf,tr->fr", act_out, lat_cot, preferred_element_type=f32) * scale
    grad_dr = jnp.einsum("tr,td->rd", lat_down, cotangent, preferred_element_type=f32) * scale
    pre_part = jnp.einsum("tf,rf->tr", pre_grad, up_right, preferred_element_type=f32)
    lat_pre = lax.psum(pre_part, "tensor").astype(bf16)
    pre_four = pre_grad.reshape(rows, blocks, ratio, BLK)
    back_parts = jnp.einsum("tirc,irjbc->tijb", pre_four, up_w, preferred_element_type=f32)
    back_sum = partner_total(back_parts).reshape(rows, local_width)
    token_grads = (
        back_sum + jnp.einsum("tr,dr->td", lat_pre, up_left, preferred_element_type=f32)
    ).astype(bf16)
    grad_up = jnp.einsum("tijb,tirc->irjbc", tok_blocks, pre_four, preferred_element_type=f32)
    grad_up = grad_up.reshape(hidden_local, factors, BLK, BLK) * scale
    grad_ul = jnp.einsum("td,tr->dr", tokens, lat_pre, preferred_element_type=f32) * scale
    grad_ur = jnp.einsum("tr,tf->rf", lat_up, pre_grad, preferred_element_type=f32) * scale
    summed = (
        lax.psum_scatter(
            grad_up.astype(jnp.bfloat16), "dp", scatter_dimension=2, tiled=True
        ).astype(jnp.float32),
        lax.psum_scatter(
            grad_down.astype(jnp.bfloat16), "dp", scatter_dimension=2, tiled=True
        ).astype(jnp.float32),
        lax.psum_scatter(
            grad_ul.astype(jnp.bfloat16), "dp", scatter_dimension=1, tiled=True
        ).astype(jnp.float32),
        lax.psum_scatter(
            grad_ur.astype(jnp.bfloat16), "dp", scatter_dimension=0, tiled=True
        ).astype(jnp.float32),
        lax.psum_scatter(
            grad_dl.astype(jnp.bfloat16), "dp", scatter_dimension=1, tiled=True
        ).astype(jnp.float32),
        lax.psum_scatter(
            grad_dr.astype(jnp.bfloat16), "dp", scatter_dimension=0, tiled=True
        ).astype(jnp.float32),
    )
    return (
        layer_out,
        token_grads,
        summed[0].astype(bf16),
        summed[1].astype(bf16),
        summed[2].astype(bf16),
        summed[3].astype(bf16),
        summed[4].astype(bf16),
        summed[5].astype(bf16),
    )


def solution(mesh):
    in_specs = (
        P("dp", "tensor"),
        P("dp", "tensor"),
        P("tensor", None, None, None),
        P("tensor", None, None, None),
        P("tensor", None),
        P(None, "tensor"),
        P("tensor", None),
        P(None, "tensor"),
    )
    out_specs = (
        P("dp", "tensor"),
        P("dp", "tensor"),
        P("tensor", None, "dp", None),
        P("tensor", None, "dp", None),
        P("tensor", "dp"),
        P("dp", "tensor"),
        P("tensor", "dp"),
        P("dp", "tensor"),
    )
    return jax.shard_map(shards, mesh=mesh, in_specs=in_specs, out_specs=out_specs, check_vma=False)
```

profile of v0, /device:TPU:0, one launch (start us, length us, event | category | flops | bytes accessed | tf_op | source)
XLA Modules:
  0.0 389.0 jit_solution(9207740805487690796)
XLA Ops:
  8.5 1.8 copy.36
  12.4 4.1 %collective-permute-start.2 = (bf16[256,4,256]{2,0,1:T(8,128)(2,1)}, bf16[256,4,256]{2,0,1:T(8,128)(2,1)}, u32[]{:S(2)}, u32[]{:S(2)}) collective-permute-start(bf16[256,4,256]{2,0,1:T(8,128)(2,1)} %copy.39), channel_id=1, source_target_pairs={{0,4},{1,5},{2,6},{3,7},{4,0},{5,1},{6,2},{7,3},{8,12},{9,13},{10,... | collective-permute-start | bytes 1572872 | tf_op jit(solution)/shard_map/ppermute | solution.py:17
  16.4 1.6 collective-permute-start.1
  22.8 42.6 %all-reduce.4 = (bf16[128,256]{1,0:T(8,128)(2,1)S(1)}, bf16[128,256]{1,0:T(8,128)(2,1)S(1)}) all-reduce(f32[128,256]{1,0:T(8,128)S(1)} %fusion.50, f32[128,256]{1,0:T(8,128)S(1)} %fusion.52), channel_id=1, replica_groups=mesh['dp'=4,'tensor'=8] {'tensor'}, use_global_device_ids=true, to_apply=%region_0.0 | all-reduce | flops 65536 | bytes 393216 | tf_op jit(solution)/shard_map/psum | solution.py:86
  66.3 1.9 bitcast_dynamic-update-slice_fusion.2
  68.2 1.9 bitcast_dynamic-update-slice_fusion.1
  70.0 1.9 bitcast_dynamic-update-slice_fusion
  71.9 5.4 %fusion.15 = f32[128,4,2,256]{3,0,2,1:T(8,128)S(1)} fusion(bf16[4,2,6,256,256]{4,3,2,1,0:T(8,128)(2,1)} %bitcast.171, bf16[256,4,6,256]{3,0,2,1:T(8,128)(2,1)} %bitcast_dynamic-update-slice_fusion), kind=kOutput, calls=%fused_computation.23 | convolution fusion | flops 805306368 | bytes 8912896 | tf_op jit(solution)/shard_map/tijb,irjcb->tirc/dot_general | solution.py:102
  78.1 1.8 reshape.71
  80.0 4.3 %convolution_bitcast_fusion.1 = f32[128,4,2,256]{3,0,2,1:T(8,128)S(1)} fusion(bf16[4,2,6,256,256]{4,3,2,1,0:T(8,128)(2,1)} %bitcast.161, bf16[256,4,6,256]{3,0,2,1:T(8,128)(2,1)} %bitcast_dynamic-update-slice_fusion), kind=kOutput, calls=%fused_computation.24 | convolution fusion | flops 805306368 | bytes 8912896 | tf_op jit(solution)/shard_map/tijb,irjbc->tirc/dot_general | solution.py:88
  85.5 1.6 copy.44
  90.3 29.0 %all-reduce.5 = (bf16[128,256]{1,0:T(8,128)(2,1)S(1)}, bf16[128,256]{1,0:T(8,128)(2,1)S(1)}) all-reduce(f32[128,256]{1,0:T(8,128)S(1)} %fusion.51, f32[128,256]{1,0:T(8,128)S(1)} %fusion.53), channel_id=1, replica_groups=mesh['dp'=4,'tensor'=8] {'tensor'}, use_global_device_ids=true, to_apply=%region_1.0 | all-reduce | flops 65536 | bytes 393216 | tf_op jit(solution)/shard_map/psum | solution.py:93
  121.8 1.4 fusion.3
  123.3 1.4 fusion.4
  125.9 5.8 %multiply_convert_fusion.1 = bf16[4,2,256,6,256]{4,2,3,1,0:T(8,128)(2,1)} fusion(bf16[128,4,2,256,1]{0,3,4,2,1:T(8,128)(2,1)S(1)} %copy.73, bf16[256,4,6,256]{3,0,2,1:T(8,128)(2,1)} %bitcast_dynamic-update-slice_fusion), kind=kOutput, calls=%fused_computation.1 | convolution fusion | flops 811597824 | bytes 8388608 | tf_op jit(solution)/shard_map/tijb,tirc->irjbc/dot_general | solution.py:119
  131.7 8.6 %copy.61 = bf16[8,6,256,256]{3,2,1,0:T(8,128)(2,1)} copy(bf16[8,6,256,256]{2,3,1,0:T(8,128)(2,1)} %bitcast.166) | data formatting | bytes 12582912 | tf_op jit(solution)/shard_map/convert_element_type | solution.py:125
  140.8 5.8 %fusion = bf16[4,2,6,256,256]{3,4,1,2,0:T(8,128)(2,1)} fusion(bf16[256,4,6,256]{3,0,2,1:T(8,128)(2,1)} %bitcast_dynamic-update-slice_fusion, bf16[128,4,2,256,1]{3,2,1,0,4:T(2,128)(2,1)S(1)} %bitcast.174), kind=kOutput, calls=%fused_computation.2 | convolution fusion | flops 811597824 | bytes 8388608 | tf_op jit(solution)/shard_map/tirc,tijb->irjcb/dot_general | solution.py:107
  146.7 8.7 %copy.64 = bf16[4,2,6,256,256]{4,3,2,1,0:T(8,128)(2,1)} copy(bf16[4,2,6,256,256]{3,4,1,2,0:T(8,128)(2,1)} %fusion) | data formatting | bytes 12582912 | tf_op jit(solution)/shard_map/convert_element_type | solution.py:128
  155.3 4.0 %fusion.7 = f32[128,4,6,256]{3,0,2,1:T(8,128)S(1)} fusion(bf16[4,2,6,256,256]{4,3,2,1,0:T(8,128)(2,1)} %bitcast.172, bf16[128,4,2,256,1]{3,2,1,0,4:T(2,128)(2,1)S(1)} %bitcast.175), kind=kOutput, calls=%fused_computation.14 | convolution fusion | flops 805306368 | bytes 9961472 | tf_op jit(solution)/shard_map/tirc,irjcb->tijb/dot_general | solution.py:97
  159.3 1.6 fusion.49
  161.6 2.2 convolution_bitcast_fusion
  168.8 2.0 collective-permute-start.7
  172.1 17.0 %collective-permute-done.5 = f32[128,4,256]{2,0,1:T(8,128)} collective-permute-done((f32[128,4,256]{2,0,1:T(8,128)}, f32[128,4,256]{2,0,1:T(8,128)}, u32[]{:S(2)}, u32[]{:S(2)}) %collective-permute-start.5) | collective-permute-done | bytes 524320 | tf_op jit(solution)/shard_map/ppermute | solution.py:17
  189.0 1.4 collective-permute-done.4
  190.4 2.5 fusion.35
  195.2 15.7 %collective-permute-done.8 = f32[128,4,256]{2,0,1:T(8,128)} collective-permute-done((f32[128,4,256]{2,0,1:T(8,128)}, f32[128,4,256]{2,0,1:T(8,128)}, u32[]{:S(2)}, u32[]{:S(2)}) %collective-permute-start.8) | collective-permute-done | bytes 524320 | tf_op jit(solution)/shard_map/ppermute | solution.py:17
  210.9 1.4 collective-permute-done.7
  212.3 2.6 fusion.30
  216.4 2.0 add_convert_fusion
  218.3 16.9 %reduce-scatter.15.cloned.1.call-done = bf16[2048,64]{0,1:T(8,128)(2,1)} async-done(((bf16[2048,256]{0,1:T(8,128)(2,1)}), bf16[2048,64]{0,1:T(8,128)(2,1)}) %reduce-scatter.15.cloned.1.call-update) | async-done | bytes 262160 | tf_op jit(solution)/shard_map/reduce_scatter | solution.py:136
  235.2 73.5 %reduce-scatter.7.cloned.1.call-done = bf16[8,6,64,256]{3,2,1,0:T(8,128)(2,1)} async-done(((bf16[8,6,256,256]{3,2,1,0:T(8,128)(2,1)}), bf16[8,6,64,256]{3,2,1,0:T(8,128)(2,1)}) %reduce-scatter.7.cloned.1.call-update) | async-done | bytes 1572880 | tf_op jit(solution)/shard_map/reduce_scatter | solution.py:124
  308.7 73.5 %reduce-scatter.9.cloned.1.call-done = bf16[8,6,64,256]{3,2,1,0:T(8,128)(2,1)} async-done(((bf16[8,6,256,256]{3,2,1,0:T(8,128)(2,1)}), bf16[8,6,64,256]{3,2,1,0:T(8,128)(2,1)}) %reduce-scatter.9.cloned.1.call-update) | async-done | bytes 1572880 | tf_op jit(solution)/shard_map/reduce_scatter | solution.py:127
  (90 shorter events, 28.9 us)
Async XLA Ops:
  7.2 79.9 %copy-start = (bf16[256,2048]{1,0:T(8,128)(2,1)S(1)}, bf16[256,2048]{1,0:T(8,128)(2,1)}, u32[]{:S(2)}) copy-start(bf16[256,2048]{1,0:T(8,128)(2,1)} %param.13) | copy-start | bytes 3145732
  7.2 10.8 %copy-start.5 = (bf16[128,1024]{1,0:T(8,128)(2,1)S(1)}, bf16[128,1024]{1,0:T(8,128)(2,1)}, u32[]{:S(2)}) copy-start(bf16[128,1024]{1,0:T(8,128)(2,1)} %param.8) | copy-start | bytes 786436
  7.2 11.1 %copy-start.4 = (bf16[128,1024]{1,0:T(8,128)(2,1)S(1)}, bf16[128,1024]{1,0:T(8,128)(2,1)}, u32[]{:S(2)}) copy-start(bf16[128,1024]{1,0:T(8,128)(2,1)} %param.9) | copy-start | bytes 786436
  7.2 10.8 %copy-start.9 = (bf16[1024,256]{1,0:T(8,128)(2,1)S(1)}, bf16[1024,256]{1,0:T(8,128)(2,1)}, u32[]{:S(2)}) copy-start(bf16[1024,256]{1,0:T(8,128)(2,1)} %param.12) | copy-start | bytes 1572868
  7.2 11.0 %copy-start.7 = (bf16[256,1024]{1,0:T(8,128)(2,1)S(1)}, bf16[256,1024]{1,0:T(8,128)(2,1)}, u32[]{:S(2)}) copy-start(bf16[256,1024]{1,0:T(8,128)(2,1)} %param.15) | copy-start | bytes 1572868
  7.2 211.1 %reduce-scatter.17.cloned.1.call-start = ((), (), s32[]{:S(2)}) async-start(), calls=%async_computation.11 | async-start | bytes 655360 | tf_op jit(solution)/shard_map/reduce_scatter | solution.py:139
  12.4 57.7 %collective-permute-start.2 = (bf16[256,4,256]{2,0,1:T(8,128)(2,1)}, bf16[256,4,256]{2,0,1:T(8,128)(2,1)}, u32[]{:S(2)}, u32[]{:S(2)}) collective-permute-start(bf16[256,4,256]{2,0,1:T(8,128)(2,1)} %copy.39), channel_id=1, source_target_pairs={{0,4},{1,5},{2,6},{3,7},{4,0},{5,1},{6,2},{7,3},{8,12},{9,13},{10,... | collective-permute-start | bytes 1572872 | tf_op jit(solution)/shard_map/ppermute | solution.py:17
  16.4 51.7 %collective-permute-start.1 = (bf16[256,4,256]{2,0,1:T(8,128)(2,1)}, bf16[256,4,256]{2,0,1:T(8,128)(2,1)}, u32[]{:S(2)}, u32[]{:S(2)}) collective-permute-start(bf16[256,4,256]{2,0,1:T(8,128)(2,1)} %copy.39), channel_id=1, source_target_pairs={{0,2},{1,3},{2,0},{3,1},{4,6},{5,7},{6,4},{7,5},{8,10},{9,11},{10,... | collective-permute-start | bytes 1572872 | tf_op jit(solution)/shard_map/ppermute | solution.py:17
  18.0 48.3 %collective-permute-start = (bf16[256,4,256]{2,0,1:T(8,128)(2,1)}, bf16[256,4,256]{2,0,1:T(8,128)(2,1)}, u32[]{:S(2)}, u32[]{:S(2)}) collective-permute-start(bf16[256,4,256]{2,0,1:T(8,128)(2,1)} %copy.39), channel_id=1, source_target_pairs={{0,1},{1,0},{2,3},{3,2},{4,5},{5,4},{6,7},{7,6},{8,9},{9,8},{10,11... | collective-permute-start | bytes 1572872 | tf_op jit(solution)/shard_map/ppermute | solution.py:17
  87.1 1.2 copy-start.10
  87.1 1.5 copy-start.11
  120.5 97.8 %reduce-scatter.11.cloned.1.call-start = ((), (), s32[]{:S(2)}) async-start(), calls=%async_computation.8 | async-start | bytes 655360 | tf_op jit(solution)/shard_map/reduce_scatter | solution.py:130
  121.7 96.6 %reduce-scatter.13.cloned.1.call-start = ((), (), s32[]{:S(2)}) async-start(), calls=%async_computation.9 | async-start | bytes 1310720 | tf_op jit(solution)/shard_map/reduce_scatter | solution.py:133
  123.2 112.0 %reduce-scatter.15.cloned.1.call-start = ((), (), s32[]{:S(2)}) async-start(), calls=%async_computation.10 | async-start | bytes 1310720 | tf_op jit(solution)/shard_map/reduce_scatter | solution.py:136
  124.8 184.0 %reduce-scatter.7.cloned.1.call-start = ((), (), s32[]{:S(2)}) async-start(), calls=%async_computation.6 | async-start | bytes 7864320 | tf_op jit(solution)/shard_map/reduce_scatter | solution.py:124
  140.4 241.8 %reduce-scatter.9.cloned.1.call-start = ((), (), s32[]{:S(2)}) async-start(), calls=%async_computation.7 | async-start | bytes 7864320 | tf_op jit(solution)/shard_map/reduce_scatter | solution.py:127
  155.3 6.3 %slice-start = ((s8[6291456]{0:T(1024)(128)(4,1)}), s8[2097152]{0:T(1024)(128)(4,1)S(1)}, s32[]{:S(2)}) async-start(s8[6291456]{0:T(1024)(128)(4,1)} %bitcast.162), calls=%async_computation.12 | async-start | bytes 4194304
  155.3 6.3 %slice-start.1 = ((s8[6291456]{0:T(1024)(128)(4,1)}), s8[4194304]{0:T(1024)(128)(4,1)S(1)}, s32[]{:S(2)}) async-start(s8[6291456]{0:T(1024)(128)(4,1)} %bitcast.162), calls=%async_computation.13 | async-start | bytes 8388608
  159.3 2.3 copy-start.3
  161.6 7.2 %collective-permute-start.3 = (f32[128,4,256]{2,0,1:T(8,128)}, f32[128,4,256]{2,0,1:T(8,128)}, u32[]{:S(2)}, u32[]{:S(2)}) collective-permute-start(f32[128,4,256]{2,0,1:T(8,128)} %get-tuple-element.18), channel_id=1, source_target_pairs={{0,1},{1,0},{2,3},{3,2},{4,5},{5,4},{6,7},{7,6},{8,9},{9,8},{10,11... | collective-permute-start | bytes 1572872 | tf_op jit(solution)/shard_map/ppermute | solution.py:17
  163.8 1.6 copy-start.2
  163.8 25.2 %collective-permute-start.5 = (f32[128,4,256]{2,0,1:T(8,128)}, f32[128,4,256]{2,0,1:T(8,128)}, u32[]{:S(2)}, u32[]{:S(2)}) collective-permute-start(f32[128,4,256]{2,0,1:T(8,128)} %get-tuple-element.19), channel_id=1, source_target_pairs={{0,4},{1,5},{2,6},{3,7},{4,0},{5,1},{6,2},{7,3},{8,12},{9,13},{10,... | collective-permute-start | bytes 1572872 | tf_op jit(solution)/shard_map/ppermute | solution.py:17
  163.9 2.8 copy-start.6
  163.9 26.5 %collective-permute-start.4 = (f32[128,4,256]{2,0,1:T(8,128)}, f32[128,4,256]{2,0,1:T(8,128)}, u32[]{:S(2)}, u32[]{:S(2)}) collective-permute-start(f32[128,4,256]{2,0,1:T(8,128)} %get-tuple-element.21), channel_id=1, source_target_pairs={{0,2},{1,3},{2,0},{3,1},{4,6},{5,7},{6,4},{7,5},{8,10},{9,11},{10,... | collective-permute-start | bytes 1572872 | tf_op jit(solution)/shard_map/ppermute | solution.py:17
  166.7 1.8 copy-start.8
  166.9 28.3 %collective-permute-start.6 = (f32[128,4,256]{2,0,1:T(8,128)}, f32[128,4,256]{2,0,1:T(8,128)}, u32[]{:S(2)}, u32[]{:S(2)}) collective-permute-start(f32[128,4,256]{2,0,1:T(8,128)} %get-tuple-element.13), channel_id=1, source_target_pairs={{0,1},{1,0},{2,3},{3,2},{4,5},{5,4},{6,7},{7,6},{8,9},{9,8},{10,11... | collective-permute-start | bytes 1572872 | tf_op jit(solution)/shard_map/ppermute | solution.py:17
  167.4 43.4 %collective-permute-start.8 = (f32[128,4,256]{2,0,1:T(8,128)}, f32[128,4,256]{2,0,1:T(8,128)}, u32[]{:S(2)}, u32[]{:S(2)}) collective-permute-start(f32[128,4,256]{2,0,1:T(8,128)} %get-tuple-element.14), channel_id=1, source_target_pairs={{0,4},{1,5},{2,6},{3,7},{4,0},{5,1},{6,2},{7,3},{8,12},{9,13},{10,... | collective-permute-start | bytes 1572872 | tf_op jit(solution)/shard_map/ppermute | solution.py:17
  168.8 43.6 %collective-permute-start.7 = (f32[128,4,256]{2,0,1:T(8,128)}, f32[128,4,256]{2,0,1:T(8,128)}, u32[]{:S(2)}, u32[]{:S(2)}) collective-permute-start(f32[128,4,256]{2,0,1:T(8,128)} %get-tuple-element.16), channel_id=1, source_target_pairs={{0,2},{1,3},{2,0},{3,1},{4,6},{5,7},{6,4},{7,5},{8,10},{9,11},{10,... | collective-permute-start | bytes 1572872 | tf_op jit(solution)/shard_map/ppermute | solution.py:17
  212.3 169.9 %copy-start.1 = (bf16[256,2048]{1,0:T(8,128)(2,1)S(1)}, bf16[256,2048]{1,0:T(8,128)(2,1)}, u32[]{:S(2)}) copy-start(bf16[256,2048]{1,0:T(8,128)(2,1)} %param.13) | copy-start | bytes 3145732
Sparse Core Ops, SparseCore 0:
  120.7 23.2 reduce-scatter.16
  147.4 25.0 reduce-scatter.10
  176.0 27.9 reduce-scatter.12
  207.3 27.9 reduce-scatter.14
  238.7 70.0 reduce-scatter.6
  312.1 70.0 reduce-scatter.8
where the time goes:
time: 390 us; the launch traced here: 389 us
  waiting for transfers between devices  199 us (51%)
  blocking collectives  71.6 us (18%)
  local copies, waits for them, and re-layouts  47.4 us (12%)
  matrix products  37 us (9%)
  between operations  14.5 us (4%)
  starting transfers between devices  11 us (3%)
  other arithmetic  8.07 us (2%)
    reduce_scatter x1, waiting for transfers between devices, shards(): lax.psum_scatter(grad_up.astype(jnp.bfloat16), 'dp', scatter_dimension=2,...  73.5 us
    reduce_scatter x1, waiting for transfers between devices, shards(): lax.psum_scatter(grad_down.astype(jnp.bfloat16), 'dp', scatter_dimension=...  73.5 us
    psum x1, blocking collectives, shards(): lat_sum = lax.psum(up_part, 'tensor')  42.6 us
    ppermute x9, waiting for transfers between devices, swapped(): lax.ppermute(x, axis, [(i, i ^ 1 << bit) for i in range(lax.axis_size(axi...  35.5 us
    psum x1, blocking collectives, shards(): lax.psum(jnp.dot(act_out, down_left, preferred_element_type=f32), 'tensor')  29 us
    reduce_scatter x1, waiting for transfers between devices, shards(): lax.psum_scatter(grad_dl.astype(jnp.bfloat16), 'dp', scatter_dimension=1,...  16.9 us
    unnamed x35, local copies, waits for them, and re-layouts  11.3 us
    ppermute x9, starting transfers between devices, swapped(): lax.ppermute(x, axis, [(i, i ^ 1 << bit) for i in range(lax.axis_size(axi...  10.6 us
  transfers between devices with their start and end apart: 15, of which 7 were waited for; matrix products, arithmetic and copies ran while one was open for 17% of the time, Pallas kernels for 0%

commit v1 on v0

v1 whole, which is shorter than its diff:
```python
import functools
import math

import jax
import jax.numpy as jnp
from jax import lax
from jax.experimental import pallas as pl
from jax.experimental.pallas import tpu as pltpu
from jax.sharding import PartitionSpec as P


STRIDES = (0, 1, 2, 4, 8, 16)
ROOT = math.sqrt(2.0 / math.pi)
CUBIC = 0.044715
F32 = jnp.float32
BF16 = jnp.bfloat16


def swapped(x, axis, mask):
    return lax.ppermute(x, axis, [(i, i ^ mask) for i in range(lax.axis_size(axis))])


def spread(x, order):
    got = {0: x}
    for mask in order:
        for m in list(got):
            got[m ^ mask] = swapped(got[m], "dp", mask)
    return [got[m] for m in range(len(got))]


def total(mine, other):
    def add(x, y):
        return (x.astype(F32) + y.astype(F32)).astype(BF16)

    x = add(mine, swapped(other, "tensor", 1))
    mask = lax.axis_size("tensor") // 2
    while mask > 1:
        x = add(x, swapped(x, "tensor", mask))
        mask //= 2
    return x, swapped(x, "tensor", 1)


def nn(a, b):
    return jnp.dot(a, b, preferred_element_type=F32)


def nt(a, b):
    return lax.dot_general(a, b, (((1,), (1,)), ((), ())), preferred_element_type=F32)


def cols(block, blk):
    return pl.ds(pl.multiple_of(block * blk, blk), blk)


def one_hot(rows, width, first):
    r = lax.broadcasted_iota(jnp.int32, (rows, width), 0)
    c = lax.broadcasted_iota(jnp.int32, (rows, width), 1)
    return jnp.where(c == r + first, 1.0, 0.0).astype(BF16)


def params(mib=8):
    return pltpu.CompilerParams(vmem_limit_bytes=mib * 2**20)


VM = pl.BlockSpec(memory_space=pltpu.VMEM)
HBM = pl.BlockSpec(memory_space=pl.ANY)


def halves():
    c = lax.axis_index("tensor") & 1
    return c, 1 - c


def put_halves(dst, mine, other):
    n = mine.shape[0]
    for c, ref in zip(halves(), (mine, other)):
        dst[pl.ds(pl.multiple_of(c * n, n), n), :] = ref[...]


def get_halves(src, mine, other):
    n = mine.shape[0]
    for c, ref in zip(halves(), (mine, other)):
        ref[...] = src[pl.ds(pl.multiple_of(c * n, n), n), :]


def in_hbm(x):
    return pltpu.with_memory_space_constraint(x, pltpu.HBM)


def shape(dims, dtype=BF16):
    return jax.ShapeDtypeStruct(dims, dtype)


class Copies:
    def __init__(self, sem):
        self.sem, self.count, self.out = sem, 0, []

    def start(self, src, dst):
        copy = pltpu.make_async_copy(src, dst, self.sem.at[self.count])
        self.count += 1
        copy.start()
        return copy

    def back(self, src, dst):
        self.out.append(self.start(src, dst))

    def finish(self):
        for copy in self.out:
            copy.wait()


def latent_kernel(tok, cot, ul, dr, mine, other, both, tmp, sem):
    rows = tok.shape[0]
    copies = Copies(sem)
    copies.back(tok, both.at[pl.ds(0, rows), :])
    copies.back(cot, both.at[pl.ds(rows, rows), :])
    tmp[:, :rows] = nn(tok[...], ul[...]).T.astype(BF16)
    tmp[:, rows:] = nt(dr[...], cot[...]).astype(BF16)
    get_halves(tmp, mine, other)
    copies.finish()


def latent_pass(tok, cot, ul, dr):
    rank, (rows, width) = dr.shape[0], tok.shape
    half = shape((rank // 2, 2 * rows))
    return pl.pallas_call(
        latent_kernel,
        in_specs=[VM] * 4,
        out_specs=[VM, VM, HBM],
        out_shape=[half, half, shape((2 * rows, width))],
        scratch_shapes=[pltpu.VMEM((rank, 2 * rows), BF16), pltpu.SemaphoreType.DMA((2,))],
        compiler_params=params(),
        name="kl",
    )(tok, cot, ul, dr)


def join_kernel(*refs):
    both, out, tmp, sem = refs[:-3], refs[-3], refs[-2], refs[-1]
    rows = both[0].shape[0] // 2
    copies = Copies(sem)
    spans = [pl.ds(g * rows, rows) for g in range(len(both))]
    reads = [copies.start(ref.at[pl.ds(rows, rows), :], tmp.at[g, :]) for ref, g in zip(both, spans)]
    for read, g in zip(reads, spans):
        read.wait()
        copies.back(tmp.at[g, :], out.at[g, :])
    copies.finish()


def join_pass(both):
    rows, width = both[0].shape[0] // 2, both[0].shape[1]
    dims = (len(both) * rows, width)
    return pl.pallas_call(
        join_kernel,
        in_specs=[HBM] * len(both),
        out_specs=HBM,
        out_shape=shape(dims),
        scratch_shapes=[pltpu.VMEM(dims, BF16), pltpu.SemaphoreType.DMA((2 * len(both),))],
        compiler_params=params(),
        name="kj",
    )(*both)


def half_kernel(back, near, n, ratio, blk, *refs):
    take = iter(refs)
    x_in = [next(take) for _ in range(1 + n)]
    lat_mine, lat_other, up, down, ur, dl = (next(take) for _ in range(6))
    slope_in, lat_down = (next(take), next(take)) if back else (None, None)
    act_out = next(take)
    slope_out = None if back else next(take)
    here_out = next(take)
    parts_out = [next(take) for _ in range(n)]
    lat_outs = [next(take) for _ in range(2 if back else 1)]
    xs = [next(take) for _ in range(1 + n)]
    lat, up_v, down_v, ur_v, dl_v, slope = (next(take) for _ in range(6))
    act, here = next(take), next(take)
    parts = [next(take) for _ in range(n)]
    lat_tmp, sem = next(take), next(take)
    rows, width = x_in[0].shape
    blocks = width // blk
    half = lat_mine.shape[0]
    copies = Copies(sem)

    def lat_half(src, c):
        return copies.start(src, lat.at[pl.ds(pl.multiple_of(c * half, half), half), :])

    first = [lat_half(src, c) for src, c in zip((lat_mine, lat_other), halves())]
    first += [copies.start(src, dst) for src, dst in zip(x_in, xs)]
    left, right = ((dl, dl_v), (ur, ur_v)) if back else ((ur, ur_v), (dl, dl_v))
    first.append(copies.start(*left))
    one, two = ((down, down_v), (up, up_v)) if back else ((up, up_v), (down, down_v))
    ones, twos = [], []
    for a in range(blocks):
        span = pl.ds(a * ratio, ratio)
        ones.append(copies.start(one[0].at[span], one[1].at[span]))
        if a == 0:
            if back:
                first.append(copies.start(slope_in, slope))
                late = [copies.start(lat_down, lat_tmp)]
            else:
                late = []
            late.append(copies.start(*right))
        twos.append(copies.start(two[0].at[span], two[1].at[span]))
    for copy in first:
        copy.wait()
    lat_t = (lat[:, rows:] if back else lat[:, :rows]).T
    acc = jnp.zeros((rows, dl.shape[1]), F32)
    here[...] = jnp.zeros_like(here)
    for a in range(blocks):
        own = slice(a * blk, (a + 1) * blk)
        at = [slice((a ^ s) * blk, ((a ^ s) + 1) * blk) for s in near]
        pieces = [xs[0][:, c] for c in at] + [x[:, own] for x in xs[1:]]
        ones[a].wait()
        ys = []
        for r in range(ratio):
            h = a * ratio + r
            sl = slice(h * blk, (h + 1) * blk)
            if back:
                g = nt(lat_t, dl_v[sl, :])
                for j, piece in enumerate(pieces):
                    g = g + nt(piece, down_v[h, j])
                y = (g * slope[:, sl]).astype(BF16)
            else:
                v = nn(lat_t, ur_v[:, sl]) + nn(jnp.concatenate(pieces, axis=1), up_v[h].reshape(-1, blk))
                th = jnp.tanh(ROOT * (v + CUBIC * v * v * v))
                y = (0.5 * v * (1.0 + th)).astype(BF16)
                slope[:, sl] = 0.5 * (1.0 + th) + 0.5 * v * (1.0 - th * th) * ROOT * (
                    1.0 + 3.0 * CUBIC * v * v
                )
            act[:, sl] = y
            ys.append(y)
        twos[a].wait()
        if a == 0:
            for copy in late:
                copy.wait()
        for r in range(ratio):
            h = a * ratio + r
            sl = slice(h * blk, (h + 1) * blk)
            acc = acc + (nt(ys[r], ur_v[:, sl]) if back else nn(ys[r], dl_v[sl, :]))
        if a == blocks - 1:
            copies.back(act, act_out)
            if not back:
                copies.back(slope, slope_out)
        for j in list(range(len(near), len(near) + n)) + list(range(len(near))):
            f = sum(
                nt(ys[r], up_v[a * ratio + r, j]) if back else nn(ys[r], down_v[a * ratio + r, j])
                for r in range(ratio)
            )
            if j < len(near):
                here[:, at[j]] += f
            else:
                parts[j - len(near)][:, own] = f.astype(BF16)
        if a == blocks - 1:
            for src, dst in zip(parts, parts_out):
                copies.back(src, dst)
    copies.back(here, here_out)
    if back:
        lat[:, :rows] = lat_tmp[...]
        lat[:, rows:] = acc.T.astype(BF16)
        for dst, c in zip(lat_outs, halves()):
            copies.back(lat.at[pl.ds(pl.multiple_of(c * half, half), half), :], dst)
    else:
        lat_tmp[...] = acc.T.astype(BF16)
        copies.back(lat_tmp, lat_outs[0])
    copies.finish()


def layer_half(x, far, lat, up, down, ur, dl, near, slope=None, lat_down=None):
    back = slope is not None
    rows, width = x.shape
    hidden, _, blk = up.shape[:3]
    blocks = width // blk
    ratio = hidden // blocks
    rank = dl.shape[1]
    n = len(far)
    block, gate, sums = shape((rows, width)), shape((rows, hidden * blk), F32), shape((rows, width), F32)
    wide = shape((rows, hidden * blk))
    outs = [wide] + ([] if back else [gate]) + [sums] + [block] * n
    outs += [shape((rank // 2, 2 * rows))] * 2 if back else [shape((rank, rows))]
    held = [block] * (1 + n) + [shape((rank, 2 * rows))] + [shape(w.shape) for w in (up, down, ur, dl)]
    held += [gate, wide, sums] + [block] * n + [shape((rank, rows))]
    args = [x, *far, *lat, up, down, ur, dl, *((slope, lat_down) if back else ())]
    return pl.pallas_call(
        functools.partial(half_kernel, back, near, n, ratio, blk),
        in_specs=[HBM] * len(args),
        out_specs=[HBM] * len(outs),
        out_shape=outs,
        scratch_shapes=[pltpu.VMEM(h.shape, h.dtype) for h in held]
        + [pltpu.SemaphoreType.DMA((len(args) + len(outs) + 2 * blocks,))],
        compiler_params=params(28),
    )(*args)


def select_kernel(n, dp, part, blk, *refs):
    toks, outs, tmp, sem = refs[:n], refs[n : n + dp], refs[n + dp], refs[n + dp + 1]
    copies = [pltpu.make_async_copy(t, tmp.at[z], sem.at[z]) for z, t in enumerate(toks)]
    for c in copies:
        c.start()
    blocks = tmp.shape[2] // blk
    k = lax.axis_index("dp")
    r = lax.broadcasted_iota(jnp.int32, (blk, blk), 0)
    c = lax.broadcasted_iota(jnp.int32, (blk, blk), 1)
    pick = jnp.where(c == jnp.bitwise_xor(r, k * part), 1.0, 0.0).astype(BF16)
    for z in range(n):
        copies[z].wait()
        for b in range(blocks):
            at = (z * blocks + b) * part
            out = nt(pick, tmp[z, :, b * blk : (b + 1) * blk]).astype(BF16)
            for m in range(dp):
                outs[m][at : at + part, :] = out[m * part : (m + 1) * part]


def select_pass(toks, dp, part, blk):
    rows, width = toks[0].shape
    n = len(toks)
    return pl.pallas_call(
        functools.partial(select_kernel, n, dp, part, blk),
        in_specs=[HBM] * n,
        out_specs=[VM] * dp,
        out_shape=[shape((n * (width // blk) * part, rows))] * dp,
        scratch_shapes=[pltpu.VMEM((n, rows, width), BF16), pltpu.SemaphoreType.DMA((n,))],
        compiler_params=params(),
        name="ks",
    )(*toks)


def cut_kernel(dp, rank_part, *refs):
    first, second = refs[:2], refs[2:4]
    outs, whole2, whole1 = refs[4 : 4 + dp], refs[4 + dp], refs[5 + dp]
    put_halves(whole1, *first)
    put_halves(whole2, *second)
    k = lax.axis_index("dp")
    for m in range(dp):
        rows = cols(jnp.bitwise_xor(k, m), rank_part)
        outs[m][:rank_part, :] = whole1[rows, :]
        outs[m][rank_part:, :] = whole2[rows, :]


def cut_pass(first, second, dp, rank_part):
    rank, count = 2 * first[0].shape[0], first[0].shape[1]
    return pl.pallas_call(
        functools.partial(cut_kernel, dp, rank_part),
        in_specs=[VM] * 4,
        out_specs=[VM] * (dp + 1),
        out_shape=[shape((2 * rank_part, count))] * dp + [shape((rank, count))],
        scratch_shapes=[pltpu.VMEM((rank, count), BF16)],
        compiler_params=params(),
        name="kc",
    )(*first, *second)


def gather_copies(groups, scratch, sem):
    made, at = [], 0
    for refs, dst in zip(groups, scratch):
        rows = refs[0].shape[0]
        some = []
        for m, ref in enumerate(refs):
            some.append(pltpu.make_async_copy(ref, dst.at[pl.ds(m * rows, rows), :], sem.at[at]))
            at += 1
        made.append(some)
    for some in made:
        for c in some:
            c.start()
    return made


def wait_all(some):
    for c in some:
        c.wait()


def split_groups(first, both, base):
    rows = first.shape[0]
    return [first] + [ref.at[pl.ds(base * rows, rows), :] for ref in both]


def down_kernel(near, kinds, dp, ratio, blk, scale, *refs):
    take = iter(refs)
    tok, cot = next(take), next(take)
    both = [next(take) for _ in range(dp - 1)]
    rows, width = tok.shape
    cots = [split_groups(cot, both, 1)]
    for joint in kinds:
        if joint:
            far, rest = next(take), next(take)
            cots.append([far] + [rest.at[pl.ds(g * rows, rows), :] for g in range(dp - 1)])
        else:
            cots.append([next(take) for _ in range(dp)])
    acts = [next(take) for _ in range(dp)]
    gd, own_rows = next(take), next(take)
    tok_all = next(take)
    cot_all = [next(take) for _ in cots]
    act_all = next(take)
    made = gather_copies([split_groups(tok, both, 0)] + cots + [acts], [tok_all] + cot_all + [act_all], next(take))
    blocks = width // blk
    part = gd.shape[2]
    pick = one_hot(part, blk, lax.axis_index("dp") * part)
    wait_all(made[0])
    for b in range(blocks):
        own_rows[b * part : (b + 1) * part, :] = nt(pick, tok_all[:, b * blk : (b + 1) * blk]).astype(BF16)
    for some in made[1:]:
        wait_all(some)
    for a in range(blocks):
        lhs = jnp.concatenate(
            [
                nt(pick, act_all[:, (a * ratio + r) * blk : (a * ratio + r + 1) * blk]).astype(BF16)
                for r in range(ratio)
            ],
            axis=0,
        )
        srcs = [(0, a ^ s) for s in near] + [(1 + j, a) for j in range(len(kinds))]
        for j, (i, b) in enumerate(srcs):
            out = (nn(lhs, cot_all[i][:, b * blk : (b + 1) * blk]) * scale).astype(BF16)
            for r in range(ratio):
                gd[a * ratio + r, j] = out[r * part : (r + 1) * part]


def stacked(dims, count):
    return [pltpu.VMEM(d, t) for d, t in dims] + [pltpu.SemaphoreType.DMA((count,))]


def down_pass(tok, cot, both, far, acts, near, part, scale, blk):
    dp = len(acts)
    rows, width = tok.shape
    hid = acts[0].shape[1]
    kinds = tuple(len(f) == 2 for f in far)
    args = [tok, cot, *both, *[x for f in far for x in f], *acts]
    dims = [((dp * rows, width), BF16)] * (2 + len(far)) + [((dp * rows, hid), BF16)]
    return pl.pallas_call(
        functools.partial(down_kernel, near, kinds, dp, hid // width, blk, scale),
        in_specs=[HBM] * len(args),
        out_specs=[VM] * 2,
        out_shape=[shape((hid // blk, len(near) + len(far), part, blk)), shape((width // blk * part, dp * rows))],
        scratch_shapes=stacked(dims, dp * len(dims)),
        compiler_params=params(24),
        name="kd",
    )(*args)


def rank_kernel(n, dp, rank_part, scale, *refs):
    take = iter(refs)
    tok, cot = next(take), next(take)
    both = [next(take) for _ in range(dp - 1)]
    acts, lats = ([next(take) for _ in range(dp)] for _ in range(2))
    singles = [[next(take)] for _ in range(5 + 2 * n)]
    gdl, gul, gdr, layer_out, token_grads = (next(take) for _ in range(5))
    groups = [acts, split_groups(tok, both, 0), split_groups(cot, both, 1), lats] + singles
    scratch = [next(take) for _ in groups]
    made = gather_copies(groups, scratch, next(take))
    act_all, tok_all, cot_all, lat_all, out_here, grad_here, dr, ul, lat2 = scratch[:9]
    rows, _ = tok.shape
    for some in made:
        wait_all(some)

    def lat_rows(second, half):
        piece = lat_all.at[:, half * rows : (half + 1) * rows]
        first = rank_part if second else 0
        return jnp.concatenate(
            [piece[2 * rank_part * m + first : 2 * rank_part * m + first + rank_part, :] for m in range(dp)],
            axis=1,
        )

    gdl[...] = (nn(lat_rows(False, 1), act_all[...]) * scale).astype(BF16)
    gdr[...] = (nn(lat_rows(True, 0), cot_all[...]) * scale).astype(BF16)
    gul[...] = (nn(lat_rows(True, 1), tok_all[...]) * scale).astype(BF16)
    out = out_here[...] + nn(lat2[:, :rows].T, dr[...])
    grad = grad_here[...] + nt(lat2[:, rows:].T, ul[...])
    for p, q in zip(scratch[9 : 9 + n], scratch[9 + n :]):
        out = out + p[...].astype(F32)
        grad = grad + q[...].astype(F32)
    layer_out[...] = out.astype(BF16)
    token_grads[...] = grad.astype(BF16)


def rank_pass(tok, cot, both, acts, lats, singles, n, rank_part, scale):
    dp = len(acts)
    rows, width = tok.shape
    hid = acts[0].shape[1]
    args = [tok, cot, *both, *acts, *lats, *singles]
    dims = [((dp * rows, hid), BF16)] + [((dp * rows, width), BF16)] * 2
    dims += [((dp * lats[0].shape[0], lats[0].shape[1]), BF16)] + [(x.shape, x.dtype) for x in singles]
    wide, full = shape((rank_part, width)), shape((rows, width))
    return pl.pallas_call(
        functools.partial(rank_kernel, n, dp, rank_part, scale),
        in_specs=[HBM] * len(args),
        out_specs=[VM] * 5,
        out_shape=[shape((rank_part, hid)), wide, wide, full, full],
        scratch_shapes=stacked(dims, 4 * dp + len(singles)),
        compiler_params=params(16),
        name="kr",
    )(*args)


def up_kernel(near, n_full, n_thin, dp, ratio, blk, rank_part, scale, *refs):
    take = iter(refs)
    pres = [next(take) for _ in range(dp)]
    lats = [next(take) for _ in range(dp)]
    thin = [next(take) for _ in range(dp)] if n_thin else []
    full = [[next(take)] for _ in range(1 + n_full)]
    gu, gur = next(take), next(take)
    groups = [lats] + ([thin] if n_thin else []) + full + [pres]
    scratch = [next(take) for _ in groups]
    lhs_all, sem = next(take), next(take)
    made = gather_copies(groups, scratch, sem)
    part = gu.shape[2]
    rows = pres[0].shape[0]
    lat_all, pre_all = scratch[0], scratch[-1]
    full_all = scratch[-2 - n_full : -1]
    blocks = full_all[0].shape[0] // part
    count = len(near) + n_full + n_thin
    step = count * part + rank_part
    for some in made[:-1]:
        wait_all(some)
    for a in range(blocks):
        pieces = [full_all[0][(a ^ s) * part : ((a ^ s) + 1) * part, :] for s in near]
        pieces += [f[a * part : (a + 1) * part, :] for f in full_all[1:]]
        for j in range(n_thin):
            at = (j * blocks + a) * part
            tall = thin[0].shape[0]
            pieces.append(
                jnp.concatenate([scratch[1][m * tall + at : m * tall + at + part, :] for m in range(dp)], axis=1)
            )
        pieces.append(
            jnp.concatenate(
                [lat_all[2 * rank_part * m : 2 * rank_part * m + rank_part, :rows] for m in range(dp)], axis=1
            )
        )
        lhs_all[a * step : (a + 1) * step, :] = jnp.concatenate(pieces, axis=0)
    wait_all(made[-1])
    for a in range(blocks):
        for r in range(ratio):
            h = a * ratio + r
            out = nn(lhs_all[a * step : (a + 1) * step, :], pre_all[:, h * blk : (h + 1) * blk])
            out = (out * scale).astype(BF16)
            for j in range(count):
                gu[h, j] = out[j * part : (j + 1) * part]
            gur[:, h * blk : (h + 1) * blk] = out[count * part :]


def up_pass(pres, lats, thin, n_thin, full, near, part, rank_part, scale, blk):
    dp = len(pres)
    rows, hid = pres[0].shape
    count = len(near) + len(full) - 1 + n_thin
    thin = list(thin) if n_thin else []
    args = [*pres, *lats, *thin, *full]
    blocks = full[0].shape[0] // part
    groups = [lats] + ([thin] if n_thin else []) + [[f] for f in full] + [pres]
    dims = [((len(g) * g[0].shape[0], g[0].shape[1]), BF16) for g in groups]
    dims.append(((blocks * (count * part + rank_part), dp * rows), BF16))
    return pl.pallas_call(
        functools.partial(up_kernel, near, len(full) - 1, n_thin, dp, hid // (blocks * blk), blk, rank_part, scale),
        in_specs=[HBM] * len(args),
        out_specs=[VM, VM],
        out_shape=[shape((hid // blk, count, part, blk)), shape((rank_part, hid))],
        scratch_shapes=stacked(dims, len(args)),
        compiler_params=params(20),
        name="ku",
    )(*args)


def shards(tokens, cotangent, up_blocks, down_blocks, up_left, up_right, down_left, down_right):
    rows, width = tokens.shape
    blk = up_blocks.shape[-1]
    blocks = width // blk
    dp = lax.axis_size("dp")
    part, rank_part = blk // dp, up_left.shape[1] // dp
    scale = 1.0 / math.sqrt(rows * dp)
    near = tuple(s for s in STRIDES if s < blocks)
    masks = [s // blocks for s in STRIDES if s >= blocks]
    bits = [1 << b for b in range(dp.bit_length() - 1)]
    flip = bits[::-1]
    thin = [i for i, m in enumerate(masks) if m != 1]
    n = len(masks)
    tokens, cotangent, up_blocks, down_blocks = (in_hbm(x) for x in (tokens, cotangent, up_blocks, down_blocks))
    up_left, up_right, down_left, down_right = (in_hbm(x) for x in (up_left, up_right, down_left, down_right))

    tok_far = [swapped(tokens, "tensor", m) for m in masks]
    cot_far = [swapped(cotangent, "tensor", m) for m in masks]
    *lat_parts, both = latent_pass(tokens, cotangent, up_left, down_right)
    both = spread(both, bits)[1:]
    lat = total(*lat_parts)
    sent = select_pass([tok_far[i] for i in thin], dp, part, blk) if thin else []
    thin_groups = [swapped(x, "dp", m) if m else x for m, x in enumerate(sent)]
    others = join_pass(both)
    far = [
        (cot_far[i], swapped(others, "tensor", m)) if m <= 2 else spread(cot_far[i], flip)
        for i, m in enumerate(masks)
    ]

    weights = (up_blocks, down_blocks, up_right, down_left)
    made = layer_half(tokens, tok_far, lat, *weights, near)
    act, slope, out_here, *out_parts, lat_down = made
    made = layer_half(cotangent, cot_far, lat, *weights, near, slope, lat_down)
    pre, grad_here, *grad_parts, lat_mine, lat_other = made
    out_parts = [swapped(x, "tensor", m) for x, m in zip(out_parts, masks)]
    grad_parts = [swapped(x, "tensor", m) for x, m in zip(grad_parts, masks)]
    act_groups = spread(act, bits)
    pre_groups = spread(pre, flip)
    *pieces, lat2 = cut_pass(lat, total(lat_mine, lat_other), dp, rank_part)
    lat_groups = [swapped(x, "dp", m) if m else x for m, x in enumerate(pieces)]

    gd, own_rows = down_pass(tokens, cotangent, both, far, act_groups, near, part, scale, blk)
    gdl, gul, gdr, layer_out, token_grads = rank_pass(
        tokens, cotangent, both, act_groups, lat_groups,
        [out_here, grad_here, down_right, up_left, lat2, *out_parts, *grad_parts], n, rank_part, scale,
    )
    full_rows = [own_rows] + [swapped(own_rows, "tensor", m) for m in masks if m == 1]
    gu, gur = up_pass(
        pre_groups, lat_groups, thin_groups, len(thin), full_rows, near, part, rank_part, scale, blk
    )
    return layer_out, token_grads, gu, gd, gul.T, gur, gdl.T, gdr


def solution(mesh):
    d, t = "dp", "tensor"
    blocks = P(t, None, None, None)
    in_specs = (P(d, t), P(d, t), blocks, blocks, P(t, None), P(None, t), P(t, None), P(None, t))
    cut = P(t, None, d, None)
    out_specs = (P(d, t), P(d, t), cut, cut, P(t, d), P(d, t), P(t, d), P(d, t))
    return jax.shard_map(shards, mesh=mesh, in_specs=in_specs, out_specs=out_specs, check_vma=False)
```

time: 390 us -> 166 us (0.43)
  waiting for transfers between devices: 199 us -> 81.8 us
  blocking collectives: 71.6 us -> 0 us
  local copies, waits for them, and re-layouts: 47.4 us -> 0.81 us
  starting transfers between devices: 11 us -> 49 us
  matrix products: 37 us -> 0 us
  Pallas kernels: 0 us -> 32.7 us
  between operations: 14.5 us -> 1.07 us
  other arithmetic: 8.07 us -> 0.11 us
    reduce_scatter x6 -> x0, waiting for transfers between devices: 164 us -> none  [the longest x1 73.5 us: shards(): lax.psum_scatter(grad_up.astype(jnp.bfloat16), 'dp', scatter_dimension=2,...]
    psum x2 -> x0, blocking collectives: 71.6 us -> none  [the longest x1 42.6 us: shards(): lat_sum = lax.psum(up_part, 'tensor')]
    ppermute x9 -> x41, waiting for transfers between devices: 35.5 us -> 81.8 us  [swapped(): lax.ppermute(x, axis, [(i, i ^ mask) for i in range(lax.axis_size(axis))])]
    ppermute x9 -> x41, starting transfers between devices: 10.6 us -> 49 us  [swapped(): lax.ppermute(x, axis, [(i, i ^ mask) for i in range(lax.axis_size(axis))])]
    dot_general x18 -> x0, matrix products: 37 us -> none  [the longest x1 5.84 us: shards(): jnp.einsum('tirc,tijb->irjcb', act_four, cot_blocks, preferred_element_ty...]
    pallas_call x0 -> x9, Pallas kernels: none -> 32.7 us  [the longest x2 16.3 us: layer_half(): pl.pallas_call(functools.partial(half_kernel, back, near, n, ratio, blk),...]
    convert_element_type x2 -> x0, local copies, waits for them, and re-layouts: 17.3 us -> none  [the longest x1 8.65 us: shards(): grad_down.astype(jnp.bfloat16)]
    unnamed x35 -> x18, local copies, waits for them, and re-layouts: 11.3 us -> 0.81 us
  transfers between devices with their start and end apart: 15 -> 41, of which waited for: 7 -> 18; matrix products, arithmetic and copies ran while one was open for 17% -> 0% of each run, Pallas kernels for 0% -> 16%
where the time goes in v1:
time: 166 us; the launch traced here: 165 us
  waiting for transfers between devices  81.8 us (49%)
  starting transfers between devices  49 us (30%)
  Pallas kernels  32.7 us (20%)
    ppermute x41, waiting for transfers between devices, swapped(): lax.ppermute(x, axis, [(i, i ^ mask) for i in range(lax.axis_size(axis))])  81.8 us
    ppermute x41, starting transfers between devices, swapped(): lax.ppermute(x, axis, [(i, i ^ mask) for i in range(lax.axis_size(axis))])  49 us
    pallas_call x2, Pallas kernels, layer_half(): pl.pallas_call(functools.partial(half_kernel, back, near, n, ratio, blk),...  16.3 us
    pallas_call x1, Pallas kernels, down_pass(): pl.pallas_call(functools.partial(down_kernel, near, kinds, dp, hid // wid...  4.88 us
    pallas_call x1, Pallas kernels, rank_pass(): pl.pallas_call(functools.partial(rank_kernel, n, dp, rank_part, scale), i...  4.17 us
    pallas_call x1, Pallas kernels, up_pass(): pl.pallas_call(functools.partial(up_kernel, near, len(full) - 1, n_thin,...  3.78 us
  transfers between devices with their start and end apart: 41, of which 18 were waited for; matrix products, arithmetic and copies ran while one was open for 0% of the time, Pallas kernels for 16%

profile of v1, /device:TPU:0, one launch (start us, length us, event | category | flops | bytes accessed | tf_op | source)
XLA Modules:
  0.0 165.5 jit_solution(4938005038629424872)
XLA Ops:
  0.6 1.8 %kl.1 = (bf16[128,256]{1,0:T(8,128)(2,1)S(1)}, bf16[128,256]{1,0:T(8,128)(2,1)S(1)}, bf16[256,1024]{1,0:T(8,128)(2,1)S(1)}) custom-call(bf16[128,1024]{1,0:T(8,128)(2,1)} %refs_0_.7, bf16[128,1024]{1,0:T(8,128)(2,1)} %refs_1_.3, bf16[1024,256]{1,0:T(8,128)(2,1)} %refs_16_.1, bf16[256,1024]{1,0:T(8,128)(2,1)} %refs_15_.1), custom_call_target="tpu_custom_call" | custom-call | tf_op jit(solution)/shard_map/kl/pallas_call | solution.py:126
  4.0 4.0 %collective-permute-start.7 = (bf16[128,256]{1,0:T(8,128)(2,1)S(1)}, bf16[128,256]{1,0:T(8,128)(2,1)S(1)}, u32[]{:S(2)}, u32[]{:S(2)}) collective-permute-start(bf16[128,256]{1,0:T(8,128)(2,1)S(1)} %add_convert_fusion.5), channel_id=1, source_target_pairs={{0,4},{1,5},{2,6},{3,7},{4,0},{5,1},{6,2},{7,3},{8,12},{9,13},{10,... | collective-permute-start | bytes 196616 | tf_op jit(solution)/shard_map/ppermute | solution.py:20
  8.0 1.8 %collective-permute-start.4 = (bf16[128,1024]{1,0:T(8,128)(2,1)}, bf16[128,1024]{1,0:T(8,128)(2,1)S(1)}, u32[]{:S(2)}, u32[]{:S(2)}) collective-permute-start(bf16[128,1024]{1,0:T(8,128)(2,1)} %refs_0_.7), channel_id=1, source_target_pairs={{0,2},{1,3},{2,0},{3,1},{4,6},{5,7},{6,4},{7,5},{8,10},{9,11},{10,... | collective-permute-start | bytes 786440 | tf_op jit(solution)/shard_map/ppermute | solution.py:20
  9.9 2.2 %collective-permute-done.7 = bf16[128,256]{1,0:T(8,128)(2,1)S(1)} collective-permute-done((bf16[128,256]{1,0:T(8,128)(2,1)S(1)}, bf16[128,256]{1,0:T(8,128)(2,1)S(1)}, u32[]{:S(2)}, u32[]{:S(2)}) %collective-permute-start.7) | collective-permute-done | bytes 65568 | tf_op jit(solution)/shard_map/ppermute | solution.py:20
  12.1 6.1 %collective-permute-start.8 = (bf16[128,256]{1,0:T(8,128)(2,1)S(1)}, bf16[128,256]{1,0:T(8,128)(2,1)S(1)}, u32[]{:S(2)}, u32[]{:S(2)}) collective-permute-start(bf16[128,256]{1,0:T(8,128)(2,1)S(1)} %add_convert_fusion.4), channel_id=1, source_target_pairs={{0,2},{1,3},{2,0},{3,1},{4,6},{5,7},{6,4},{7,5},{8,10},{9,11},{10,... | collective-permute-start | bytes 196616 | tf_op jit(solution)/shard_map/ppermute | solution.py:20
  18.2 3.5 %collective-permute-start.15 = (bf16[128,1024]{1,0:T(8,128)(2,1)}, bf16[128,1024]{1,0:T(8,128)(2,1)S(1)}, u32[]{:S(2)}, u32[]{:S(2)}) collective-permute-start(bf16[128,1024]{1,0:T(8,128)(2,1)} %refs_1_.3), channel_id=1, source_target_pairs={{0,4},{1,5},{2,6},{3,7},{4,0},{5,1},{6,2},{7,3},{8,12},{9,13},{10,... | collective-permute-start | bytes 786440 | tf_op jit(solution)/shard_map/ppermute | solution.py:20
  21.8 4.4 %collective-permute-done.8 = bf16[128,256]{1,0:T(8,128)(2,1)S(1)} collective-permute-done((bf16[128,256]{1,0:T(8,128)(2,1)S(1)}, bf16[128,256]{1,0:T(8,128)(2,1)S(1)}, u32[]{:S(2)}, u32[]{:S(2)}) %collective-permute-start.8) | collective-permute-done | bytes 65568 | tf_op jit(solution)/shard_map/ppermute | solution.py:20
  26.2 1.9 %collective-permute-start = (bf16[256,1024]{1,0:T(8,128)(2,1)S(1)}, bf16[256,1024]{1,0:T(8,128)(2,1)S(1)}, u32[]{:S(2)}, u32[]{:S(2)}) collective-permute-start(bf16[256,1024]{1,0:T(8,128)(2,1)S(1)} %get-tuple-element.43), channel_id=1, source_target_pairs={{0,8},{8,0},{16,24},{24,16},{1,9},{9,1},{17,25},{25,17},{2,10},{10... | collective-permute-start | bytes 1572872 | tf_op jit(solution)/shard_map/ppermute | solution.py:20
  29.5 7.3 %shard_map.143 = (bf16[128,2048]{1,0:T(8,128)(2,1)S(1)}, f32[128,2048]{1,0:T(8,128)S(1)}, f32[128,1024]{1,0:T(8,128)S(1)}, bf16[128,1024]{1,0:T(8,128)(2,1)S(1)}...) custom-call(bf16[128,1024]{1,0:T(8,128)(2,1)} %refs_0_.7, ...), custom_call_target="tpu_custom_call" | custom-call | tf_op jit(solution)/shard_map/pallas_call | solution.py:282
  38.6 9.0 %shard_map.144 = (bf16[128,2048]{1,0:T(8,128)(2,1)S(1)}, f32[128,1024]{1,0:T(8,128)S(1)}, bf16[128,1024]{1,0:T(8,128)(2,1)S(1)}, bf16[128,1024]{1,0:T(8,128)(2,1...) custom-call(bf16[128,1024]{1,0:T(8,128)(2,1)} %refs_1_.3, ...), custom_call_target="tpu_custom_call" | custom-call | tf_op jit(solution)/shard_map/pallas_call | solution.py:282
  47.7 1.9 %collective-permute-start.1 = (bf16[256,1024]{1,0:T(8,128)(2,1)S(1)}, bf16[256,1024]{1,0:T(8,128)(2,1)S(1)}, u32[]{:S(2)}, u32[]{:S(2)}) collective-permute-start(bf16[256,1024]{1,0:T(8,128)(2,1)S(1)} %get-tuple-element.43), channel_id=1, source_target_pairs={{0,16},{8,24},{16,0},{24,8},{1,17},{9,25},{17,1},{25,9},{2,18},{10... | collective-permute-start | bytes 1572872 | tf_op jit(solution)/shard_map/ppermute | solution.py:20
  49.6 2.4 %collective-permute-start.17 = (bf16[128,256]{1,0:T(8,128)(2,1)S(1)}, bf16[128,256]{1,0:T(8,128)(2,1)S(1)}, u32[]{:S(2)}, u32[]{:S(2)}) collective-permute-start(bf16[128,256]{1,0:T(8,128)(2,1)S(1)} %add_convert_fusion.2), channel_id=1, source_target_pairs={{0,4},{1,5},{2,6},{3,7},{4,0},{5,1},{6,2},{7,3},{8,12},{9,13},{10,... | collective-permute-start | bytes 196616 | tf_op jit(solution)/shard_map/ppermute | solution.py:20
  53.1 1.6 ks.1
  54.7 1.6 collective-permute-start.32
  57.1 2.4 %collective-permute-start.18 = (bf16[128,256]{1,0:T(8,128)(2,1)S(1)}, bf16[128,256]{1,0:T(8,128)(2,1)S(1)}, u32[]{:S(2)}, u32[]{:S(2)}) collective-permute-start(bf16[128,256]{1,0:T(8,128)(2,1)S(1)} %add_convert_fusion.1), channel_id=1, source_target_pairs={{0,2},{1,3},{2,0},{3,1},{4,6},{5,7},{6,4},{7,5},{8,10},{9,11},{10,... | collective-permute-start | bytes 196616 | tf_op jit(solution)/shard_map/ppermute | solution.py:20
  59.8 1.5 collective-permute-start.37
  61.8 17.1 %collective-permute-done.38.refs_11_ = bf16[128,1024]{1,0:T(8,128)(2,1)S(1)} collective-permute-done((bf16[128,1024]{1,0:T(8,128)(2,1)}, bf16[128,1024]{1,0:T(8,128)(2,1)S(1)}, u32[]{:S(2)}, u32[]{:S(2)}) %collective-permute-start.38) | collective-permute-done | bytes 262176 | tf_op jit(solution)/shard_map/ppermute | solution.py:20
  80.7 4.6 %collective-permute-start.25 = (bf16[128,1024]{1,0:T(8,128)(2,1)S(1)}, bf16[128,1024]{1,0:T(8,128)(2,1)S(1)}, u32[]{:S(2)}, u32[]{:S(2)}) collective-permute-start(bf16[128,1024]{1,0:T(8,128)(2,1)S(1)} %get-tuple-element.60), channel_id=1, source_target_pairs={{0,4},{1,5},{2,6},{3,7},{4,0},{5,1},{6,2},{7,3},{8,12},{9,13},{10,... | collective-permute-start | bytes 786440 | tf_op jit(solution)/shard_map/ppermute | solution.py:20
  86.2 4.7 %collective-permute-done.24.refs_19_ = bf16[128,1024]{1,0:T(8,128)(2,1)S(1)} collective-permute-done((bf16[128,1024]{1,0:T(8,128)(2,1)S(1)}, bf16[128,1024]{1,0:T(8,128)(2,1)S(1)}, u32[]{:S(2)}, u32[]{:S(2)}) %collective-permute-start.24) | collective-permute-done | bytes 262176 | tf_op jit(solution)/shard_map/ppermute | solution.py:20
  91.0 5.6 %collective-permute-done.25.refs_20_ = bf16[128,1024]{1,0:T(8,128)(2,1)S(1)} collective-permute-done((bf16[128,1024]{1,0:T(8,128)(2,1)S(1)}, bf16[128,1024]{1,0:T(8,128)(2,1)S(1)}, u32[]{:S(2)}, u32[]{:S(2)}) %collective-permute-start.25) | collective-permute-done | bytes 262176 | tf_op jit(solution)/shard_map/ppermute | solution.py:20
  98.0 1.5 collective-permute-start.11
  101.6 11.2 %collective-permute-done.11.refs_7_.refs_15_ = bf16[128,2048]{1,0:T(8,128)(2,1)S(1)} collective-permute-done((bf16[128,2048]{1,0:T(8,128)(2,1)S(1)}, bf16[128,2048]{1,0:T(8,128)(2,1)S(1)}, u32[]{:S(2)}, u32[]{:S(2)}) %collective-permute-start.11) | collective-permute-done | bytes 524320 | tf_op jit(solution)/shard_map/ppermute | solution.py:20
  112.8 11.2 %collective-permute-done.30.refs_2_ = bf16[128,2048]{1,0:T(8,128)(2,1)S(1)} collective-permute-done((bf16[128,2048]{1,0:T(8,128)(2,1)S(1)}, bf16[128,2048]{1,0:T(8,128)(2,1)S(1)}, u32[]{:S(2)}, u32[]{:S(2)}) %collective-permute-start.30) | collective-permute-done | bytes 524320 | tf_op jit(solution)/shard_map/ppermute | solution.py:20
  124.1 10.6 %collective-permute-done.12.refs_8_.refs_16_ = bf16[128,2048]{1,0:T(8,128)(2,1)S(1)} collective-permute-done((bf16[128,2048]{1,0:T(8,128)(2,1)S(1)}, bf16[128,2048]{1,0:T(8,128)(2,1)S(1)}, u32[]{:S(2)}, u32[]{:S(2)}) %collective-permute-start.12) | collective-permute-done | bytes 524320 | tf_op jit(solution)/shard_map/ppermute | solution.py:20
  134.7 2.1 %collective-permute-start.20 = (bf16[128,256]{1,0:T(8,128)(2,1)S(1)}, bf16[128,256]{1,0:T(8,128)(2,1)S(1)}, u32[]{:S(2)}, u32[]{:S(2)}) collective-permute-start(bf16[128,256]{1,0:T(8,128)(2,1)S(1)} %get-tuple-element.52), channel_id=1, source_target_pairs={{0,8},{8,0},{16,24},{24,16},{1,9},{9,1},{17,25},{25,17},{2,10},{10... | collective-permute-start | bytes 196616 | tf_op jit(solution)/shard_map/ppermute | solution.py:20
  136.8 4.9 %kd.1 = (bf16[8,6,64,256]{3,2,1,0:T(8,128)(2,1)}, bf16[256,512]{1,0:T(8,128)(2,1)S(1)}) custom-call(bf16[128,1024]{1,0:T(8,128)(2,1)} %refs_0_.7, bf16[128,1024]{1,0:T(8,128)(2,1)} %refs_1_.3, bf16[256,1024]{1,0:T(8,128)(2,1)S(1)} %collective-permute-done.refs_2_.refs_0_, bf16[256,1024]{1,0:T(8,128)(2,1)S(1)} %collective-permute-done.1.refs_3_.refs_1_, ...), custom_call_target="tpu_custom_call" | custom-call | tf_op jit(solution)/shard_map/kd/pallas_call | solution.py:428
  141.8 7.1 %collective-permute-done.28.refs_23_ = bf16[128,1024]{1,0:T(8,128)(2,1)S(1)} collective-permute-done((bf16[128,1024]{1,0:T(8,128)(2,1)S(1)}, bf16[128,1024]{1,0:T(8,128)(2,1)S(1)}, u32[]{:S(2)}, u32[]{:S(2)}) %collective-permute-start.28) | collective-permute-done | bytes 262176 | tf_op jit(solution)/shard_map/ppermute | solution.py:20
  148.9 1.5 collective-permute-start.21
  151.9 2.0 %collective-permute-done.21.refs_11_.refs_6_ = bf16[128,256]{1,0:T(8,128)(2,1)S(1)} collective-permute-done((bf16[128,256]{1,0:T(8,128)(2,1)S(1)}, bf16[128,256]{1,0:T(8,128)(2,1)S(1)}, u32[]{:S(2)}, u32[]{:S(2)}) %collective-permute-start.21) | collective-permute-done | bytes 65568 | tf_op jit(solution)/shard_map/ppermute | solution.py:20
  153.9 1.5 collective-permute-start.33
  157.0 4.2 %kr.1 = (bf16[64,2048]{1,0:T(8,128)(2,1)}, bf16[64,1024]{1,0:T(8,128)(2,1)}, bf16[64,1024]{1,0:T(8,128)(2,1)}, bf16[128,1024]{1,0:T(8,128)(2,1)}, bf16[128,1024]{1,0:T(8,128)(2,1)}) custom-call(bf16[128,1024]{1,0:T(8,128)(2,1)} %refs_0_.7, bf16[128,1024]{1,0:T(8,128)(2,1)} %refs_1_.3, bf16[256,1024]{1,0:T(8,128)(2,1)S(1)} %collective-permute-done.refs_2_.refs_0_, ...), custom_call_target="tpu_custom_call" | custom-call | tf_op jit(solution)/shard_map/kr/pallas_call | solution.py:482
  161.6 3.8 %ku.1 = (bf16[8,6,64,256]{3,2,1,0:T(8,128)(2,1)}, bf16[64,2048]{1,0:T(8,128)(2,1)}) custom-call(bf16[128,2048]{1,0:T(8,128)(2,1)S(1)} %get-tuple-element.66.refs_0_, bf16[128,2048]{1,0:T(8,128)(2,1)S(1)} %collective-permute-done.29.refs_1_, bf16[128,2048]{1,0:T(8,128)(2,1)S(1)} %collective-permute-done.30.refs_2_, ...), custom_call_target="tpu_custom_call" | custom-call | tf_op jit(solution)/shard_map/ku/pallas_call | solution.py:549
  (83 shorter events, 17.4 us)
Async XLA Ops:
  4.0 8.1 %collective-permute-start.7 = (bf16[128,256]{1,0:T(8,128)(2,1)S(1)}, bf16[128,256]{1,0:T(8,128)(2,1)S(1)}, u32[]{:S(2)}, u32[]{:S(2)}) collective-permute-start(bf16[128,256]{1,0:T(8,128)(2,1)S(1)} %add_convert_fusion.5), channel_id=1, source_target_pairs={{0,4},{1,5},{2,6},{3,7},{4,0},{5,1},{6,2},{7,3},{8,12},{9,13},{10,... | collective-permute-start | bytes 196616 | tf_op jit(solution)/shard_map/ppermute | solution.py:20
  8.0 18.2 %collective-permute-start.5 = (bf16[128,1024]{1,0:T(8,128)(2,1)}, bf16[128,1024]{1,0:T(8,128)(2,1)S(1)}, u32[]{:S(2)}, u32[]{:S(2)}) collective-permute-start(bf16[128,1024]{1,0:T(8,128)(2,1)} %refs_0_.7), channel_id=1, source_target_pairs={{0,4},{1,5},{2,6},{3,7},{4,0},{5,1},{6,2},{7,3},{8,12},{9,13},{10,... | collective-permute-start | bytes 786440 | tf_op jit(solution)/shard_map/ppermute | solution.py:20
  8.0 18.2 %collective-permute-start.4 = (bf16[128,1024]{1,0:T(8,128)(2,1)}, bf16[128,1024]{1,0:T(8,128)(2,1)S(1)}, u32[]{:S(2)}, u32[]{:S(2)}) collective-permute-start(bf16[128,1024]{1,0:T(8,128)(2,1)} %refs_0_.7), channel_id=1, source_target_pairs={{0,2},{1,3},{2,0},{3,1},{4,6},{5,7},{6,4},{7,5},{8,10},{9,11},{10,... | collective-permute-start | bytes 786440 | tf_op jit(solution)/shard_map/ppermute | solution.py:20
  12.1 14.0 %collective-permute-start.8 = (bf16[128,256]{1,0:T(8,128)(2,1)S(1)}, bf16[128,256]{1,0:T(8,128)(2,1)S(1)}, u32[]{:S(2)}, u32[]{:S(2)}) collective-permute-start(bf16[128,256]{1,0:T(8,128)(2,1)S(1)} %add_convert_fusion.4), channel_id=1, source_target_pairs={{0,2},{1,3},{2,0},{3,1},{4,6},{5,7},{6,4},{7,5},{8,10},{9,11},{10,... | collective-permute-start | bytes 196616 | tf_op jit(solution)/shard_map/ppermute | solution.py:20
  18.2 9.9 %collective-permute-start.3 = (bf16[128,1024]{1,0:T(8,128)(2,1)}, bf16[128,1024]{1,0:T(8,128)(2,1)S(1)}, u32[]{:S(2)}, u32[]{:S(2)}) collective-permute-start(bf16[128,1024]{1,0:T(8,128)(2,1)} %refs_0_.7), channel_id=1, source_target_pairs={{0,1},{1,0},{2,3},{3,2},{4,5},{5,4},{6,7},{7,6},{8,9},{9,8},{10,11... | collective-permute-start | bytes 786440 | tf_op jit(solution)/shard_map/ppermute | solution.py:20
  18.2 18.5 %collective-permute-start.15 = (bf16[128,1024]{1,0:T(8,128)(2,1)}, bf16[128,1024]{1,0:T(8,128)(2,1)S(1)}, u32[]{:S(2)}, u32[]{:S(2)}) collective-permute-start(bf16[128,1024]{1,0:T(8,128)(2,1)} %refs_1_.3), channel_id=1, source_target_pairs={{0,4},{1,5},{2,6},{3,7},{4,0},{5,1},{6,2},{7,3},{8,12},{9,13},{10,... | collective-permute-start | bytes 786440 | tf_op jit(solution)/shard_map/ppermute | solution.py:20
  26.1 11.6 %collective-permute-start.14 = (bf16[128,1024]{1,0:T(8,128)(2,1)}, bf16[128,1024]{1,0:T(8,128)(2,1)S(1)}, u32[]{:S(2)}, u32[]{:S(2)}) collective-permute-start(bf16[128,1024]{1,0:T(8,128)(2,1)} %refs_1_.3), channel_id=1, source_target_pairs={{0,2},{1,3},{2,0},{3,1},{4,6},{5,7},{6,4},{7,5},{8,10},{9,11},{10,... | collective-permute-start | bytes 786440 | tf_op jit(solution)/shard_map/ppermute | solution.py:20
  26.1 11.6 %collective-permute-start.13 = (bf16[128,1024]{1,0:T(8,128)(2,1)}, bf16[128,1024]{1,0:T(8,128)(2,1)S(1)}, u32[]{:S(2)}, u32[]{:S(2)}) collective-permute-start(bf16[128,1024]{1,0:T(8,128)(2,1)} %refs_1_.3), channel_id=1, source_target_pairs={{0,1},{1,0},{2,3},{3,2},{4,5},{5,4},{6,7},{7,6},{8,9},{9,8},{10,11... | collective-permute-start | bytes 786440 | tf_op jit(solution)/shard_map/ppermute | solution.py:20
  26.2 25.7 %collective-permute-start = (bf16[256,1024]{1,0:T(8,128)(2,1)S(1)}, bf16[256,1024]{1,0:T(8,128)(2,1)S(1)}, u32[]{:S(2)}, u32[]{:S(2)}) collective-permute-start(bf16[256,1024]{1,0:T(8,128)(2,1)S(1)} %get-tuple-element.43), channel_id=1, source_target_pairs={{0,8},{8,0},{16,24},{24,16},{1,9},{9,1},{17,25},{25,17},{2,10},{10... | collective-permute-start | bytes 1572872 | tf_op jit(solution)/shard_map/ppermute | solution.py:20
  47.7 32.2 %collective-permute-start.1 = (bf16[256,1024]{1,0:T(8,128)(2,1)S(1)}, bf16[256,1024]{1,0:T(8,128)(2,1)S(1)}, u32[]{:S(2)}, u32[]{:S(2)}) collective-permute-start(bf16[256,1024]{1,0:T(8,128)(2,1)S(1)} %get-tuple-element.43), channel_id=1, source_target_pairs={{0,16},{8,24},{16,0},{24,8},{1,17},{9,25},{17,1},{25,9},{2,18},{10... | collective-permute-start | bytes 1572872 | tf_op jit(solution)/shard_map/ppermute | solution.py:20
  49.6 7.5 %collective-permute-start.17 = (bf16[128,256]{1,0:T(8,128)(2,1)S(1)}, bf16[128,256]{1,0:T(8,128)(2,1)S(1)}, u32[]{:S(2)}, u32[]{:S(2)}) collective-permute-start(bf16[128,256]{1,0:T(8,128)(2,1)S(1)} %add_convert_fusion.2), channel_id=1, source_target_pairs={{0,4},{1,5},{2,6},{3,7},{4,0},{5,1},{6,2},{7,3},{8,12},{9,13},{10,... | collective-permute-start | bytes 196616 | tf_op jit(solution)/shard_map/ppermute | solution.py:20
  52.0 28.7 %collective-permute-start.2 = (bf16[256,1024]{1,0:T(8,128)(2,1)S(1)}, bf16[256,1024]{1,0:T(8,128)(2,1)S(1)}, u32[]{:S(2)}, u32[]{:S(2)}) collective-permute-start(bf16[256,1024]{1,0:T(8,128)(2,1)S(1)} %collective-permute-done.refs_2_.refs_0_), channel_id=1, source_target_pairs={{0,16},{8,24},{16,0},{24,8},{1,17},{9,25},{17,1},{25,9},{2,18},{10... | collective-permute-start | bytes 1572872 | tf_op jit(solution)/shard_map/ppermute | solution.py:20
  56.3 22.7 %collective-permute-start.38 = (bf16[128,1024]{1,0:T(8,128)(2,1)}, bf16[128,1024]{1,0:T(8,128)(2,1)S(1)}, u32[]{:S(2)}, u32[]{:S(2)}) collective-permute-start(bf16[128,1024]{1,0:T(8,128)(2,1)} %copy-done), channel_id=1, source_target_pairs={{0,16},{8,24},{16,0},{24,8},{1,17},{9,25},{17,1},{25,9},{2,18},{10... | collective-permute-start | bytes 786440 | tf_op jit(solution)/shard_map/ppermute | solution.py:20
  59.8 25.7 %collective-permute-start.37 = (bf16[128,1024]{1,0:T(8,128)(2,1)}, bf16[128,1024]{1,0:T(8,128)(2,1)S(1)}, u32[]{:S(2)}, u32[]{:S(2)}) collective-permute-start(bf16[128,1024]{1,0:T(8,128)(2,1)} %copy-done), channel_id=1, source_target_pairs={{0,8},{8,0},{16,24},{24,16},{1,9},{9,1},{17,25},{25,17},{2,10},{10... | collective-permute-start | bytes 786440 | tf_op jit(solution)/shard_map/ppermute | solution.py:20
  61.8 23.8 %collective-permute-start.23 = (bf16[128,1024]{1,0:T(8,128)(2,1)S(1)}, bf16[128,1024]{1,0:T(8,128)(2,1)S(1)}, u32[]{:S(2)}, u32[]{:S(2)}) collective-permute-start(bf16[128,1024]{1,0:T(8,128)(2,1)S(1)} %get-tuple-element.58), channel_id=1, source_target_pairs={{0,1},{1,0},{2,3},{3,2},{4,5},{5,4},{6,7},{7,6},{8,9},{9,8},{10,11... | collective-permute-start | bytes 786440 | tf_op jit(solution)/shard_map/ppermute | solution.py:20
  78.9 12.0 %collective-permute-start.24 = (bf16[128,1024]{1,0:T(8,128)(2,1)S(1)}, bf16[128,1024]{1,0:T(8,128)(2,1)S(1)}, u32[]{:S(2)}, u32[]{:S(2)}) collective-permute-start(bf16[128,1024]{1,0:T(8,128)(2,1)S(1)} %get-tuple-element.59), channel_id=1, source_target_pairs={{0,2},{1,3},{2,0},{3,1},{4,6},{5,7},{6,4},{7,5},{8,10},{9,11},{10,... | collective-permute-start | bytes 786440 | tf_op jit(solution)/shard_map/ppermute | solution.py:20
  79.9 20.2 %collective-permute-start.10 = (bf16[128,2048]{1,0:T(8,128)(2,1)S(1)}, bf16[128,2048]{1,0:T(8,128)(2,1)S(1)}, u32[]{:S(2)}, u32[]{:S(2)}) collective-permute-start(bf16[128,2048]{1,0:T(8,128)(2,1)S(1)} %get-tuple-element.46.refs_5_.refs_13_), channel_id=1, source_target_pairs={{0,8},{8,0},{16,24},{24,16},{1,9},{9,1},{17,25},{25,17},{2,10},{10... | collective-permute-start | bytes 1572872 | tf_op jit(solution)/shard_map/ppermute | solution.py:20
  80.7 15.9 %collective-permute-start.25 = (bf16[128,1024]{1,0:T(8,128)(2,1)S(1)}, bf16[128,1024]{1,0:T(8,128)(2,1)S(1)}, u32[]{:S(2)}, u32[]{:S(2)}) collective-permute-start(bf16[128,1024]{1,0:T(8,128)(2,1)S(1)} %get-tuple-element.60), channel_id=1, source_target_pairs={{0,4},{1,5},{2,6},{3,7},{4,0},{5,1},{6,2},{7,3},{8,12},{9,13},{10,... | collective-permute-start | bytes 786440 | tf_op jit(solution)/shard_map/ppermute | solution.py:20
  85.5 12.5 %collective-permute-start.26 = (bf16[128,1024]{1,0:T(8,128)(2,1)S(1)}, bf16[128,1024]{1,0:T(8,128)(2,1)S(1)}, u32[]{:S(2)}, u32[]{:S(2)}) collective-permute-start(bf16[128,1024]{1,0:T(8,128)(2,1)S(1)} %get-tuple-element.61), channel_id=1, source_target_pairs={{0,1},{1,0},{2,3},{3,2},{4,5},{5,4},{6,7},{7,6},{8,9},{9,8},{10,11... | collective-permute-start | bytes 786440 | tf_op jit(solution)/shard_map/ppermute | solution.py:20
  85.6 13.9 %collective-permute-start.39 = (bf16[128,1024]{1,0:T(8,128)(2,1)S(1)}, bf16[128,1024]{1,0:T(8,128)(2,1)S(1)}, u32[]{:S(2)}, u32[]{:S(2)}) collective-permute-start(bf16[128,1024]{1,0:T(8,128)(2,1)S(1)} %collective-permute-done.38.refs_11_), channel_id=1, source_target_pairs={{0,8},{8,0},{16,24},{24,16},{1,9},{9,1},{17,25},{25,17},{2,10},{10... | collective-permute-start | bytes 786440 | tf_op jit(solution)/shard_map/ppermute | solution.py:20
  90.9 43.7 %collective-permute-start.36 = (bf16[384,1024]{1,0:T(8,128)(2,1)S(1)}, bf16[384,1024]{1,0:T(8,128)(2,1)S(1)}, u32[]{:S(2)}, u32[]{:S(2)}) collective-permute-start(bf16[384,1024]{1,0:T(8,128)(2,1)S(1)} %kj.1), channel_id=1, source_target_pairs={{0,2},{1,3},{2,0},{3,1},{4,6},{5,7},{6,4},{7,5},{8,10},{9,11},{10,... | collective-permute-start | bytes 2359304 | tf_op jit(solution)/shard_map/ppermute | solution.py:20
  97.8 36.9 %collective-permute-start.35 = (bf16[384,1024]{1,0:T(8,128)(2,1)S(1)}, bf16[384,1024]{1,0:T(8,128)(2,1)S(1)}, u32[]{:S(2)}, u32[]{:S(2)}) collective-permute-start(bf16[384,1024]{1,0:T(8,128)(2,1)S(1)} %kj.1), channel_id=1, source_target_pairs={{0,1},{1,0},{2,3},{3,2},{4,5},{5,4},{6,7},{7,6},{8,9},{9,8},{10,11... | collective-permute-start | bytes 2359304 | tf_op jit(solution)/shard_map/ppermute | solution.py:20
  98.0 14.8 %collective-permute-start.11 = (bf16[128,2048]{1,0:T(8,128)(2,1)S(1)}, bf16[128,2048]{1,0:T(8,128)(2,1)S(1)}, u32[]{:S(2)}, u32[]{:S(2)}) collective-permute-start(bf16[128,2048]{1,0:T(8,128)(2,1)S(1)} %get-tuple-element.46.refs_5_.refs_13_), channel_id=1, source_target_pairs={{0,16},{8,24},{16,0},{24,8},{1,17},{9,25},{17,1},{25,9},{2,18},{10... | collective-permute-start | bytes 1572872 | tf_op jit(solution)/shard_map/ppermute | solution.py:20
  99.5 24.5 %collective-permute-start.30 = (bf16[128,2048]{1,0:T(8,128)(2,1)S(1)}, bf16[128,2048]{1,0:T(8,128)(2,1)S(1)}, u32[]{:S(2)}, u32[]{:S(2)}) collective-permute-start(bf16[128,2048]{1,0:T(8,128)(2,1)S(1)} %get-tuple-element.66.refs_0_), channel_id=1, source_target_pairs={{0,16},{8,24},{16,0},{24,8},{1,17},{9,25},{17,1},{25,9},{2,18},{10... | collective-permute-start | bytes 1572872 | tf_op jit(solution)/shard_map/ppermute | solution.py:20
  100.1 34.6 %collective-permute-start.12 = (bf16[128,2048]{1,0:T(8,128)(2,1)S(1)}, bf16[128,2048]{1,0:T(8,128)(2,1)S(1)}, u32[]{:S(2)}, u32[]{:S(2)}) collective-permute-start(bf16[128,2048]{1,0:T(8,128)(2,1)S(1)} %collective-permute-done.10.refs_6_.refs_14_), channel_id=1, source_target_pairs={{0,16},{8,24},{16,0},{24,8},{1,17},{9,25},{17,1},{25,9},{2,18},{10... | collective-permute-start | bytes 1572872 | tf_op jit(solution)/shard_map/ppermute | solution.py:20
  112.8 48.7 %collective-permute-start.29 = (bf16[128,2048]{1,0:T(8,128)(2,1)S(1)}, bf16[128,2048]{1,0:T(8,128)(2,1)S(1)}, u32[]{:S(2)}, u32[]{:S(2)}) collective-permute-start(bf16[128,2048]{1,0:T(8,128)(2,1)S(1)} %get-tuple-element.66.refs_0_), channel_id=1, source_target_pairs={{0,8},{8,0},{16,24},{24,16},{1,9},{9,1},{17,25},{25,17},{2,10},{10... | collective-permute-start | bytes 1572872 | tf_op jit(solution)/shard_map/ppermute | solution.py:20
  124.0 17.7 %collective-permute-start.27 = (bf16[128,1024]{1,0:T(8,128)(2,1)S(1)}, bf16[128,1024]{1,0:T(8,128)(2,1)S(1)}, u32[]{:S(2)}, u32[]{:S(2)}) collective-permute-start(bf16[128,1024]{1,0:T(8,128)(2,1)S(1)} %get-tuple-element.62), channel_id=1, source_target_pairs={{0,2},{1,3},{2,0},{3,1},{4,6},{5,7},{6,4},{7,5},{8,10},{9,11},{10,... | collective-permute-start | bytes 786440 | tf_op jit(solution)/shard_map/ppermute | solution.py:20
  134.7 26.9 %collective-permute-start.31 = (bf16[128,2048]{1,0:T(8,128)(2,1)S(1)}, bf16[128,2048]{1,0:T(8,128)(2,1)S(1)}, u32[]{:S(2)}, u32[]{:S(2)}) collective-permute-start(bf16[128,2048]{1,0:T(8,128)(2,1)S(1)} %collective-permute-done.30.refs_2_), channel_id=1, source_target_pairs={{0,8},{8,0},{16,24},{24,16},{1,9},{9,1},{17,25},{25,17},{2,10},{10... | collective-permute-start | bytes 1572872 | tf_op jit(solution)/shard_map/ppermute | solution.py:20
  134.7 14.2 %collective-permute-start.28 = (bf16[128,1024]{1,0:T(8,128)(2,1)S(1)}, bf16[128,1024]{1,0:T(8,128)(2,1)S(1)}, u32[]{:S(2)}, u32[]{:S(2)}) collective-permute-start(bf16[128,1024]{1,0:T(8,128)(2,1)S(1)} %get-tuple-element.63), channel_id=1, source_target_pairs={{0,4},{1,5},{2,6},{3,7},{4,0},{5,1},{6,2},{7,3},{8,12},{9,13},{10,... | collective-permute-start | bytes 786440 | tf_op jit(solution)/shard_map/ppermute | solution.py:20
  134.7 15.7 %collective-permute-start.20 = (bf16[128,256]{1,0:T(8,128)(2,1)S(1)}, bf16[128,256]{1,0:T(8,128)(2,1)S(1)}, u32[]{:S(2)}, u32[]{:S(2)}) collective-permute-start(bf16[128,256]{1,0:T(8,128)(2,1)S(1)} %get-tuple-element.52), channel_id=1, source_target_pairs={{0,8},{8,0},{16,24},{24,16},{1,9},{9,1},{17,25},{25,17},{2,10},{10... | collective-permute-start | bytes 196616 | tf_op jit(solution)/shard_map/ppermute | solution.py:20
  141.7 19.8 %collective-permute-start.40 = (bf16[256,512]{1,0:T(8,128)(2,1)S(1)}, bf16[256,512]{1,0:T(8,128)(2,1)S(1)}, u32[]{:S(2)}, u32[]{:S(2)}) collective-permute-start(bf16[256,512]{1,0:T(8,128)(2,1)S(1)} %get-tuple-element.71.refs_12_), channel_id=1, source_target_pairs={{0,1},{1,0},{2,3},{3,2},{4,5},{5,4},{6,7},{7,6},{8,9},{9,8},{10,11... | collective-permute-start | bytes 786440 | tf_op jit(solution)/shard_map/ppermute | solution.py:20
  153.9 7.4 %collective-permute-start.33 = (bf16[512,128]{1,0:T(8,128)(2,1)S(1)}, bf16[512,128]{1,0:T(8,128)(2,1)S(1)}, u32[]{:S(2)}, u32[]{:S(2)}) collective-permute-start(bf16[512,128]{1,0:T(8,128)(2,1)S(1)} %get-tuple-element.69), channel_id=1, source_target_pairs={{0,16},{8,24},{16,0},{24,8},{1,17},{9,25},{17,1},{25,9},{2,18},{10... | collective-permute-start | bytes 393224 | tf_op jit(solution)/shard_map/ppermute | solution.py:20
  (18 other events, 188.8 us)

commit v2 on v1

--- a/solution.py
+++ b/solution.py
@@ -26,6 +26,10 @@
         for m in list(got):
             got[m ^ mask] = swapped(got[m], "dp", mask)
     return [got[m] for m in range(len(got))]
+
+
+def exchange(pieces):
+    return [swapped(x, "dp", m) if m else x for m, x in enumerate(pieces)]
 
 
 def total(mine, other):
@@ -160,12 +164,12 @@
     )(*both)
 
 
-def half_kernel(back, near, n, ratio, blk, *refs):
+def half_kernel(back, near, thin, n, dp, ratio, blk, *refs):
     take = iter(refs)
     x_in = [next(take) for _ in range(1 + n)]
     lat_mine, lat_other, up, down, ur, dl = (next(take) for _ in range(6))
     slope_in, lat_down = (next(take), next(take)) if back else (None, None)
-    act_out = next(take)
+    act_outs = [next(take) for _ in range(1 if back else dp)]
     slope_out = None if back else next(take)
     here_out = next(take)
     parts_out = [next(take) for _ in range(n)]
@@ -174,7 +178,9 @@
     lat, up_v, down_v, ur_v, dl_v, slope = (next(take) for _ in range(6))
     act, here = next(take), next(take)
     parts = [next(take) for _ in range(n)]
-    lat_tmp, sem = next(take), next(take)
+    lat_tmp = next(take)
+    lat_slabs = None if back else next(take)
+    sem = next(take)
     rows, width = x_in[0].shape
     blocks = width // blk
     half = lat_mine.shape[0]
@@ -200,8 +206,17 @@
                 late = []
             late.append(copies.start(*right))
         twos.append(copies.start(two[0].at[span], two[1].at[span]))
+    part = blk // dp
+    hidden = blocks * ratio
     for copy in first:
         copy.wait()
+    if not back:
+        for q in range(2 * dp):
+            side, m = divmod(q, dp)
+            lat_slabs[q] = lat[m * part : (m + 1) * part, side * rows : (side + 1) * rows]
+        for z, i in enumerate(thin):
+            for b in range(blocks):
+                act[hidden + z * blocks + b] = xs[1 + i][:, b * blk : (b + 1) * blk].T
     lat_t = (lat[:, rows:] if back else lat[:, :rows]).T
     acc = jnp.zeros((rows, dl.shape[1]), F32)
     here[...] = jnp.zeros_like(here)
@@ -226,7 +241,10 @@
                 slope[:, sl] = 0.5 * (1.0 + th) + 0.5 * v * (1.0 - th * th) * ROOT * (
                     1.0 + 3.0 * CUBIC * v * v
                 )
-            act[:, sl] = y
+            if back:
+                act[:, sl] = y
+            else:
+                act[h] = y.T
             ys.append(y)
         twos[a].wait()
         if a == 0:
@@ -237,8 +255,15 @@
             sl = slice(h * blk, (h + 1) * blk)
             acc = acc + (nt(ys[r], ur_v[:, sl]) if back else nn(ys[r], dl_v[sl, :]))
         if a == blocks - 1:
-            copies.back(act, act_out)
-            if not back:
+            if back:
+                copies.back(act, act_outs[0])
+            else:
+                k, top = lax.axis_index("dp"), act.shape[0]
+                for m, dst in enumerate(act_outs):
+                    to = jnp.bitwise_xor(k, m)
+                    copies.back(act.at[:, cols(to, part), :], dst.at[pl.ds(0, top)])
+                    copies.back(lat_slabs.at[pl.ds(dp, dp)], dst.at[pl.ds(top, dp)])
+                    copies.back(lat_slabs.at[to], dst.at[top + dp])
                 copies.back(slope, slope_out)
         for j in list(range(len(near), len(near) + n)) + list(range(len(near))):
             f = sum(
@@ -264,7 +289,7 @@
     copies.finish()
 
 
-def layer_half(x, far, lat, up, down, ur, dl, near, slope=None, lat_down=None):
+def layer_half(dp, thin, x, far, lat, up, down, ur, dl, near, slope=None, lat_down=None):
     back = slope is not None
     rows, width = x.shape
     hidden, _, blk = up.shape[:3]
@@ -273,93 +298,58 @@
     rank = dl.shape[1]
     n = len(far)
     block, gate, sums = shape((rows, width)), shape((rows, hidden * blk), F32), shape((rows, width), F32)
-    wide = shape((rows, hidden * blk))
-    outs = [wide] + ([] if back else [gate]) + [sums] + [block] * n
+    tall, part = hidden + len(thin) * blocks, blk // dp
+    wide = [shape((rows, hidden * blk))] if back else [shape((tall + dp + 1, part, rows))] * dp
+    outs = wide + ([] if back else [gate]) + [sums] + [block] * n
     outs += [shape((rank // 2, 2 * rows))] * 2 if back else [shape((rank, rows))]
     held = [block] * (1 + n) + [shape((rank, 2 * rows))] + [shape(w.shape) for w in (up, down, ur, dl)]
-    held += [gate, wide, sums] + [block] * n + [shape((rank, rows))]
+    held += [gate, wide[0] if back else shape((tall, blk, rows)), sums] + [block] * n + [shape((rank, rows))] + ([] if back else [shape((2 * dp, part, rows))])
     args = [x, *far, *lat, up, down, ur, dl, *((slope, lat_down) if back else ())]
     return pl.pallas_call(
-        functools.partial(half_kernel, back, near, n, ratio, blk),
+        functools.partial(half_kernel, back, near, thin, n, dp, ratio, blk),
         in_specs=[HBM] * len(args),
         out_specs=[HBM] * len(outs),
         out_shape=outs,
         scratch_shapes=[pltpu.VMEM(h.shape, h.dtype) for h in held]
-        + [pltpu.SemaphoreType.DMA((len(args) + len(outs) + 2 * blocks,))],
+        + [pltpu.SemaphoreType.DMA((len(args) + len(outs) + 2 * blocks + 2 * dp,))],
         compiler_params=params(28),
     )(*args)
 
 
-def select_kernel(n, dp, part, blk, *refs):
-    toks, outs, tmp, sem = refs[:n], refs[n : n + dp], refs[n + dp], refs[n + dp + 1]
-    copies = [pltpu.make_async_copy(t, tmp.at[z], sem.at[z]) for z, t in enumerate(toks)]
-    for c in copies:
-        c.start()
-    blocks = tmp.shape[2] // blk
-    k = lax.axis_index("dp")
-    r = lax.broadcasted_iota(jnp.int32, (blk, blk), 0)
-    c = lax.broadcasted_iota(jnp.int32, (blk, blk), 1)
-    pick = jnp.where(c == jnp.bitwise_xor(r, k * part), 1.0, 0.0).astype(BF16)
-    for z in range(n):
-        copies[z].wait()
-        for b in range(blocks):
-            at = (z * blocks + b) * part
-            out = nt(pick, tmp[z, :, b * blk : (b + 1) * blk]).astype(BF16)
-            for m in range(dp):
-                outs[m][at : at + part, :] = out[m * part : (m + 1) * part]
-
-
-def select_pass(toks, dp, part, blk):
-    rows, width = toks[0].shape
-    n = len(toks)
-    return pl.pallas_call(
-        functools.partial(select_kernel, n, dp, part, blk),
-        in_specs=[HBM] * n,
-        out_specs=[VM] * dp,
-        out_shape=[shape((n * (width // blk) * part, rows))] * dp,
-        scratch_shapes=[pltpu.VMEM((n, rows, width), BF16), pltpu.SemaphoreType.DMA((n,))],
-        compiler_params=params(),
-        name="ks",
-    )(*toks)
-
-
-def cut_kernel(dp, rank_part, *refs):
-    first, second = refs[:2], refs[2:4]
-    outs, whole2, whole1 = refs[4 : 4 + dp], refs[4 + dp], refs[5 + dp]
-    put_halves(whole1, *first)
-    put_halves(whole2, *second)
+def cut_kernel(dp, rank_part, mine, other, *outs):
+    whole = outs[dp]
+    put_halves(whole, mine, other)
     k = lax.axis_index("dp")
     for m in range(dp):
-        rows = cols(jnp.bitwise_xor(k, m), rank_part)
-        outs[m][:rank_part, :] = whole1[rows, :]
-        outs[m][rank_part:, :] = whole2[rows, :]
-
-
-def cut_pass(first, second, dp, rank_part):
-    rank, count = 2 * first[0].shape[0], first[0].shape[1]
+        outs[m][...] = whole[cols(jnp.bitwise_xor(k, m), rank_part), :]
+
+
+def cut_pass(lat, dp, rank_part):
+    rank, count = 2 * lat[0].shape[0], lat[0].shape[1]
     return pl.pallas_call(
         functools.partial(cut_kernel, dp, rank_part),
-        in_specs=[VM] * 4,
+        in_specs=[VM] * 2,
         out_specs=[VM] * (dp + 1),
-        out_shape=[shape((2 * rank_part, count))] * dp + [shape((rank, count))],
-        scratch_shapes=[pltpu.VMEM((rank, count), BF16)],
+        out_shape=[shape((rank_part, count))] * dp + [shape((rank, count))],
         compiler_params=params(),
         name="kc",
-    )(*first, *second)
+    )(*lat)
 
 
 def gather_copies(groups, scratch, sem):
-    made, at = [], 0
+    copies = Copies(sem)
+    made = []
     for refs, dst in zip(groups, scratch):
-        rows = refs[0].shape[0]
-        some = []
-        for m, ref in enumerate(refs):
-            some.append(pltpu.make_async_copy(ref, dst.at[pl.ds(m * rows, rows), :], sem.at[at]))
-            at += 1
-        made.append(some)
-    for some in made:
-        for c in some:
-            c.start()
+        rows, width = refs[0].shape
+        side = dst.shape[0] == rows
+        made.append(
+            [
+                copies.start(
+                    ref, dst.at[:, pl.ds(m * width, width)] if side else dst.at[pl.ds(m * rows, rows), :]
+                )
+                for m, ref in enumerate(refs)
+            ]
+        )
     return made
 
 
@@ -373,7 +363,7 @@
     return [first] + [ref.at[pl.ds(base * rows, rows), :] for ref in both]
 
 
-def down_kernel(near, kinds, dp, ratio, blk, scale, *refs):
+def down_kernel(near, kinds, dp, ratio, blk, rank_part, scale, *refs):
     take = iter(refs)
     tok, cot = next(take), next(take)
     both = [next(take) for _ in range(dp - 1)]
@@ -386,27 +376,44 @@
         else:
             cots.append([next(take) for _ in range(dp)])
     acts = [next(take) for _ in range(dp)]
-    gd, own_rows = next(take), next(take)
+    lats = [next(take) for _ in range(dp)]
+    gd, own_rows, gul, gdr = (next(take) for _ in range(4))
+    gdl = [next(take) for _ in range(dp)]
     tok_all = next(take)
     cot_all = [next(take) for _ in cots]
-    act_all = next(take)
-    made = gather_copies([split_groups(tok, both, 0)] + cots + [acts], [tok_all] + cot_all + [act_all], next(take))
+    act_all, lat_all, gdl_all = (next(take) for _ in range(3))
+    made = gather_copies(
+        [split_groups(tok, both, 0), acts] + cots + [lats], [tok_all, act_all] + cot_all + [lat_all], next(take)
+    )
     blocks = width // blk
-    part = gd.shape[2]
-    pick = one_hot(part, blk, lax.axis_index("dp") * part)
+    hidden, part = gd.shape[0], gd.shape[2]
+    rank = dp * rank_part
+    k = lax.axis_index("dp")
+    pick = one_hot(part, blk, k * part)
     wait_all(made[0])
     for b in range(blocks):
         own_rows[b * part : (b + 1) * part, :] = nt(pick, tok_all[:, b * blk : (b + 1) * blk]).astype(BF16)
-    for some in made[1:]:
+    wait_all(made[1])
+    lat_cot = act_all[act_all.shape[0] - rank - rank_part : act_all.shape[0] - rank_part, :]
+    gdl_all[...] = (nt(lat_cot, act_all[: hidden * part, :]) * scale).astype(BF16)
+    for m in range(dp):
+        gdl[m][...] = gdl_all[cols(jnp.bitwise_xor(k, m), rank_part), :]
+    for some in made[2:]:
         wait_all(some)
+
+    def lat_rows(half):
+        return jnp.concatenate(
+            [
+                lat_all[m * rank_part : (m + 1) * rank_part, half * rows : (half + 1) * rows]
+                for m in range(dp)
+            ],
+            axis=1,
+        )
+
+    gdr[...] = (nn(lat_rows(0), cot_all[0][...]) * scale).astype(BF16)
+    gul[...] = (nn(lat_rows(1), tok_all[...]) * scale).astype(BF16)
     for a in range(blocks):
-        lhs = jnp.concatenate(
-            [
-                nt(pick, act_all[:, (a * ratio + r) * blk : (a * ratio + r + 1) * blk]).astype(BF16)
-                for r in range(ratio)
-            ],
-            axis=0,
-        )
+        lhs = act_all[a * ratio * part : (a + 1) * ratio * part, :]
         srcs = [(0, a ^ s) for s in near] + [(1 + j, a) for j in range(len(kinds))]
         for j, (i, b) in enumerate(srcs):
             out = (nn(lhs, cot_all[i][:, b * blk : (b + 1) * blk]) * scale).astype(BF16)
@@ -418,93 +425,102 @@
     return [pltpu.VMEM(d, t) for d, t in dims] + [pltpu.SemaphoreType.DMA((count,))]
 
 
-def down_pass(tok, cot, both, far, acts, near, part, scale, blk):
+def down_pass(tok, cot, both, far, acts, lats, hidden, near, part, scale, blk):
     dp = len(acts)
     rows, width = tok.shape
-    hid = acts[0].shape[1]
+    rank_part = lats[0].shape[0]
+    count = hidden * part
     kinds = tuple(len(f) == 2 for f in far)
-    args = [tok, cot, *both, *[x for f in far for x in f], *acts]
-    dims = [((dp * rows, width), BF16)] * (2 + len(far)) + [((dp * rows, hid), BF16)]
+    args = [tok, cot, *both, *[x for f in far for x in f], *acts, *lats]
+    dims = [((dp * rows, width), BF16), ((acts[0].shape[0], dp * rows), BF16)]
+    dims = dims[:1] + [((dp * rows, width), BF16)] * (1 + len(far)) + dims[1:]
+    dims += [((dp * rank_part, 2 * rows), BF16), ((dp * rank_part, count), BF16)]
+    wide = shape((rank_part, width))
     return pl.pallas_call(
-        functools.partial(down_kernel, near, kinds, dp, hid // width, blk, scale),
+        functools.partial(down_kernel, near, kinds, dp, hidden * blk // width, blk, rank_part, scale),
         in_specs=[HBM] * len(args),
-        out_specs=[VM] * 2,
-        out_shape=[shape((hid // blk, len(near) + len(far), part, blk)), shape((width // blk * part, dp * rows))],
-        scratch_shapes=stacked(dims, dp * len(dims)),
+        out_specs=[VM] * (4 + dp),
+        out_shape=[
+            shape((hidden, len(near) + len(far), part, blk)),
+            shape((width // blk * part, dp * rows)),
+            wide,
+            wide,
+        ]
+        + [shape((rank_part, count))] * dp,
+        scratch_shapes=stacked(dims, dp * (len(dims) - 1)),
         compiler_params=params(24),
         name="kd",
     )(*args)
 
 
-def rank_kernel(n, dp, rank_part, scale, *refs):
+def rank_kernel(n, dp, blk, *refs):
     take = iter(refs)
-    tok, cot = next(take), next(take)
-    both = [next(take) for _ in range(dp - 1)]
-    acts, lats = ([next(take) for _ in range(dp)] for _ in range(2))
+    pieces = [next(take) for _ in range(dp)]
     singles = [[next(take)] for _ in range(5 + 2 * n)]
-    gdl, gul, gdr, layer_out, token_grads = (next(take) for _ in range(5))
-    groups = [acts, split_groups(tok, both, 0), split_groups(cot, both, 1), lats] + singles
+    gdl, layer_out, token_grads = (next(take) for _ in range(3))
+    groups = [pieces] + singles
     scratch = [next(take) for _ in groups]
     made = gather_copies(groups, scratch, next(take))
-    act_all, tok_all, cot_all, lat_all, out_here, grad_here, dr, ul, lat2 = scratch[:9]
-    rows, _ = tok.shape
-    for some in made:
+    gdl_all, out_here, grad_here, dr, ul, lat2 = scratch[:6]
+    rows = out_here.shape[0]
+    part = blk // dp
+    rank_part, count = pieces[0].shape
+    some = min(count, max(128, part))
+    each = some // part * blk
+    r = lax.broadcasted_iota(jnp.int32, (some, each), 0)
+    c = lax.broadcasted_iota(jnp.int32, (some, each), 1)
+    places = [
+        jnp.where(
+            c == r // part * blk + jnp.bitwise_xor(lax.axis_index("dp"), m) * part + r % part, 1.0, 0.0
+        ).astype(BF16)
+        for m in range(dp)
+    ]
+    wait_all(made[0])
+    for g in range(count // some):
+        out = sum(
+            nn(gdl_all[m * rank_part : (m + 1) * rank_part, g * some : (g + 1) * some], places[m])
+            for m in range(dp)
+        )
+        gdl[:, g * each : (g + 1) * each] = out.astype(BF16)
+    for some in made[1:]:
         wait_all(some)
-
-    def lat_rows(second, half):
-        piece = lat_all.at[:, half * rows : (half + 1) * rows]
-        first = rank_part if second else 0
-        return jnp.concatenate(
-            [piece[2 * rank_part * m + first : 2 * rank_part * m + first + rank_part, :] for m in range(dp)],
-            axis=1,
-        )
-
-    gdl[...] = (nn(lat_rows(False, 1), act_all[...]) * scale).astype(BF16)
-    gdr[...] = (nn(lat_rows(True, 0), cot_all[...]) * scale).astype(BF16)
-    gul[...] = (nn(lat_rows(True, 1), tok_all[...]) * scale).astype(BF16)
     out = out_here[...] + nn(lat2[:, :rows].T, dr[...])
     grad = grad_here[...] + nt(lat2[:, rows:].T, ul[...])
-    for p, q in zip(scratch[9 : 9 + n], scratch[9 + n :]):
+    for p, q in zip(scratch[6 : 6 + n], scratch[6 + n :]):
         out = out + p[...].astype(F32)
         grad = grad + q[...].astype(F32)
     layer_out[...] = out.astype(BF16)
     token_grads[...] = grad.astype(BF16)
 
 
-def rank_pass(tok, cot, both, acts, lats, singles, n, rank_part, scale):
-    dp = len(acts)
-    rows, width = tok.shape
-    hid = acts[0].shape[1]
-    args = [tok, cot, *both, *acts, *lats, *singles]
-    dims = [((dp * rows, hid), BF16)] + [((dp * rows, width), BF16)] * 2
-    dims += [((dp * lats[0].shape[0], lats[0].shape[1]), BF16)] + [(x.shape, x.dtype) for x in singles]
-    wide, full = shape((rank_part, width)), shape((rows, width))
+def rank_pass(pieces, singles, n, blk):
+    dp = len(pieces)
+    rank_part, count = pieces[0].shape
+    args = [*pieces, *singles]
+    dims = [((dp * rank_part, count), BF16)] + [(x.shape, x.dtype) for x in singles]
+    full = shape(singles[0].shape)
     return pl.pallas_call(
-        functools.partial(rank_kernel, n, dp, rank_part, scale),
+        functools.partial(rank_kernel, n, dp, blk),
         in_specs=[HBM] * len(args),
-        out_specs=[VM] * 5,
-        out_shape=[shape((rank_part, hid)), wide, wide, full, full],
-        scratch_shapes=stacked(dims, 4 * dp + len(singles)),
+        out_specs=[VM] * 3,
+        out_shape=[shape((rank_part, count * dp)), full, full],
+        scratch_shapes=stacked(dims, len(args)),
         compiler_params=params(16),
         name="kr",
     )(*args)
 
 
-def up_kernel(near, n_full, n_thin, dp, ratio, blk, rank_part, scale, *refs):
+def up_kernel(near, n_full, n_thin, first, dp, ratio, blk, rank_part, scale, *refs):
     take = iter(refs)
-    pres = [next(take) for _ in range(dp)]
-    lats = [next(take) for _ in range(dp)]
-    thin = [next(take) for _ in range(dp)] if n_thin else []
+    pres, acts = ([next(take) for _ in range(dp)] for _ in range(2))
     full = [[next(take)] for _ in range(1 + n_full)]
     gu, gur = next(take), next(take)
-    groups = [lats] + ([thin] if n_thin else []) + full + [pres]
+    groups = [acts] + full + [pres]
     scratch = [next(take) for _ in groups]
     lhs_all, sem = next(take), next(take)
     made = gather_copies(groups, scratch, sem)
     part = gu.shape[2]
-    rows = pres[0].shape[0]
-    lat_all, pre_all = scratch[0], scratch[-1]
-    full_all = scratch[-2 - n_full : -1]
+    act_all, full_all, pre_all = scratch[0], scratch[1:-1], scratch[-1]
     blocks = full_all[0].shape[0] // part
     count = len(near) + n_full + n_thin
     step = count * part + rank_part
@@ -514,16 +530,9 @@
         pieces = [full_all[0][(a ^ s) * part : ((a ^ s) + 1) * part, :] for s in near]
         pieces += [f[a * part : (a + 1) * part, :] for f in full_all[1:]]
         for j in range(n_thin):
-            at = (j * blocks + a) * part
-            tall = thin[0].shape[0]
-            pieces.append(
-                jnp.concatenate([scratch[1][m * tall + at : m * tall + at + part, :] for m in range(dp)], axis=1)
-            )
-        pieces.append(
-            jnp.concatenate(
-                [lat_all[2 * rank_part * m : 2 * rank_part * m + rank_part, :rows] for m in range(dp)], axis=1
-            )
-        )
+            at = first + (j * blocks + a) * part
+            pieces.append(act_all[at : at + part, :])
+        pieces.append(act_all[act_all.shape[0] - rank_part :, :])
         lhs_all[a * step : (a + 1) * step, :] = jnp.concatenate(pieces, axis=0)
     wait_all(made[-1])
     for a in range(blocks):
@@ -536,18 +545,19 @@
             gur[:, h * blk : (h + 1) * blk] = out[count * part :]
 
 
-def up_pass(pres, lats, thin, n_thin, full, near, part, rank_part, scale, blk):
+def up_pass(pres, acts, n_thin, full, near, part, rank_part, scale, blk):
     dp = len(pres)
     rows, hid = pres[0].shape
     count = len(near) + len(full) - 1 + n_thin
-    thin = list(thin) if n_thin else []
-    args = [*pres, *lats, *thin, *full]
+    args = [*pres, *acts, *full]
     blocks = full[0].shape[0] // part
-    groups = [lats] + ([thin] if n_thin else []) + [[f] for f in full] + [pres]
-    dims = [((len(g) * g[0].shape[0], g[0].shape[1]), BF16) for g in groups]
-    dims.append(((blocks * (count * part + rank_part), dp * rows), BF16))
+    dims = [((acts[0].shape[0], dp * rows), BF16)] + [(f.shape, BF16) for f in full]
+    dims += [((dp * rows, hid), BF16), ((blocks * (count * part + rank_part), dp * rows), BF16)]
+    first = hid // blk * part
     return pl.pallas_call(
-        functools.partial(up_kernel, near, len(full) - 1, n_thin, dp, hid // (blocks * blk), blk, rank_part, scale),
+        functools.partial(
+            up_kernel, near, len(full) - 1, n_thin, first, dp, hid // (blocks * blk), blk, rank_part, scale
+        ),
         in_specs=[HBM] * len(args),
         out_specs=[VM, VM],
         out_shape=[shape((hid // blk, count, part, blk)), shape((rank_part, hid))],
@@ -578,35 +588,33 @@
     *lat_parts, both = latent_pass(tokens, cotangent, up_left, down_right)
     both = spread(both, bits)[1:]
     lat = total(*lat_parts)
-    sent = select_pass([tok_far[i] for i in thin], dp, part, blk) if thin else []
-    thin_groups = [swapped(x, "dp", m) if m else x for m, x in enumerate(sent)]
     others = join_pass(both)
     far = [
-        (cot_far[i], swapped(others, "tensor", m)) if m <= 2 else spread(cot_far[i], flip)
+        (cot_far[i], swapped(others, "tensor", m)) if m <= 2 else spread(cot_far[i], bits)
         for i, m in enumerate(masks)
     ]
 
     weights = (up_blocks, down_blocks, up_right, down_left)
-    made = layer_half(tokens, tok_far, lat, *weights, near)
-    act, slope, out_here, *out_parts, lat_down = made
-    made = layer_half(cotangent, cot_far, lat, *weights, near, slope, lat_down)
+    made = layer_half(dp, tuple(thin), tokens, tok_far, lat, *weights, near)
+    acts, slope, out_here, out_parts, lat_down = made[:dp], made[dp], made[dp + 1], made[dp + 2 : -1], made[-1]
+    made = layer_half(dp, (), cotangent, cot_far, lat, *weights, near, slope, lat_down)
     pre, grad_here, *grad_parts, lat_mine, lat_other = made
     out_parts = [swapped(x, "tensor", m) for x, m in zip(out_parts, masks)]
     grad_parts = [swapped(x, "tensor", m) for x, m in zip(grad_parts, masks)]
-    act_groups = spread(act, bits)
+    act_groups = [x.reshape(-1, rows) for x in exchange(acts)]
     pre_groups = spread(pre, flip)
-    *pieces, lat2 = cut_pass(lat, total(lat_mine, lat_other), dp, rank_part)
-    lat_groups = [swapped(x, "dp", m) if m else x for m, x in enumerate(pieces)]
-
-    gd, own_rows = down_pass(tokens, cotangent, both, far, act_groups, near, part, scale, blk)
-    gdl, gul, gdr, layer_out, token_grads = rank_pass(
-        tokens, cotangent, both, act_groups, lat_groups,
-        [out_here, grad_here, down_right, up_left, lat2, *out_parts, *grad_parts], n, rank_part, scale,
+    *pieces, lat2 = cut_pass(total(lat_mine, lat_other), dp, rank_part)
+    lat2_groups = exchange(pieces)
+
+    hidden = up_blocks.shape[0]
+    gd, own_rows, gul, gdr, *pieces = down_pass(
+        tokens, cotangent, both, far, act_groups, lat2_groups, hidden, near, part, scale, blk
+    )
+    gdl, layer_out, token_grads = rank_pass(
+        exchange(pieces), [out_here, grad_here, down_right, up_left, lat2, *out_parts, *grad_parts], n, blk
     )
     full_rows = [own_rows] + [swapped(own_rows, "tensor", m) for m in masks if m == 1]
-    gu, gur = up_pass(
-        pre_groups, lat_groups, thin_groups, len(thin), full_rows, near, part, rank_part, scale, blk
-    )
+    gu, gur = up_pass(pre_groups, act_groups, len(thin), full_rows, near, part, rank_part, scale, blk)
     return layer_out, token_grads, gu, gd, gul.T, gur, gdl.T, gdr
 
 

time: 166 us -> 156 us (0.940)
  waiting for transfers between devices: 81.8 us -> 69.9 us
  starting transfers between devices: 49 us -> 54.3 us
  Pallas kernels: 32.7 us -> 29.5 us
    ppermute x41, waiting for transfers between devices: 81.8 us -> 69.9 us  [swapped(): lax.ppermute(x, axis, [(i, i ^ mask) for i in range(lax.axis_size(axis))])]
    ppermute x41, starting transfers between devices: 49 us -> 54.3 us  [swapped(): lax.ppermute(x, axis, [(i, i ^ mask) for i in range(lax.axis_size(axis))])]
    pallas_call x5 -> x4, Pallas kernels: 26.9 us -> 24.7 us  [the longest x2 17.1 us: layer_half(): pl.pallas_call(functools.partial(half_kernel, back, near, thin, n, dp, ra...]
where the time goes in v2:
time: 156 us
  waiting for transfers between devices  69.9 us (45%)
  starting transfers between devices  54.3 us (35%)
  Pallas kernels  29.5 us (19%)
    ppermute x41, waiting for transfers between devices, swapped(): lax.ppermute(x, axis, [(i, i ^ mask) for i in range(lax.axis_size(axis))])  69.9 us
    ppermute x41, starting transfers between devices, swapped(): lax.ppermute(x, axis, [(i, i ^ mask) for i in range(lax.axis_size(axis))])  54.3 us
    pallas_call x2, Pallas kernels, layer_half(): pl.pallas_call(functools.partial(half_kernel, back, near, thin, n, dp, ra...  17.1 us
    pallas_call x1, Pallas kernels, down_pass(): pl.pallas_call(functools.partial(down_kernel, near, kinds, dp, hidden * b...  4.57 us
  transfers between devices with their start and end apart: 41, of which 18 were waited for; matrix products, arithmetic and copies ran while one was open for 0% of the time, Pallas kernels for 16%

profile of v2, /device:TPU:0, one launch (start us, length us, event | category | flops | bytes accessed | tf_op | source)
XLA Modules:
  0.0 155.6 jit_solution(16392274374165633646)
XLA Ops:
  0.6 1.8 %kl.1 = (bf16[128,256]{1,0:T(8,128)(2,1)S(1)}, bf16[128,256]{1,0:T(8,128)(2,1)S(1)}, bf16[256,1024]{1,0:T(8,128)(2,1)S(1)}) custom-call(bf16[128,1024]{1,0:T(8,128)(2,1)} %refs_0_.5, bf16[128,1024]{1,0:T(8,128)(2,1)} %refs_1_.1, bf16[1024,256]{1,0:T(8,128)(2,1)} %refs_7_.5, bf16[256,1024]{1,0:T(8,128)(2,1)} %refs_6_.5), custom_call_target="tpu_custom_call" | custom-call | tf_op jit(solution)/shard_map/kl/pallas_call | solution.py:130
  4.0 4.0 %collective-permute-start.15 = (bf16[128,256]{1,0:T(8,128)(2,1)S(1)}, bf16[128,256]{1,0:T(8,128)(2,1)S(1)}, u32[]{:S(2)}, u32[]{:S(2)}) collective-permute-start(bf16[128,256]{1,0:T(8,128)(2,1)S(1)} %add_convert_fusion.5), channel_id=1, source_target_pairs={{0,4},{1,5},{2,6},{3,7},{4,0},{5,1},{6,2},{7,3},{8,12},{9,13},{10,... | collective-permute-start | bytes 196616 | tf_op jit(solution)/shard_map/ppermute | solution.py:20
  8.0 1.8 %collective-permute-start.12 = (bf16[128,1024]{1,0:T(8,128)(2,1)}, bf16[128,1024]{1,0:T(8,128)(2,1)S(1)}, u32[]{:S(2)}, u32[]{:S(2)}) collective-permute-start(bf16[128,1024]{1,0:T(8,128)(2,1)} %refs_0_.5), channel_id=1, source_target_pairs={{0,2},{1,3},{2,0},{3,1},{4,6},{5,7},{6,4},{7,5},{8,10},{9,11},{10,... | collective-permute-start | bytes 786440 | tf_op jit(solution)/shard_map/ppermute | solution.py:20
  9.9 2.2 %collective-permute-done.15 = bf16[128,256]{1,0:T(8,128)(2,1)S(1)} collective-permute-done((bf16[128,256]{1,0:T(8,128)(2,1)S(1)}, bf16[128,256]{1,0:T(8,128)(2,1)S(1)}, u32[]{:S(2)}, u32[]{:S(2)}) %collective-permute-start.15) | collective-permute-done | bytes 65568 | tf_op jit(solution)/shard_map/ppermute | solution.py:20
  12.1 6.1 %collective-permute-start.16 = (bf16[128,256]{1,0:T(8,128)(2,1)S(1)}, bf16[128,256]{1,0:T(8,128)(2,1)S(1)}, u32[]{:S(2)}, u32[]{:S(2)}) collective-permute-start(bf16[128,256]{1,0:T(8,128)(2,1)S(1)} %add_convert_fusion.4), channel_id=1, source_target_pairs={{0,2},{1,3},{2,0},{3,1},{4,6},{5,7},{6,4},{7,5},{8,10},{9,11},{10,... | collective-permute-start | bytes 196616 | tf_op jit(solution)/shard_map/ppermute | solution.py:20
  18.2 3.5 %collective-permute-start.7 = (bf16[128,1024]{1,0:T(8,128)(2,1)}, bf16[128,1024]{1,0:T(8,128)(2,1)S(1)}, u32[]{:S(2)}, u32[]{:S(2)}) collective-permute-start(bf16[128,1024]{1,0:T(8,128)(2,1)} %refs_1_.1), channel_id=1, source_target_pairs={{0,4},{1,5},{2,6},{3,7},{4,0},{5,1},{6,2},{7,3},{8,12},{9,13},{10,... | collective-permute-start | bytes 786440 | tf_op jit(solution)/shard_map/ppermute | solution.py:20
  21.8 4.4 %collective-permute-done.16 = bf16[128,256]{1,0:T(8,128)(2,1)S(1)} collective-permute-done((bf16[128,256]{1,0:T(8,128)(2,1)S(1)}, bf16[128,256]{1,0:T(8,128)(2,1)S(1)}, u32[]{:S(2)}, u32[]{:S(2)}) %collective-permute-start.16) | collective-permute-done | bytes 65568 | tf_op jit(solution)/shard_map/ppermute | solution.py:20
  26.2 1.9 %collective-permute-start = (bf16[256,1024]{1,0:T(8,128)(2,1)S(1)}, bf16[256,1024]{1,0:T(8,128)(2,1)S(1)}, u32[]{:S(2)}, u32[]{:S(2)}) collective-permute-start(bf16[256,1024]{1,0:T(8,128)(2,1)S(1)} %get-tuple-element.46), channel_id=1, source_target_pairs={{0,8},{8,0},{16,24},{24,16},{1,9},{9,1},{17,25},{25,17},{2,10},{10... | collective-permute-start | bytes 1572872 | tf_op jit(solution)/shard_map/ppermute | solution.py:20
  29.5 8.0 %shard_map.143 = (bf16[21,64,128]{2,1,0:T(8,128)(2,1)S(1)}, bf16[21,64,128]{2,1,0:T(8,128)(2,1)S(1)}, bf16[21,64,128]{2,1,0:T(8,128)(2,1)S(1)}, bf16[21,64,128]{...) custom-call(bf16[128,1024]{1,0:T(8,128)(2,1)} %refs_0_.5, ...), custom_call_target="tpu_custom_call" | custom-call | tf_op jit(solution)/shard_map/pallas_call | solution.py:308
  38.6 9.1 %shard_map.144 = (bf16[128,2048]{1,0:T(8,128)(2,1)S(1)}, f32[128,1024]{1,0:T(8,128)S(1)}, bf16[128,1024]{1,0:T(8,128)(2,1)S(1)}, bf16[128,1024]{1,0:T(8,128)(2,1...) custom-call(bf16[128,1024]{1,0:T(8,128)(2,1)} %refs_1_.1, ...), custom_call_target="tpu_custom_call" | custom-call | tf_op jit(solution)/shard_map/pallas_call | solution.py:308
  49.0 2.7 %collective-permute-start.22 = (bf16[128,256]{1,0:T(8,128)(2,1)S(1)}, bf16[128,256]{1,0:T(8,128)(2,1)S(1)}, u32[]{:S(2)}, u32[]{:S(2)}) collective-permute-start(bf16[128,256]{1,0:T(8,128)(2,1)S(1)} %add_convert_fusion.2), channel_id=1, source_target_pairs={{0,4},{1,5},{2,6},{3,7},{4,0},{5,1},{6,2},{7,3},{8,12},{9,13},{10,... | collective-permute-start | bytes 196616 | tf_op jit(solution)/shard_map/ppermute | solution.py:20
  56.7 2.4 %collective-permute-start.23 = (bf16[128,256]{1,0:T(8,128)(2,1)S(1)}, bf16[128,256]{1,0:T(8,128)(2,1)S(1)}, u32[]{:S(2)}, u32[]{:S(2)}) collective-permute-start(bf16[128,256]{1,0:T(8,128)(2,1)S(1)} %add_convert_fusion.1), channel_id=1, source_target_pairs={{0,2},{1,3},{2,0},{3,1},{4,6},{5,7},{6,4},{7,5},{8,10},{9,11},{10,... | collective-permute-start | bytes 196616 | tf_op jit(solution)/shard_map/ppermute | solution.py:20
  59.2 2.2 %collective-permute-done.23 = bf16[128,256]{1,0:T(8,128)(2,1)S(1)} collective-permute-done((bf16[128,256]{1,0:T(8,128)(2,1)S(1)}, bf16[128,256]{1,0:T(8,128)(2,1)S(1)}, u32[]{:S(2)}, u32[]{:S(2)}) %collective-permute-start.23) | collective-permute-done | bytes 65568 | tf_op jit(solution)/shard_map/ppermute | solution.py:20
  61.4 10.7 %collective-permute-done.9.refs_11_ = bf16[128,1024]{1,0:T(8,128)(2,1)S(1)} collective-permute-done((bf16[128,1024]{1,0:T(8,128)(2,1)}, bf16[128,1024]{1,0:T(8,128)(2,1)S(1)}, u32[]{:S(2)}, u32[]{:S(2)}) %collective-permute-start.9) | collective-permute-done | bytes 262176 | tf_op jit(solution)/shard_map/ppermute | solution.py:20
  72.1 2.4 %collective-permute-start.32 = (bf16[128,1024]{1,0:T(8,128)(2,1)S(1)}, bf16[128,1024]{1,0:T(8,128)(2,1)S(1)}, u32[]{:S(2)}, u32[]{:S(2)}) collective-permute-start(bf16[128,1024]{1,0:T(8,128)(2,1)S(1)} %get-tuple-element.69), channel_id=1, source_target_pairs={{0,2},{1,3},{2,0},{3,1},{4,6},{5,7},{6,4},{7,5},{8,10},{9,11},{10,... | collective-permute-start | bytes 786440 | tf_op jit(solution)/shard_map/ppermute | solution.py:20
  74.7 7.6 %collective-permute-done.2.refs_2_.refs_4_ = bf16[256,1024]{1,0:T(8,128)(2,1)S(1)} collective-permute-done((bf16[256,1024]{1,0:T(8,128)(2,1)S(1)}, bf16[256,1024]{1,0:T(8,128)(2,1)S(1)}, u32[]{:S(2)}, u32[]{:S(2)}) %collective-permute-start.2) | collective-permute-done | bytes 524320 | tf_op jit(solution)/shard_map/ppermute | solution.py:20
  83.9 2.4 %collective-permute-start.6 = (bf16[384,1024]{1,0:T(8,128)(2,1)S(1)}, bf16[384,1024]{1,0:T(8,128)(2,1)S(1)}, u32[]{:S(2)}, u32[]{:S(2)}) collective-permute-start(bf16[384,1024]{1,0:T(8,128)(2,1)S(1)} %kj.1), channel_id=1, source_target_pairs={{0,2},{1,3},{2,0},{3,1},{4,6},{5,7},{6,4},{7,5},{8,10},{9,11},{10,... | collective-permute-start | bytes 2359304 | tf_op jit(solution)/shard_map/ppermute | solution.py:20
  88.5 3.4 %collective-permute-done.25.refs_18_ = bf16[64,256]{1,0:T(8,128)(2,1)S(1)} collective-permute-done((bf16[64,256]{1,0:T(8,128)(2,1)S(1)}, bf16[64,256]{1,0:T(8,128)(2,1)S(1)}, u32[]{:S(2)}, u32[]{:S(2)}) %collective-permute-start.25) | collective-permute-done | bytes 32800 | tf_op jit(solution)/shard_map/ppermute | solution.py:20
  93.4 2.4 %collective-permute-done.26.refs_19_ = bf16[64,256]{1,0:T(8,128)(2,1)S(1)} collective-permute-done((bf16[64,256]{1,0:T(8,128)(2,1)S(1)}, bf16[64,256]{1,0:T(8,128)(2,1)S(1)}, u32[]{:S(2)}, u32[]{:S(2)}) %collective-permute-start.26) | collective-permute-done | bytes 32800 | tf_op jit(solution)/shard_map/ppermute | solution.py:20
  95.9 2.4 %collective-permute-start.27 = (bf16[64,256]{1,0:T(8,128)(2,1)S(1)}, bf16[64,256]{1,0:T(8,128)(2,1)S(1)}, u32[]{:S(2)}, u32[]{:S(2)}) collective-permute-start(bf16[64,256]{1,0:T(8,128)(2,1)S(1)} %get-tuple-element.60), channel_id=1, source_target_pairs={{0,24},{8,16},{16,8},{24,0},{1,25},{9,17},{17,9},{25,1},{2,26},{10... | collective-permute-start | bytes 98312 | tf_op jit(solution)/shard_map/ppermute | solution.py:20
  98.3 2.5 %collective-permute-done.27.refs_20_ = bf16[64,256]{1,0:T(8,128)(2,1)S(1)} collective-permute-done((bf16[64,256]{1,0:T(8,128)(2,1)S(1)}, bf16[64,256]{1,0:T(8,128)(2,1)S(1)}, u32[]{:S(2)}, u32[]{:S(2)}) %collective-permute-start.27) | collective-permute-done | bytes 32800 | tf_op jit(solution)/shard_map/ppermute | solution.py:20
  105.2 7.8 %collective-permute-done.20 = bf16[21,64,128]{2,1,0:T(8,128)(2,1)S(1)} collective-permute-done((bf16[21,64,128]{2,1,0:T(8,128)(2,1)S(1)}, bf16[21,64,128]{2,1,0:T(8,128)(2,1)S(1)}, u32[]{:S(2)}, u32[]{:S(2)}) %collective-permute-start.20) | collective-permute-done | bytes 344096 | tf_op jit(solution)/shard_map/ppermute | solution.py:20
  114.5 9.8 %collective-permute-done.10.refs_12_ = bf16[128,1024]{1,0:T(8,128)(2,1)S(1)} collective-permute-done((bf16[128,1024]{1,0:T(8,128)(2,1)S(1)}, bf16[128,1024]{1,0:T(8,128)(2,1)S(1)}, u32[]{:S(2)}, u32[]{:S(2)}) %collective-permute-start.10) | collective-permute-done | bytes 262176 | tf_op jit(solution)/shard_map/ppermute | solution.py:20
  124.3 1.6 %collective-permute-start.39 = (bf16[128,2048]{1,0:T(8,128)(2,1)S(1)}, bf16[128,2048]{1,0:T(8,128)(2,1)S(1)}, u32[]{:S(2)}, u32[]{:S(2)}) collective-permute-start(bf16[128,2048]{1,0:T(8,128)(2,1)S(1)} %collective-permute-done.38.refs_2_), channel_id=1, source_target_pairs={{0,8},{8,0},{16,24},{24,16},{1,9},{9,1},{17,25},{25,17},{2,10},{10... | collective-permute-start | bytes 1572872 | tf_op jit(solution)/shard_map/ppermute | solution.py:20
  125.9 2.4 %collective-permute-start.35 = (bf16[128,1024]{1,0:T(8,128)(2,1)S(1)}, bf16[128,1024]{1,0:T(8,128)(2,1)S(1)}, u32[]{:S(2)}, u32[]{:S(2)}) collective-permute-start(bf16[128,1024]{1,0:T(8,128)(2,1)S(1)} %get-tuple-element.72), channel_id=1, source_target_pairs={{0,2},{1,3},{2,0},{3,1},{4,6},{5,7},{6,4},{7,5},{8,10},{9,11},{10,... | collective-permute-start | bytes 786440 | tf_op jit(solution)/shard_map/ppermute | solution.py:20
  129.0 4.6 %kd.1 = (bf16[8,6,64,256]{3,2,1,0:T(8,128)(2,1)}, bf16[256,512]{1,0:T(8,128)(2,1)S(1)}, bf16[64,1024]{1,0:T(8,128)(2,1)}, bf16[64,1024]{1,0:T(8,128)(2,1)}, bf16...) custom-call(bf16[128,1024]{1,0:T(8,128)(2,1)} %refs_0_.5, ...), custom_call_target="tpu_custom_call" | custom-call | tf_op jit(solution)/shard_map/kd/pallas_call | solution.py:439
  133.6 4.7 %collective-permute-done.35.refs_13_ = bf16[128,1024]{1,0:T(8,128)(2,1)S(1)} collective-permute-done((bf16[128,1024]{1,0:T(8,128)(2,1)S(1)}, bf16[128,1024]{1,0:T(8,128)(2,1)S(1)}, u32[]{:S(2)}, u32[]{:S(2)}) %collective-permute-start.35) | collective-permute-done | bytes 262176 | tf_op jit(solution)/shard_map/ppermute | solution.py:20
  138.9 4.1 %collective-permute-done.36.refs_14_ = bf16[128,1024]{1,0:T(8,128)(2,1)S(1)} collective-permute-done((bf16[128,1024]{1,0:T(8,128)(2,1)S(1)}, bf16[128,1024]{1,0:T(8,128)(2,1)S(1)}, u32[]{:S(2)}, u32[]{:S(2)}) %collective-permute-start.36) | collective-permute-done | bytes 262176 | tf_op jit(solution)/shard_map/ppermute | solution.py:20
  144.9 3.0 %collective-permute-done.29.refs_2_ = bf16[64,512]{1,0:T(8,128)(2,1)S(1)} collective-permute-done((bf16[64,512]{1,0:T(8,128)(2,1)S(1)}, bf16[64,512]{1,0:T(8,128)(2,1)S(1)}, u32[]{:S(2)}, u32[]{:S(2)}) %collective-permute-start.29) | collective-permute-done | bytes 65568 | tf_op jit(solution)/shard_map/ppermute | solution.py:20
  147.9 1.7 %collective-permute-done.30.refs_3_ = bf16[64,512]{1,0:T(8,128)(2,1)S(1)} collective-permute-done((bf16[64,512]{1,0:T(8,128)(2,1)S(1)}, bf16[64,512]{1,0:T(8,128)(2,1)S(1)}, u32[]{:S(2)}, u32[]{:S(2)}) %collective-permute-start.30) | collective-permute-done | bytes 65568 | tf_op jit(solution)/shard_map/ppermute | solution.py:20
  149.6 3.0 %kr.1 = (bf16[64,2048]{1,0:T(8,128)(2,1)}, bf16[128,1024]{1,0:T(8,128)(2,1)}, bf16[128,1024]{1,0:T(8,128)(2,1)}) custom-call(bf16[64,512]{1,0:T(8,128)(2,1)S(1)} %get-tuple-element.61.refs_0_, bf16[64,512]{1,0:T(8,128)(2,1)S(1)} %collective-permute-done.28.refs_1_, bf16[64,512]{1,0:T(8,128)(2,1)S(1)} %collective-permute-done.29.refs_2_, ...), custom_call_target="tpu_custom_call" | custom-call | tf_op jit(solution)/shard_map/kr/pallas_call | solution.py:502
  152.7 2.8 %ku.1 = (bf16[8,6,64,256]{3,2,1,0:T(8,128)(2,1)}, bf16[64,2048]{1,0:T(8,128)(2,1)}) custom-call(bf16[128,2048]{1,0:T(8,128)(2,1)S(1)} %get-tuple-element.76.refs_0_, bf16[128,2048]{1,0:T(8,128)(2,1)S(1)} %collective-permute-done.37.refs_1_, bf16[128,2048]{1,0:T(8,128)(2,1)S(1)} %collective-permute-done.38.refs_2_, ...), custom_call_target="tpu_custom_call" | custom-call | tf_op jit(solution)/shard_map/ku/pallas_call | solution.py:557
  (82 shorter events, 25.2 us)
Async XLA Ops:
  4.0 8.1 %collective-permute-start.15 = (bf16[128,256]{1,0:T(8,128)(2,1)S(1)}, bf16[128,256]{1,0:T(8,128)(2,1)S(1)}, u32[]{:S(2)}, u32[]{:S(2)}) collective-permute-start(bf16[128,256]{1,0:T(8,128)(2,1)S(1)} %add_convert_fusion.5), channel_id=1, source_target_pairs={{0,4},{1,5},{2,6},{3,7},{4,0},{5,1},{6,2},{7,3},{8,12},{9,13},{10,... | collective-permute-start | bytes 196616 | tf_op jit(solution)/shard_map/ppermute | solution.py:20
  8.0 18.2 %collective-permute-start.13 = (bf16[128,1024]{1,0:T(8,128)(2,1)}, bf16[128,1024]{1,0:T(8,128)(2,1)S(1)}, u32[]{:S(2)}, u32[]{:S(2)}) collective-permute-start(bf16[128,1024]{1,0:T(8,128)(2,1)} %refs_0_.5), channel_id=1, source_target_pairs={{0,4},{1,5},{2,6},{3,7},{4,0},{5,1},{6,2},{7,3},{8,12},{9,13},{10,... | collective-permute-start | bytes 786440 | tf_op jit(solution)/shard_map/ppermute | solution.py:20
  8.0 18.2 %collective-permute-start.12 = (bf16[128,1024]{1,0:T(8,128)(2,1)}, bf16[128,1024]{1,0:T(8,128)(2,1)S(1)}, u32[]{:S(2)}, u32[]{:S(2)}) collective-permute-start(bf16[128,1024]{1,0:T(8,128)(2,1)} %refs_0_.5), channel_id=1, source_target_pairs={{0,2},{1,3},{2,0},{3,1},{4,6},{5,7},{6,4},{7,5},{8,10},{9,11},{10,... | collective-permute-start | bytes 786440 | tf_op jit(solution)/shard_map/ppermute | solution.py:20
  12.1 14.0 %collective-permute-start.16 = (bf16[128,256]{1,0:T(8,128)(2,1)S(1)}, bf16[128,256]{1,0:T(8,128)(2,1)S(1)}, u32[]{:S(2)}, u32[]{:S(2)}) collective-permute-start(bf16[128,256]{1,0:T(8,128)(2,1)S(1)} %add_convert_fusion.4), channel_id=1, source_target_pairs={{0,2},{1,3},{2,0},{3,1},{4,6},{5,7},{6,4},{7,5},{8,10},{9,11},{10,... | collective-permute-start | bytes 196616 | tf_op jit(solution)/shard_map/ppermute | solution.py:20
  18.2 9.9 %collective-permute-start.11 = (bf16[128,1024]{1,0:T(8,128)(2,1)}, bf16[128,1024]{1,0:T(8,128)(2,1)S(1)}, u32[]{:S(2)}, u32[]{:S(2)}) collective-permute-start(bf16[128,1024]{1,0:T(8,128)(2,1)} %refs_0_.5), channel_id=1, source_target_pairs={{0,1},{1,0},{2,3},{3,2},{4,5},{5,4},{6,7},{7,6},{8,9},{9,8},{10,11... | collective-permute-start | bytes 786440 | tf_op jit(solution)/shard_map/ppermute | solution.py:20
  18.2 19.3 %collective-permute-start.7 = (bf16[128,1024]{1,0:T(8,128)(2,1)}, bf16[128,1024]{1,0:T(8,128)(2,1)S(1)}, u32[]{:S(2)}, u32[]{:S(2)}) collective-permute-start(bf16[128,1024]{1,0:T(8,128)(2,1)} %refs_1_.1), channel_id=1, source_target_pairs={{0,4},{1,5},{2,6},{3,7},{4,0},{5,1},{6,2},{7,3},{8,12},{9,13},{10,... | collective-permute-start | bytes 786440 | tf_op jit(solution)/shard_map/ppermute | solution.py:20
  26.1 11.6 %collective-permute-start.5 = (bf16[128,1024]{1,0:T(8,128)(2,1)}, bf16[128,1024]{1,0:T(8,128)(2,1)S(1)}, u32[]{:S(2)}, u32[]{:S(2)}) collective-permute-start(bf16[128,1024]{1,0:T(8,128)(2,1)} %refs_1_.1), channel_id=1, source_target_pairs={{0,2},{1,3},{2,0},{3,1},{4,6},{5,7},{6,4},{7,5},{8,10},{9,11},{10,... | collective-permute-start | bytes 786440 | tf_op jit(solution)/shard_map/ppermute | solution.py:20
  26.1 11.6 %collective-permute-start.3 = (bf16[128,1024]{1,0:T(8,128)(2,1)}, bf16[128,1024]{1,0:T(8,128)(2,1)S(1)}, u32[]{:S(2)}, u32[]{:S(2)}) collective-permute-start(bf16[128,1024]{1,0:T(8,128)(2,1)} %refs_1_.1), channel_id=1, source_target_pairs={{0,1},{1,0},{2,3},{3,2},{4,5},{5,4},{6,7},{7,6},{8,9},{9,8},{10,11... | collective-permute-start | bytes 786440 | tf_op jit(solution)/shard_map/ppermute | solution.py:20
  26.2 29.0 %collective-permute-start = (bf16[256,1024]{1,0:T(8,128)(2,1)S(1)}, bf16[256,1024]{1,0:T(8,128)(2,1)S(1)}, u32[]{:S(2)}, u32[]{:S(2)}) collective-permute-start(bf16[256,1024]{1,0:T(8,128)(2,1)S(1)} %get-tuple-element.46), channel_id=1, source_target_pairs={{0,8},{8,0},{16,24},{24,16},{1,9},{9,1},{17,25},{25,17},{2,10},{10... | collective-permute-start | bytes 1572872 | tf_op jit(solution)/shard_map/ppermute | solution.py:20
  49.0 7.7 %collective-permute-start.22 = (bf16[128,256]{1,0:T(8,128)(2,1)S(1)}, bf16[128,256]{1,0:T(8,128)(2,1)S(1)}, u32[]{:S(2)}, u32[]{:S(2)}) collective-permute-start(bf16[128,256]{1,0:T(8,128)(2,1)S(1)} %add_convert_fusion.2), channel_id=1, source_target_pairs={{0,4},{1,5},{2,6},{3,7},{4,0},{5,1},{6,2},{7,3},{8,12},{9,13},{10,... | collective-permute-start | bytes 196616 | tf_op jit(solution)/shard_map/ppermute | solution.py:20
  51.7 22.9 %collective-permute-start.1 = (bf16[256,1024]{1,0:T(8,128)(2,1)S(1)}, bf16[256,1024]{1,0:T(8,128)(2,1)S(1)}, u32[]{:S(2)}, u32[]{:S(2)}) collective-permute-start(bf16[256,1024]{1,0:T(8,128)(2,1)S(1)} %get-tuple-element.46), channel_id=1, source_target_pairs={{0,16},{8,24},{16,0},{24,8},{1,17},{9,25},{17,1},{25,9},{2,18},{10... | collective-permute-start | bytes 1572872 | tf_op jit(solution)/shard_map/ppermute | solution.py:20
  53.2 18.9 %collective-permute-start.9 = (bf16[128,1024]{1,0:T(8,128)(2,1)}, bf16[128,1024]{1,0:T(8,128)(2,1)S(1)}, u32[]{:S(2)}, u32[]{:S(2)}) collective-permute-start(bf16[128,1024]{1,0:T(8,128)(2,1)} %copy-done), channel_id=1, source_target_pairs={{0,16},{8,24},{16,0},{24,8},{1,17},{9,25},{17,1},{25,9},{2,18},{10... | collective-permute-start | bytes 786440 | tf_op jit(solution)/shard_map/ppermute | solution.py:20
  53.7 20.8 %collective-permute-start.8 = (bf16[128,1024]{1,0:T(8,128)(2,1)}, bf16[128,1024]{1,0:T(8,128)(2,1)S(1)}, u32[]{:S(2)}, u32[]{:S(2)}) collective-permute-start(bf16[128,1024]{1,0:T(8,128)(2,1)} %copy-done), channel_id=1, source_target_pairs={{0,8},{8,0},{16,24},{24,16},{1,9},{9,1},{17,25},{25,17},{2,10},{10... | collective-permute-start | bytes 786440 | tf_op jit(solution)/shard_map/ppermute | solution.py:20
  55.2 27.0 %collective-permute-start.2 = (bf16[256,1024]{1,0:T(8,128)(2,1)S(1)}, bf16[256,1024]{1,0:T(8,128)(2,1)S(1)}, u32[]{:S(2)}, u32[]{:S(2)}) collective-permute-start(bf16[256,1024]{1,0:T(8,128)(2,1)S(1)} %collective-permute-done.refs_0_.refs_2_), channel_id=1, source_target_pairs={{0,16},{8,24},{16,0},{24,8},{1,17},{9,25},{17,1},{25,9},{2,18},{10... | collective-permute-start | bytes 1572872 | tf_op jit(solution)/shard_map/ppermute | solution.py:20
  61.4 25.0 %collective-permute-start.31 = (bf16[128,1024]{1,0:T(8,128)(2,1)S(1)}, bf16[128,1024]{1,0:T(8,128)(2,1)S(1)}, u32[]{:S(2)}, u32[]{:S(2)}) collective-permute-start(bf16[128,1024]{1,0:T(8,128)(2,1)S(1)} %get-tuple-element.68), channel_id=1, source_target_pairs={{0,1},{1,0},{2,3},{3,2},{4,5},{5,4},{6,7},{7,6},{8,9},{9,8},{10,11... | collective-permute-start | bytes 786440 | tf_op jit(solution)/shard_map/ppermute | solution.py:20
  72.1 14.9 %collective-permute-start.32 = (bf16[128,1024]{1,0:T(8,128)(2,1)S(1)}, bf16[128,1024]{1,0:T(8,128)(2,1)S(1)}, u32[]{:S(2)}, u32[]{:S(2)}) collective-permute-start(bf16[128,1024]{1,0:T(8,128)(2,1)S(1)} %get-tuple-element.69), channel_id=1, source_target_pairs={{0,2},{1,3},{2,0},{3,1},{4,6},{5,7},{6,4},{7,5},{8,10},{9,11},{10,... | collective-permute-start | bytes 786440 | tf_op jit(solution)/shard_map/ppermute | solution.py:20
  74.5 14.1 %collective-permute-start.33 = (bf16[128,1024]{1,0:T(8,128)(2,1)S(1)}, bf16[128,1024]{1,0:T(8,128)(2,1)S(1)}, u32[]{:S(2)}, u32[]{:S(2)}) collective-permute-start(bf16[128,1024]{1,0:T(8,128)(2,1)S(1)} %get-tuple-element.70), channel_id=1, source_target_pairs={{0,4},{1,5},{2,6},{3,7},{4,0},{5,1},{6,2},{7,3},{8,12},{9,13},{10,... | collective-permute-start | bytes 786440 | tf_op jit(solution)/shard_map/ppermute | solution.py:20
  74.6 9.3 %collective-permute-start.24 = (bf16[128,256]{1,0:T(8,128)(2,1)S(1)}, bf16[128,256]{1,0:T(8,128)(2,1)S(1)}, u32[]{:S(2)}, u32[]{:S(2)}) collective-permute-start(bf16[128,256]{1,0:T(8,128)(2,1)S(1)} %add_convert_fusion.mine), channel_id=1, source_target_pairs={{0,1},{1,0},{2,3},{3,2},{4,5},{5,4},{6,7},{7,6},{8,9},{9,8},{10,11... | collective-permute-start | bytes 196616 | tf_op jit(solution)/shard_map/ppermute | solution.py:20
  82.2 20.1 %collective-permute-start.18 = (bf16[21,64,128]{2,1,0:T(8,128)(2,1)S(1)}, bf16[21,64,128]{2,1,0:T(8,128)(2,1)S(1)}, u32[]{:S(2)}, u32[]{:S(2)}) collective-permute-start(bf16[21,64,128]{2,1,0:T(8,128)(2,1)S(1)} %get-tuple-element.50), channel_id=1, source_target_pairs={{0,8},{8,0},{16,24},{24,16},{1,9},{9,1},{17,25},{25,17},{2,10},{10... | collective-permute-start | bytes 1032200 | tf_op jit(solution)/shard_map/ppermute | solution.py:20
  83.9 42.0 %collective-permute-start.6 = (bf16[384,1024]{1,0:T(8,128)(2,1)S(1)}, bf16[384,1024]{1,0:T(8,128)(2,1)S(1)}, u32[]{:S(2)}, u32[]{:S(2)}) collective-permute-start(bf16[384,1024]{1,0:T(8,128)(2,1)S(1)} %kj.1), channel_id=1, source_target_pairs={{0,2},{1,3},{2,0},{3,1},{4,6},{5,7},{6,4},{7,5},{8,10},{9,11},{10,... | collective-permute-start | bytes 2359304 | tf_op jit(solution)/shard_map/ppermute | solution.py:20
  87.0 16.7 %collective-permute-start.19 = (bf16[21,64,128]{2,1,0:T(8,128)(2,1)S(1)}, bf16[21,64,128]{2,1,0:T(8,128)(2,1)S(1)}, u32[]{:S(2)}, u32[]{:S(2)}) collective-permute-start(bf16[21,64,128]{2,1,0:T(8,128)(2,1)S(1)} %get-tuple-element.51), channel_id=1, source_target_pairs={{0,16},{8,24},{16,0},{24,8},{1,17},{9,25},{17,1},{25,9},{2,18},{10... | collective-permute-start | bytes 1032200 | tf_op jit(solution)/shard_map/ppermute | solution.py:20
  88.5 39.8 %collective-permute-start.4 = (bf16[384,1024]{1,0:T(8,128)(2,1)S(1)}, bf16[384,1024]{1,0:T(8,128)(2,1)S(1)}, u32[]{:S(2)}, u32[]{:S(2)}) collective-permute-start(bf16[384,1024]{1,0:T(8,128)(2,1)S(1)} %kj.1), channel_id=1, source_target_pairs={{0,1},{1,0},{2,3},{3,2},{4,5},{5,4},{6,7},{7,6},{8,9},{9,8},{10,11... | collective-permute-start | bytes 2359304 | tf_op jit(solution)/shard_map/ppermute | solution.py:20
  100.8 23.6 %collective-permute-start.38 = (bf16[128,2048]{1,0:T(8,128)(2,1)S(1)}, bf16[128,2048]{1,0:T(8,128)(2,1)S(1)}, u32[]{:S(2)}, u32[]{:S(2)}) collective-permute-start(bf16[128,2048]{1,0:T(8,128)(2,1)S(1)} %get-tuple-element.76.refs_0_), channel_id=1, source_target_pairs={{0,16},{8,24},{16,0},{24,8},{1,17},{9,25},{17,1},{25,9},{2,18},{10... | collective-permute-start | bytes 1572872 | tf_op jit(solution)/shard_map/ppermute | solution.py:20
  102.3 10.7 %collective-permute-start.20 = (bf16[21,64,128]{2,1,0:T(8,128)(2,1)S(1)}, bf16[21,64,128]{2,1,0:T(8,128)(2,1)S(1)}, u32[]{:S(2)}, u32[]{:S(2)}) collective-permute-start(bf16[21,64,128]{2,1,0:T(8,128)(2,1)S(1)} %get-tuple-element.52), channel_id=1, source_target_pairs={{0,24},{8,16},{16,8},{24,0},{1,25},{9,17},{17,9},{25,1},{2,26},{10... | collective-permute-start | bytes 1032200 | tf_op jit(solution)/shard_map/ppermute | solution.py:20
  103.7 20.6 %collective-permute-start.10 = (bf16[128,1024]{1,0:T(8,128)(2,1)S(1)}, bf16[128,1024]{1,0:T(8,128)(2,1)S(1)}, u32[]{:S(2)}, u32[]{:S(2)}) collective-permute-start(bf16[128,1024]{1,0:T(8,128)(2,1)S(1)} %collective-permute-done.8.refs_10_), channel_id=1, source_target_pairs={{0,16},{8,24},{16,0},{24,8},{1,17},{9,25},{17,1},{25,9},{2,18},{10... | collective-permute-start | bytes 786440 | tf_op jit(solution)/shard_map/ppermute | solution.py:20
  113.0 39.6 %collective-permute-start.37 = (bf16[128,2048]{1,0:T(8,128)(2,1)S(1)}, bf16[128,2048]{1,0:T(8,128)(2,1)S(1)}, u32[]{:S(2)}, u32[]{:S(2)}) collective-permute-start(bf16[128,2048]{1,0:T(8,128)(2,1)S(1)} %get-tuple-element.76.refs_0_), channel_id=1, source_target_pairs={{0,8},{8,0},{16,24},{24,16},{1,9},{9,1},{17,25},{25,17},{2,10},{10... | collective-permute-start | bytes 1572872 | tf_op jit(solution)/shard_map/ppermute | solution.py:20
  124.3 9.2 %collective-permute-start.34 = (bf16[128,1024]{1,0:T(8,128)(2,1)S(1)}, bf16[128,1024]{1,0:T(8,128)(2,1)S(1)}, u32[]{:S(2)}, u32[]{:S(2)}) collective-permute-start(bf16[128,1024]{1,0:T(8,128)(2,1)S(1)} %get-tuple-element.71), channel_id=1, source_target_pairs={{0,1},{1,0},{2,3},{3,2},{4,5},{5,4},{6,7},{7,6},{8,9},{9,8},{10,11... | collective-permute-start | bytes 786440 | tf_op jit(solution)/shard_map/ppermute | solution.py:20
  124.3 28.3 %collective-permute-start.39 = (bf16[128,2048]{1,0:T(8,128)(2,1)S(1)}, bf16[128,2048]{1,0:T(8,128)(2,1)S(1)}, u32[]{:S(2)}, u32[]{:S(2)}) collective-permute-start(bf16[128,2048]{1,0:T(8,128)(2,1)S(1)} %collective-permute-done.38.refs_2_), channel_id=1, source_target_pairs={{0,8},{8,0},{16,24},{24,16},{1,9},{9,1},{17,25},{25,17},{2,10},{10... | collective-permute-start | bytes 1572872 | tf_op jit(solution)/shard_map/ppermute | solution.py:20
  125.9 12.4 %collective-permute-start.35 = (bf16[128,1024]{1,0:T(8,128)(2,1)S(1)}, bf16[128,1024]{1,0:T(8,128)(2,1)S(1)}, u32[]{:S(2)}, u32[]{:S(2)}) collective-permute-start(bf16[128,1024]{1,0:T(8,128)(2,1)S(1)} %get-tuple-element.72), channel_id=1, source_target_pairs={{0,2},{1,3},{2,0},{3,1},{4,6},{5,7},{6,4},{7,5},{8,10},{9,11},{10,... | collective-permute-start | bytes 786440 | tf_op jit(solution)/shard_map/ppermute | solution.py:20
  128.3 14.7 %collective-permute-start.36 = (bf16[128,1024]{1,0:T(8,128)(2,1)S(1)}, bf16[128,1024]{1,0:T(8,128)(2,1)S(1)}, u32[]{:S(2)}, u32[]{:S(2)}) collective-permute-start(bf16[128,1024]{1,0:T(8,128)(2,1)S(1)} %get-tuple-element.73), channel_id=1, source_target_pairs={{0,4},{1,5},{2,6},{3,7},{4,0},{5,1},{6,2},{7,3},{8,12},{9,13},{10,... | collective-permute-start | bytes 786440 | tf_op jit(solution)/shard_map/ppermute | solution.py:20
  133.6 19.1 %collective-permute-start.40 = (bf16[256,512]{1,0:T(8,128)(2,1)S(1)}, bf16[256,512]{1,0:T(8,128)(2,1)S(1)}, u32[]{:S(2)}, u32[]{:S(2)}) collective-permute-start(bf16[256,512]{1,0:T(8,128)(2,1)S(1)} %get-tuple-element.77.refs_8_), channel_id=1, source_target_pairs={{0,1},{1,0},{2,3},{3,2},{4,5},{5,4},{6,7},{7,6},{8,9},{9,8},{10,11... | collective-permute-start | bytes 786440 | tf_op jit(solution)/shard_map/ppermute | solution.py:20
  138.3 6.1 %collective-permute-start.28 = (bf16[64,512]{1,0:T(8,128)(2,1)S(1)}, bf16[64,512]{1,0:T(8,128)(2,1)S(1)}, u32[]{:S(2)}, u32[]{:S(2)}) collective-permute-start(bf16[64,512]{1,0:T(8,128)(2,1)S(1)} %get-tuple-element.62), channel_id=1, source_target_pairs={{0,8},{8,0},{16,24},{24,16},{1,9},{9,1},{17,25},{25,17},{2,10},{10... | collective-permute-start | bytes 196616 | tf_op jit(solution)/shard_map/ppermute | solution.py:20
  (18 other events, 159.5 us)

commit v3 on v2

--- a/solution.py
+++ b/solution.py
@@ -93,6 +93,11 @@
 
 def shape(dims, dtype=BF16):
     return jax.ShapeDtypeStruct(dims, dtype)
+
+
+def wait_all(some):
+    for c in some:
+        c.wait()
 
 
 class Copies:
@@ -191,21 +196,22 @@
 
     first = [lat_half(src, c) for src, c in zip((lat_mine, lat_other), halves())]
     first += [copies.start(src, dst) for src, dst in zip(x_in, xs)]
-    left, right = ((dl, dl_v), (ur, ur_v)) if back else ((ur, ur_v), (dl, dl_v))
-    first.append(copies.start(*left))
     one, two = ((down, down_v), (up, up_v)) if back else ((up, up_v), (down, down_v))
     ones, twos = [], []
+    if not back:
+        first.append(copies.start(ur, ur_v))
     for a in range(blocks):
         span = pl.ds(a * ratio, ratio)
-        ones.append(copies.start(one[0].at[span], one[1].at[span]))
+        now = []
+        if back:
+            piece = pl.ds(a * ratio * blk, ratio * blk)
+            now = [copies.start(dl.at[piece, :], dl_v.at[piece, :]), copies.start(slope_in.at[a], slope.at[a])]
+        ones.append(now + [copies.start(one[0].at[span], one[1].at[span])])
+        rest = []
         if a == 0:
-            if back:
-                first.append(copies.start(slope_in, slope))
-                late = [copies.start(lat_down, lat_tmp)]
-            else:
-                late = []
-            late.append(copies.start(*right))
-        twos.append(copies.start(two[0].at[span], two[1].at[span]))
+            rest.append(copies.start(ur, ur_v) if back else copies.start(dl, dl_v))
+        twos.append(rest + [copies.start(two[0].at[span], two[1].at[span])])
+    late = [copies.start(lat_down, lat_tmp)] if back else []
     part = blk // dp
     hidden = blocks * ratio
     for copy in first:
@@ -224,7 +230,7 @@
         own = slice(a * blk, (a + 1) * blk)
         at = [slice((a ^ s) * blk, ((a ^ s) + 1) * blk) for s in near]
         pieces = [xs[0][:, c] for c in at] + [x[:, own] for x in xs[1:]]
-        ones[a].wait()
+        wait_all(ones[a])
         ys = []
         for r in range(ratio):
             h = a * ratio + r
@@ -233,23 +239,21 @@
                 g = nt(lat_t, dl_v[sl, :])
                 for j, piece in enumerate(pieces):
                     g = g + nt(piece, down_v[h, j])
-                y = (g * slope[:, sl]).astype(BF16)
+                y = (g * slope[a, :, r * blk : (r + 1) * blk].astype(F32)).astype(BF16)
             else:
                 v = nn(lat_t, ur_v[:, sl]) + nn(jnp.concatenate(pieces, axis=1), up_v[h].reshape(-1, blk))
                 th = jnp.tanh(ROOT * (v + CUBIC * v * v * v))
                 y = (0.5 * v * (1.0 + th)).astype(BF16)
-                slope[:, sl] = 0.5 * (1.0 + th) + 0.5 * v * (1.0 - th * th) * ROOT * (
-                    1.0 + 3.0 * CUBIC * v * v
-                )
+                slope[a, :, r * blk : (r + 1) * blk] = (
+                    0.5 * (1.0 + th)
+                    + 0.5 * v * (1.0 - th * th) * ROOT * (1.0 + 3.0 * CUBIC * v * v)
+                ).astype(BF16)
             if back:
                 act[:, sl] = y
             else:
                 act[h] = y.T
             ys.append(y)
-        twos[a].wait()
-        if a == 0:
-            for copy in late:
-                copy.wait()
+        wait_all(twos[a])
         for r in range(ratio):
             h = a * ratio + r
             sl = slice(h * blk, (h + 1) * blk)
@@ -278,6 +282,7 @@
             for src, dst in zip(parts, parts_out):
                 copies.back(src, dst)
     copies.back(here, here_out)
+    wait_all(late)
     if back:
         lat[:, :rows] = lat_tmp[...]
         lat[:, rows:] = acc.T.astype(BF16)
@@ -297,7 +302,7 @@
     ratio = hidden // blocks
     rank = dl.shape[1]
     n = len(far)
-    block, gate, sums = shape((rows, width)), shape((rows, hidden * blk), F32), shape((rows, width), F32)
+    block, gate, sums = shape((rows, width)), shape((blocks, rows, ratio * blk)), shape((rows, width), F32)
     tall, part = hidden + len(thin) * blocks, blk // dp
     wide = [shape((rows, hidden * blk))] if back else [shape((tall + dp + 1, part, rows))] * dp
     outs = wide + ([] if back else [gate]) + [sums] + [block] * n
@@ -311,29 +316,9 @@
         out_specs=[HBM] * len(outs),
         out_shape=outs,
         scratch_shapes=[pltpu.VMEM(h.shape, h.dtype) for h in held]
-        + [pltpu.SemaphoreType.DMA((len(args) + len(outs) + 2 * blocks + 2 * dp,))],
+        + [pltpu.SemaphoreType.DMA((len(args) + len(outs) + 4 * blocks + 2 * dp,))],
         compiler_params=params(28),
     )(*args)
-
-
-def cut_kernel(dp, rank_part, mine, other, *outs):
-    whole = outs[dp]
-    put_halves(whole, mine, other)
-    k = lax.axis_index("dp")
-    for m in range(dp):
-        outs[m][...] = whole[cols(jnp.bitwise_xor(k, m), rank_part), :]
-
-
-def cut_pass(lat, dp, rank_part):
-    rank, count = 2 * lat[0].shape[0], lat[0].shape[1]
-    return pl.pallas_call(
-        functools.partial(cut_kernel, dp, rank_part),
-        in_specs=[VM] * 2,
-        out_specs=[VM] * (dp + 1),
-        out_shape=[shape((rank_part, count))] * dp + [shape((rank, count))],
-        compiler_params=params(),
-        name="kc",
-    )(*lat)
 
 
 def gather_copies(groups, scratch, sem):
@@ -353,11 +338,6 @@
     return made
 
 
-def wait_all(some):
-    for c in some:
-        c.wait()
-
-
 def split_groups(first, both, base):
     rows = first.shape[0]
     return [first] + [ref.at[pl.ds(base * rows, rows), :] for ref in both]
@@ -378,27 +358,21 @@
     acts = [next(take) for _ in range(dp)]
     lats = [next(take) for _ in range(dp)]
     gd, own_rows, gul, gdr = (next(take) for _ in range(4))
-    gdl = [next(take) for _ in range(dp)]
+    lats = [ref.at[:, pl.ds(0, 2 * rows)] for ref in lats]
     tok_all = next(take)
     cot_all = [next(take) for _ in cots]
-    act_all, lat_all, gdl_all = (next(take) for _ in range(3))
+    act_all, lat_all = next(take), next(take)
     made = gather_copies(
         [split_groups(tok, both, 0), acts] + cots + [lats], [tok_all, act_all] + cot_all + [lat_all], next(take)
     )
     blocks = width // blk
-    hidden, part = gd.shape[0], gd.shape[2]
-    rank = dp * rank_part
+    part = gd.shape[2]
     k = lax.axis_index("dp")
     pick = one_hot(part, blk, k * part)
     wait_all(made[0])
     for b in range(blocks):
         own_rows[b * part : (b + 1) * part, :] = nt(pick, tok_all[:, b * blk : (b + 1) * blk]).astype(BF16)
-    wait_all(made[1])
-    lat_cot = act_all[act_all.shape[0] - rank - rank_part : act_all.shape[0] - rank_part, :]
-    gdl_all[...] = (nt(lat_cot, act_all[: hidden * part, :]) * scale).astype(BF16)
-    for m in range(dp):
-        gdl[m][...] = gdl_all[cols(jnp.bitwise_xor(k, m), rank_part), :]
-    for some in made[2:]:
+    for some in made[1:]:
         wait_all(some)
 
     def lat_rows(half):
@@ -425,29 +399,58 @@
     return [pltpu.VMEM(d, t) for d, t in dims] + [pltpu.SemaphoreType.DMA((count,))]
 
 
+def cut_kernel(dp, count, scale, *refs):
+    mine, other, acts, outs, whole = refs[0], refs[1], refs[2 : 2 + dp], refs[2 + dp : 2 + 2 * dp], refs[2 + 2 * dp]
+    act_all, out_all, sem = refs[3 + 2 * dp :]
+    rank_part, width = outs[0].shape
+    made = gather_copies([acts], [act_all], sem)
+    put_halves(whole, mine, other)
+    wait_all(made[0])
+    tall = act_all.shape[0]
+    lat_cot = act_all[tall - (dp + 1) * rank_part : tall - rank_part, :]
+    out_all[...] = (nt(lat_cot, act_all[:count, :]) * scale).astype(BF16)
+    for m in range(dp):
+        rows = cols(jnp.bitwise_xor(lax.axis_index("dp"), m), rank_part)
+        outs[m][:, : width - count] = whole[rows, :]
+        outs[m][:, width - count :] = out_all[rows, :]
+
+
+def cut_pass(lat, acts, count, rank_part, scale):
+    dp, rank = len(acts), 2 * lat[0].shape[0]
+    tall, rows = acts[0].shape
+    piece = shape((rank_part, 2 * rows + count))
+    return pl.pallas_call(
+        functools.partial(cut_kernel, dp, count, scale),
+        in_specs=[VM] * 2 + [HBM] * dp,
+        out_specs=[VM] * (dp + 1),
+        out_shape=[piece] * dp + [shape((rank, 2 * rows))],
+        scratch_shapes=stacked([((tall, dp * rows), BF16), ((rank, count), BF16)], dp),
+        compiler_params=params(),
+        name="kc",
+    )(*lat, *acts)
+
+
 def down_pass(tok, cot, both, far, acts, lats, hidden, near, part, scale, blk):
     dp = len(acts)
     rows, width = tok.shape
     rank_part = lats[0].shape[0]
-    count = hidden * part
     kinds = tuple(len(f) == 2 for f in far)
     args = [tok, cot, *both, *[x for f in far for x in f], *acts, *lats]
     dims = [((dp * rows, width), BF16), ((acts[0].shape[0], dp * rows), BF16)]
     dims = dims[:1] + [((dp * rows, width), BF16)] * (1 + len(far)) + dims[1:]
-    dims += [((dp * rank_part, 2 * rows), BF16), ((dp * rank_part, count), BF16)]
+    dims += [((dp * rank_part, 2 * rows), BF16)]
     wide = shape((rank_part, width))
     return pl.pallas_call(
         functools.partial(down_kernel, near, kinds, dp, hidden * blk // width, blk, rank_part, scale),
         in_specs=[HBM] * len(args),
-        out_specs=[VM] * (4 + dp),
+        out_specs=[VM] * 4,
         out_shape=[
             shape((hidden, len(near) + len(far), part, blk)),
             shape((width // blk * part, dp * rows)),
             wide,
             wide,
-        ]
-        + [shape((rank_part, count))] * dp,
-        scratch_shapes=stacked(dims, dp * (len(dims) - 1)),
+        ],
+        scratch_shapes=stacked(dims, dp * len(dims)),
         compiler_params=params(24),
         name="kd",
     )(*args)
@@ -458,13 +461,14 @@
     pieces = [next(take) for _ in range(dp)]
     singles = [[next(take)] for _ in range(5 + 2 * n)]
     gdl, layer_out, token_grads = (next(take) for _ in range(3))
-    groups = [pieces] + singles
+    count = gdl.shape[1] // dp
+    groups = [[ref.at[:, pl.ds(ref.shape[1] - count, count)] for ref in pieces]] + singles
     scratch = [next(take) for _ in groups]
     made = gather_copies(groups, scratch, next(take))
     gdl_all, out_here, grad_here, dr, ul, lat2 = scratch[:6]
     rows = out_here.shape[0]
     part = blk // dp
-    rank_part, count = pieces[0].shape
+    rank_part = pieces[0].shape[0]
     some = min(count, max(128, part))
     each = some // part * blk
     r = lax.broadcasted_iota(jnp.int32, (some, each), 0)
@@ -493,9 +497,8 @@
     token_grads[...] = grad.astype(BF16)
 
 
-def rank_pass(pieces, singles, n, blk):
-    dp = len(pieces)
-    rank_part, count = pieces[0].shape
+def rank_pass(pieces, singles, n, count, blk):
+    dp, rank_part = len(pieces), pieces[0].shape[0]
     args = [*pieces, *singles]
     dims = [((dp * rank_part, count), BF16)] + [(x.shape, x.dtype) for x in singles]
     full = shape(singles[0].shape)
@@ -603,15 +606,14 @@
     grad_parts = [swapped(x, "tensor", m) for x, m in zip(grad_parts, masks)]
     act_groups = [x.reshape(-1, rows) for x in exchange(acts)]
     pre_groups = spread(pre, flip)
-    *pieces, lat2 = cut_pass(total(lat_mine, lat_other), dp, rank_part)
-    lat2_groups = exchange(pieces)
-
     hidden = up_blocks.shape[0]
-    gd, own_rows, gul, gdr, *pieces = down_pass(
-        tokens, cotangent, both, far, act_groups, lat2_groups, hidden, near, part, scale, blk
+    *pieces, lat2 = cut_pass(total(lat_mine, lat_other), act_groups, hidden * part, rank_part, scale)
+    pieces = exchange(pieces)
+    gd, own_rows, gul, gdr = down_pass(
+        tokens, cotangent, both, far, act_groups, pieces, hidden, near, part, scale, blk
     )
     gdl, layer_out, token_grads = rank_pass(
-        exchange(pieces), [out_here, grad_here, down_right, up_left, lat2, *out_parts, *grad_parts], n, blk
+        pieces, [out_here, grad_here, down_right, up_left, lat2, *out_parts, *grad_parts], n, hidden * part, blk
     )
     full_rows = [own_rows] + [swapped(own_rows, "tensor", m) for m in masks if m == 1]
     gu, gur = up_pass(pre_groups, act_groups, len(thin), full_rows, near, part, rank_part, scale, blk)

time: 156 us -> 154 us (0.987)
  starting transfers between devices: 54.3 us -> 37.1 us
  waiting for transfers between devices: 69.9 us -> 84.2 us
    ppermute x41 -> x38, starting transfers between devices: 54.3 us -> 37.1 us  [swapped(): lax.ppermute(x, axis, [(i, i ^ mask) for i in range(lax.axis_size(axis))])]
    ppermute x41 -> x38, waiting for transfers between devices: 69.9 us -> 84.2 us  [swapped(): lax.ppermute(x, axis, [(i, i ^ mask) for i in range(lax.axis_size(axis))])]
  transfers between devices with their start and end apart: 41 -> 38, of which waited for: 18 -> 16; matrix products, arithmetic and copies ran while one was open for 0% -> 0% of each run, Pallas kernels for 16% -> 10%
where the time goes in v3:
time: 154 us; the launch traced here: 153 us
  waiting for transfers between devices  84.2 us (55%)
  starting transfers between devices  37.1 us (24%)
  Pallas kernels  29.4 us (19%)
    ppermute x38, waiting for transfers between devices, swapped(): lax.ppermute(x, axis, [(i, i ^ mask) for i in range(lax.axis_size(axis))])  84.2 us
    ppermute x38, starting transfers between devices, swapped(): lax.ppermute(x, axis, [(i, i ^ mask) for i in range(lax.axis_size(axis))])  37.1 us
    pallas_call x2, Pallas kernels, layer_half(): pl.pallas_call(functools.partial(half_kernel, back, near, thin, n, dp, ra...  17 us
    pallas_call x1, Pallas kernels, down_pass(): pl.pallas_call(functools.partial(down_kernel, near, kinds, dp, hidden * b...  4.41 us
  transfers between devices with their start and end apart: 38, of which 16 were waited for; matrix products, arithmetic and copies ran while one was open for 0% of the time, Pallas kernels for 10%

profile of v3, /device:TPU:0, one launch (start us, length us, event | category | flops | bytes accessed | tf_op | source)
XLA Modules:
  0.0 153.3 jit_solution(4954657069728535596)
XLA Ops:
  0.6 1.8 %kl.1 = (bf16[128,256]{1,0:T(8,128)(2,1)S(1)}, bf16[128,256]{1,0:T(8,128)(2,1)S(1)}, bf16[256,1024]{1,0:T(8,128)(2,1)S(1)}) custom-call(bf16[128,1024]{1,0:T(8,128)(2,1)} %refs_0_.5, bf16[128,1024]{1,0:T(8,128)(2,1)} %refs_1_.1, bf16[1024,256]{1,0:T(8,128)(2,1)} %refs_7_.5, bf16[256,1024]{1,0:T(8,128)(2,1)} %refs_6_.5), custom_call_target="tpu_custom_call" | custom-call | tf_op jit(solution)/shard_map/kl/pallas_call | solution.py:135
  4.0 4.0 %collective-permute-start.4 = (bf16[128,256]{1,0:T(8,128)(2,1)S(1)}, bf16[128,256]{1,0:T(8,128)(2,1)S(1)}, u32[]{:S(2)}, u32[]{:S(2)}) collective-permute-start(bf16[128,256]{1,0:T(8,128)(2,1)S(1)} %add_convert_fusion.5), channel_id=1, source_target_pairs={{0,4},{1,5},{2,6},{3,7},{4,0},{5,1},{6,2},{7,3},{8,12},{9,13},{10,... | collective-permute-start | bytes 196616 | tf_op jit(solution)/shard_map/ppermute | solution.py:20
  8.0 3.8 %collective-permute-done.4 = bf16[128,256]{1,0:T(8,128)(2,1)S(1)} collective-permute-done((bf16[128,256]{1,0:T(8,128)(2,1)S(1)}, bf16[128,256]{1,0:T(8,128)(2,1)S(1)}, u32[]{:S(2)}, u32[]{:S(2)}) %collective-permute-start.4) | collective-permute-done | bytes 65568 | tf_op jit(solution)/shard_map/ppermute | solution.py:20
  12.6 3.5 %collective-permute-done.5 = bf16[128,256]{1,0:T(8,128)(2,1)S(1)} collective-permute-done((bf16[128,256]{1,0:T(8,128)(2,1)S(1)}, bf16[128,256]{1,0:T(8,128)(2,1)S(1)}, u32[]{:S(2)}, u32[]{:S(2)}) %collective-permute-start.5) | collective-permute-done | bytes 65568 | tf_op jit(solution)/shard_map/ppermute | solution.py:20
  17.0 3.4 %collective-permute-start.9 = (bf16[128,1024]{1,0:T(8,128)(2,1)}, bf16[128,1024]{1,0:T(8,128)(2,1)S(1)}, u32[]{:S(2)}, u32[]{:S(2)}) collective-permute-start(bf16[128,1024]{1,0:T(8,128)(2,1)} %refs_0_.5), channel_id=1, source_target_pairs={{0,4},{1,5},{2,6},{3,7},{4,0},{5,1},{6,2},{7,3},{8,12},{9,13},{10,... | collective-permute-start | bytes 786440 | tf_op jit(solution)/shard_map/ppermute | solution.py:20
  21.6 9.5 %collective-permute-done.8.refs_2_ = bf16[128,1024]{1,0:T(8,128)(2,1)S(1)} collective-permute-done((bf16[128,1024]{1,0:T(8,128)(2,1)}, bf16[128,1024]{1,0:T(8,128)(2,1)S(1)}, u32[]{:S(2)}, u32[]{:S(2)}) %collective-permute-start.8) | collective-permute-done | bytes 262176 | tf_op jit(solution)/shard_map/ppermute | solution.py:20
  31.0 2.5 %collective-permute-done.9.refs_3_ = bf16[128,1024]{1,0:T(8,128)(2,1)S(1)} collective-permute-done((bf16[128,1024]{1,0:T(8,128)(2,1)}, bf16[128,1024]{1,0:T(8,128)(2,1)S(1)}, u32[]{:S(2)}, u32[]{:S(2)}) %collective-permute-start.9) | collective-permute-done | bytes 262176 | tf_op jit(solution)/shard_map/ppermute | solution.py:20
  34.3 8.0 %shard_map.143 = (bf16[21,64,128]{2,1,0:T(8,128)(2,1)S(1)}, bf16[21,64,128]{2,1,0:T(8,128)(2,1)S(1)}, bf16[21,64,128]{2,1,0:T(8,128)(2,1)S(1)}, bf16[21,64,128]{...) custom-call(bf16[128,1024]{1,0:T(8,128)(2,1)} %refs_0_.5, ...), custom_call_target="tpu_custom_call" | custom-call | tf_op jit(solution)/shard_map/pallas_call | solution.py:313
  42.3 1.9 %collective-permute-done.2.refs_3_.refs_9_ = bf16[128,1024]{1,0:T(8,128)(2,1)S(1)} collective-permute-done((bf16[128,1024]{1,0:T(8,128)(2,1)}, bf16[128,1024]{1,0:T(8,128)(2,1)S(1)}, u32[]{:S(2)}, u32[]{:S(2)}) %collective-permute-start.2) | collective-permute-done | bytes 262176 | tf_op jit(solution)/shard_map/ppermute | solution.py:20
  44.9 8.9 %shard_map.144 = (bf16[128,2048]{1,0:T(8,128)(2,1)S(1)}, f32[128,1024]{1,0:T(8,128)S(1)}, bf16[128,1024]{1,0:T(8,128)(2,1)S(1)}, bf16[128,1024]{1,0:T(8,128)(2,1...) custom-call(bf16[128,1024]{1,0:T(8,128)(2,1)} %refs_1_.1, ...), custom_call_target="tpu_custom_call" | custom-call | tf_op jit(solution)/shard_map/pallas_call | solution.py:313
  53.9 1.5 %collective-permute-start.29 = (bf16[256,1024]{1,0:T(8,128)(2,1)S(1)}, bf16[256,1024]{1,0:T(8,128)(2,1)S(1)}, u32[]{:S(2)}, u32[]{:S(2)}) collective-permute-start(bf16[256,1024]{1,0:T(8,128)(2,1)S(1)} %get-tuple-element.68), channel_id=1, source_target_pairs={{0,8},{8,0},{16,24},{24,16},{1,9},{9,1},{17,25},{25,17},{2,10},{10... | collective-permute-start | bytes 1572872 | tf_op jit(solution)/shard_map/ppermute | solution.py:20
  55.6 1.6 %collective-permute-start.30 = (bf16[256,1024]{1,0:T(8,128)(2,1)S(1)}, bf16[256,1024]{1,0:T(8,128)(2,1)S(1)}, u32[]{:S(2)}, u32[]{:S(2)}) collective-permute-start(bf16[256,1024]{1,0:T(8,128)(2,1)S(1)} %get-tuple-element.68), channel_id=1, source_target_pairs={{0,16},{8,24},{16,0},{24,8},{1,17},{9,25},{17,1},{25,9},{2,18},{10... | collective-permute-start | bytes 1572872 | tf_op jit(solution)/shard_map/ppermute | solution.py:20
  57.2 4.6 %collective-permute-done.11 = bf16[128,256]{1,0:T(8,128)(2,1)S(1)} collective-permute-done((bf16[128,256]{1,0:T(8,128)(2,1)S(1)}, bf16[128,256]{1,0:T(8,128)(2,1)S(1)}, u32[]{:S(2)}, u32[]{:S(2)}) %collective-permute-start.11) | collective-permute-done | bytes 65568 | tf_op jit(solution)/shard_map/ppermute | solution.py:20
  61.9 1.9 %collective-permute-start.21 = (bf16[128,1024]{1,0:T(8,128)(2,1)S(1)}, bf16[128,1024]{1,0:T(8,128)(2,1)S(1)}, u32[]{:S(2)}, u32[]{:S(2)}) collective-permute-start(bf16[128,1024]{1,0:T(8,128)(2,1)S(1)} %get-tuple-element.60), channel_id=1, source_target_pairs={{0,2},{1,3},{2,0},{3,1},{4,6},{5,7},{6,4},{7,5},{8,10},{9,11},{10,... | collective-permute-start | bytes 786440 | tf_op jit(solution)/shard_map/ppermute | solution.py:20
  63.9 4.4 %collective-permute-done.29.refs_0_.refs_2_ = bf16[256,1024]{1,0:T(8,128)(2,1)S(1)} collective-permute-done((bf16[256,1024]{1,0:T(8,128)(2,1)S(1)}, bf16[256,1024]{1,0:T(8,128)(2,1)S(1)}, u32[]{:S(2)}, u32[]{:S(2)}) %collective-permute-start.29) | collective-permute-done | bytes 524320 | tf_op jit(solution)/shard_map/ppermute | solution.py:20
  68.3 1.5 collective-permute-start.31
  73.1 1.5 collective-permute-start.16
  74.7 15.7 %collective-permute-done.31.refs_2_.refs_4_ = bf16[256,1024]{1,0:T(8,128)(2,1)S(1)} collective-permute-done((bf16[256,1024]{1,0:T(8,128)(2,1)S(1)}, bf16[256,1024]{1,0:T(8,128)(2,1)S(1)}, u32[]{:S(2)}, u32[]{:S(2)}) %collective-permute-start.31) | collective-permute-done | bytes 524320 | tf_op jit(solution)/shard_map/ppermute | solution.py:20
  93.4 3.0 %collective-permute-done.15 = bf16[21,64,128]{2,1,0:T(8,128)(2,1)S(1)} collective-permute-done((bf16[21,64,128]{2,1,0:T(8,128)(2,1)S(1)}, bf16[21,64,128]{2,1,0:T(8,128)(2,1)S(1)}, u32[]{:S(2)}, u32[]{:S(2)}) %collective-permute-start.15) | collective-permute-done | bytes 344096 | tf_op jit(solution)/shard_map/ppermute | solution.py:20
  96.4 1.5 collective-permute-start.27
  99.0 1.5 %collective-permute-start.17 = (bf16[64,768]{1,0:T(8,128)(2,1)S(1)}, bf16[64,768]{1,0:T(8,128)(2,1)S(1)}, u32[]{:S(2)}, u32[]{:S(2)}) collective-permute-start(bf16[64,768]{1,0:T(8,128)(2,1)S(1)} %get-tuple-element.53), channel_id=1, source_target_pairs={{0,8},{8,0},{16,24},{24,16},{1,9},{9,1},{17,25},{25,17},{2,10},{10... | collective-permute-start | bytes 294920 | tf_op jit(solution)/shard_map/ppermute | solution.py:20
  100.6 14.0 %collective-permute-done.35.refs_11_ = bf16[128,1024]{1,0:T(8,128)(2,1)S(1)} collective-permute-done((bf16[128,1024]{1,0:T(8,128)(2,1)}, bf16[128,1024]{1,0:T(8,128)(2,1)S(1)}, u32[]{:S(2)}, u32[]{:S(2)}) %collective-permute-start.35) | collective-permute-done | bytes 262176 | tf_op jit(solution)/shard_map/ppermute | solution.py:20
  114.6 1.5 collective-permute-start.36
  116.6 6.1 %collective-permute-done.18.refs_2_.refs_19_ = bf16[64,768]{1,0:T(8,128)(2,1)S(1)} collective-permute-done((bf16[64,768]{1,0:T(8,128)(2,1)S(1)}, bf16[64,768]{1,0:T(8,128)(2,1)S(1)}, u32[]{:S(2)}, u32[]{:S(2)}) %collective-permute-start.18) | collective-permute-done | bytes 98336 | tf_op jit(solution)/shard_map/ppermute | solution.py:20
  122.8 2.4 %collective-permute-start.19 = (bf16[64,768]{1,0:T(8,128)(2,1)S(1)}, bf16[64,768]{1,0:T(8,128)(2,1)S(1)}, u32[]{:S(2)}, u32[]{:S(2)}) collective-permute-start(bf16[64,768]{1,0:T(8,128)(2,1)S(1)} %get-tuple-element.55), channel_id=1, source_target_pairs={{0,24},{8,16},{16,8},{24,0},{1,25},{9,17},{17,9},{25,1},{2,26},{10... | collective-permute-start | bytes 294920 | tf_op jit(solution)/shard_map/ppermute | solution.py:20
  125.2 3.7 %collective-permute-done.19.refs_3_.refs_20_ = bf16[64,768]{1,0:T(8,128)(2,1)S(1)} collective-permute-done((bf16[64,768]{1,0:T(8,128)(2,1)S(1)}, bf16[64,768]{1,0:T(8,128)(2,1)S(1)}, u32[]{:S(2)}, u32[]{:S(2)}) %collective-permute-start.19) | collective-permute-done | bytes 98336 | tf_op jit(solution)/shard_map/ppermute | solution.py:20
  131.0 2.0 %collective-permute-start.24 = (bf16[128,1024]{1,0:T(8,128)(2,1)S(1)}, bf16[128,1024]{1,0:T(8,128)(2,1)S(1)}, u32[]{:S(2)}, u32[]{:S(2)}) collective-permute-start(bf16[128,1024]{1,0:T(8,128)(2,1)S(1)} %get-tuple-element.63), channel_id=1, source_target_pairs={{0,2},{1,3},{2,0},{3,1},{4,6},{5,7},{6,4},{7,5},{8,10},{9,11},{10,... | collective-permute-start | bytes 786440 | tf_op jit(solution)/shard_map/ppermute | solution.py:20
  133.9 4.4 %kd.1 = (bf16[8,6,64,256]{3,2,1,0:T(8,128)(2,1)}, bf16[256,512]{1,0:T(8,128)(2,1)S(1)}, bf16[64,1024]{1,0:T(8,128)(2,1)}, bf16[64,1024]{1,0:T(8,128)(2,1)}) custom-call(bf16[128,1024]{1,0:T(8,128)(2,1)} %refs_0_.5, bf16[128,1024]{1,0:T(8,128)(2,1)} %refs_1_.1, bf16[256,1024]{1,0:T(8,128)(2,1)S(1)} %collective-permute-done.29.refs_0_.refs_2_, ...), custom_call_target="tpu_custom_call" | custom-call | tf_op jit(solution)/shard_map/kd/pallas_call | solution.py:443
  138.4 5.8 %collective-permute-done.24.refs_13_ = bf16[128,1024]{1,0:T(8,128)(2,1)S(1)} collective-permute-done((bf16[128,1024]{1,0:T(8,128)(2,1)S(1)}, bf16[128,1024]{1,0:T(8,128)(2,1)S(1)}, u32[]{:S(2)}, u32[]{:S(2)}) %collective-permute-start.24) | collective-permute-done | bytes 262176 | tf_op jit(solution)/shard_map/ppermute | solution.py:20
  144.1 3.5 %collective-permute-done.25.refs_14_ = bf16[128,1024]{1,0:T(8,128)(2,1)S(1)} collective-permute-done((bf16[128,1024]{1,0:T(8,128)(2,1)S(1)}, bf16[128,1024]{1,0:T(8,128)(2,1)S(1)}, u32[]{:S(2)}, u32[]{:S(2)}) %collective-permute-start.25) | collective-permute-done | bytes 262176 | tf_op jit(solution)/shard_map/ppermute | solution.py:20
  147.7 2.7 %kr.1 = (bf16[64,2048]{1,0:T(8,128)(2,1)}, bf16[128,1024]{1,0:T(8,128)(2,1)}, bf16[128,1024]{1,0:T(8,128)(2,1)}) custom-call(bf16[64,768]{1,0:T(8,128)(2,1)S(1)} %get-tuple-element.52.refs_0_.refs_17_, bf16[64,768]{1,0:T(8,128)(2,1)S(1)} %collective-permute-done.17.refs_1_.refs_18_, bf16[64,768]{1,0:T(8,128)(2,1)S(1)} %collective-permute-done.18.refs_2_.refs_19_, ...), custom_call_target="tpu_custom_call" | custom-call | tf_op jit(solution)/shard_map/kr/pallas_call | solution.py:505
  150.4 2.8 %ku.1 = (bf16[8,6,64,256]{3,2,1,0:T(8,128)(2,1)}, bf16[64,2048]{1,0:T(8,128)(2,1)}) custom-call(bf16[128,2048]{1,0:T(8,128)(2,1)S(1)} %get-tuple-element.67.refs_0_, bf16[128,2048]{1,0:T(8,128)(2,1)S(1)} %collective-permute-done.26.refs_1_, bf16[128,2048]{1,0:T(8,128)(2,1)S(1)} %collective-permute-done.27.refs_2_, ...), custom_call_target="tpu_custom_call" | custom-call | tf_op jit(solution)/shard_map/ku/pallas_call | solution.py:560
  (76 shorter events, 17.1 us)
Async XLA Ops:
  4.0 7.8 %collective-permute-start.4 = (bf16[128,256]{1,0:T(8,128)(2,1)S(1)}, bf16[128,256]{1,0:T(8,128)(2,1)S(1)}, u32[]{:S(2)}, u32[]{:S(2)}) collective-permute-start(bf16[128,256]{1,0:T(8,128)(2,1)S(1)} %add_convert_fusion.5), channel_id=1, source_target_pairs={{0,4},{1,5},{2,6},{3,7},{4,0},{5,1},{6,2},{7,3},{8,12},{9,13},{10,... | collective-permute-start | bytes 196616 | tf_op jit(solution)/shard_map/ppermute | solution.py:20
  12.6 8.0 %collective-permute-start.7 = (bf16[128,1024]{1,0:T(8,128)(2,1)}, bf16[128,1024]{1,0:T(8,128)(2,1)S(1)}, u32[]{:S(2)}, u32[]{:S(2)}) collective-permute-start(bf16[128,1024]{1,0:T(8,128)(2,1)} %refs_0_.5), channel_id=1, source_target_pairs={{0,1},{1,0},{2,3},{3,2},{4,5},{5,4},{6,7},{7,6},{8,9},{9,8},{10,11... | collective-permute-start | bytes 786440 | tf_op jit(solution)/shard_map/ppermute | solution.py:20
  16.2 14.8 %collective-permute-start.8 = (bf16[128,1024]{1,0:T(8,128)(2,1)}, bf16[128,1024]{1,0:T(8,128)(2,1)S(1)}, u32[]{:S(2)}, u32[]{:S(2)}) collective-permute-start(bf16[128,1024]{1,0:T(8,128)(2,1)} %refs_0_.5), channel_id=1, source_target_pairs={{0,2},{1,3},{2,0},{3,1},{4,6},{5,7},{6,4},{7,5},{8,10},{9,11},{10,... | collective-permute-start | bytes 786440 | tf_op jit(solution)/shard_map/ppermute | solution.py:20
  17.0 16.5 %collective-permute-start.9 = (bf16[128,1024]{1,0:T(8,128)(2,1)}, bf16[128,1024]{1,0:T(8,128)(2,1)S(1)}, u32[]{:S(2)}, u32[]{:S(2)}) collective-permute-start(bf16[128,1024]{1,0:T(8,128)(2,1)} %refs_0_.5), channel_id=1, source_target_pairs={{0,4},{1,5},{2,6},{3,7},{4,0},{5,1},{6,2},{7,3},{8,12},{9,13},{10,... | collective-permute-start | bytes 786440 | tf_op jit(solution)/shard_map/ppermute | solution.py:20
  20.4 21.9 %collective-permute-start = (bf16[128,1024]{1,0:T(8,128)(2,1)}, bf16[128,1024]{1,0:T(8,128)(2,1)S(1)}, u32[]{:S(2)}, u32[]{:S(2)}) collective-permute-start(bf16[128,1024]{1,0:T(8,128)(2,1)} %refs_1_.1), channel_id=1, source_target_pairs={{0,1},{1,0},{2,3},{3,2},{4,5},{5,4},{6,7},{7,6},{8,9},{9,8},{10,11... | collective-permute-start | bytes 786440 | tf_op jit(solution)/shard_map/ppermute | solution.py:20
  20.4 21.9 %collective-permute-start.1 = (bf16[128,1024]{1,0:T(8,128)(2,1)}, bf16[128,1024]{1,0:T(8,128)(2,1)S(1)}, u32[]{:S(2)}, u32[]{:S(2)}) collective-permute-start(bf16[128,1024]{1,0:T(8,128)(2,1)} %refs_1_.1), channel_id=1, source_target_pairs={{0,2},{1,3},{2,0},{3,1},{4,6},{5,7},{6,4},{7,5},{8,10},{9,11},{10,... | collective-permute-start | bytes 786440 | tf_op jit(solution)/shard_map/ppermute | solution.py:20
  20.6 23.6 %collective-permute-start.2 = (bf16[128,1024]{1,0:T(8,128)(2,1)}, bf16[128,1024]{1,0:T(8,128)(2,1)S(1)}, u32[]{:S(2)}, u32[]{:S(2)}) collective-permute-start(bf16[128,1024]{1,0:T(8,128)(2,1)} %refs_1_.1), channel_id=1, source_target_pairs={{0,4},{1,5},{2,6},{3,7},{4,0},{5,1},{6,2},{7,3},{8,12},{9,13},{10,... | collective-permute-start | bytes 786440 | tf_op jit(solution)/shard_map/ppermute | solution.py:20
  53.9 14.3 %collective-permute-start.29 = (bf16[256,1024]{1,0:T(8,128)(2,1)S(1)}, bf16[256,1024]{1,0:T(8,128)(2,1)S(1)}, u32[]{:S(2)}, u32[]{:S(2)}) collective-permute-start(bf16[256,1024]{1,0:T(8,128)(2,1)S(1)} %get-tuple-element.68), channel_id=1, source_target_pairs={{0,8},{8,0},{16,24},{24,16},{1,9},{9,1},{17,25},{25,17},{2,10},{10... | collective-permute-start | bytes 1572872 | tf_op jit(solution)/shard_map/ppermute | solution.py:20
  55.5 6.3 %collective-permute-start.11 = (bf16[128,256]{1,0:T(8,128)(2,1)S(1)}, bf16[128,256]{1,0:T(8,128)(2,1)S(1)}, u32[]{:S(2)}, u32[]{:S(2)}) collective-permute-start(bf16[128,256]{1,0:T(8,128)(2,1)S(1)} %add_convert_fusion.2), channel_id=1, source_target_pairs={{0,4},{1,5},{2,6},{3,7},{4,0},{5,1},{6,2},{7,3},{8,12},{9,13},{10,... | collective-permute-start | bytes 196616 | tf_op jit(solution)/shard_map/ppermute | solution.py:20
  55.6 19.0 %collective-permute-start.30 = (bf16[256,1024]{1,0:T(8,128)(2,1)S(1)}, bf16[256,1024]{1,0:T(8,128)(2,1)S(1)}, u32[]{:S(2)}, u32[]{:S(2)}) collective-permute-start(bf16[256,1024]{1,0:T(8,128)(2,1)S(1)} %get-tuple-element.68), channel_id=1, source_target_pairs={{0,16},{8,24},{16,0},{24,8},{1,17},{9,25},{17,1},{25,9},{2,18},{10... | collective-permute-start | bytes 1572872 | tf_op jit(solution)/shard_map/ppermute | solution.py:20
  61.8 8.0 %collective-permute-start.12 = (bf16[128,256]{1,0:T(8,128)(2,1)S(1)}, bf16[128,256]{1,0:T(8,128)(2,1)S(1)}, u32[]{:S(2)}, u32[]{:S(2)}) collective-permute-start(bf16[128,256]{1,0:T(8,128)(2,1)S(1)} %add_convert_fusion.1), channel_id=1, source_target_pairs={{0,2},{1,3},{2,0},{3,1},{4,6},{5,7},{6,4},{7,5},{8,10},{9,11},{10,... | collective-permute-start | bytes 196616 | tf_op jit(solution)/shard_map/ppermute | solution.py:20
  61.9 10.8 %collective-permute-start.20 = (bf16[128,1024]{1,0:T(8,128)(2,1)S(1)}, bf16[128,1024]{1,0:T(8,128)(2,1)S(1)}, u32[]{:S(2)}, u32[]{:S(2)}) collective-permute-start(bf16[128,1024]{1,0:T(8,128)(2,1)S(1)} %get-tuple-element.59), channel_id=1, source_target_pairs={{0,1},{1,0},{2,3},{3,2},{4,5},{5,4},{6,7},{7,6},{8,9},{9,8},{10,11... | collective-permute-start | bytes 786440 | tf_op jit(solution)/shard_map/ppermute | solution.py:20
  61.9 11.2 %collective-permute-start.21 = (bf16[128,1024]{1,0:T(8,128)(2,1)S(1)}, bf16[128,1024]{1,0:T(8,128)(2,1)S(1)}, u32[]{:S(2)}, u32[]{:S(2)}) collective-permute-start(bf16[128,1024]{1,0:T(8,128)(2,1)S(1)} %get-tuple-element.60), channel_id=1, source_target_pairs={{0,2},{1,3},{2,0},{3,1},{4,6},{5,7},{6,4},{7,5},{8,10},{9,11},{10,... | collective-permute-start | bytes 786440 | tf_op jit(solution)/shard_map/ppermute | solution.py:20
  68.3 22.2 %collective-permute-start.31 = (bf16[256,1024]{1,0:T(8,128)(2,1)S(1)}, bf16[256,1024]{1,0:T(8,128)(2,1)S(1)}, u32[]{:S(2)}, u32[]{:S(2)}) collective-permute-start(bf16[256,1024]{1,0:T(8,128)(2,1)S(1)} %collective-permute-done.29.refs_0_.refs_2_), channel_id=1, source_target_pairs={{0,16},{8,24},{16,0},{24,8},{1,17},{9,25},{17,1},{25,9},{2,18},{10... | collective-permute-start | bytes 1572872 | tf_op jit(solution)/shard_map/ppermute | solution.py:20
  71.1 21.1 %collective-permute-start.14 = (bf16[21,64,128]{2,1,0:T(8,128)(2,1)S(1)}, bf16[21,64,128]{2,1,0:T(8,128)(2,1)S(1)}, u32[]{:S(2)}, u32[]{:S(2)}) collective-permute-start(bf16[21,64,128]{2,1,0:T(8,128)(2,1)S(1)} %get-tuple-element.49), channel_id=1, source_target_pairs={{0,8},{8,0},{16,24},{24,16},{1,9},{9,1},{17,25},{25,17},{2,10},{10... | collective-permute-start | bytes 1032200 | tf_op jit(solution)/shard_map/ppermute | solution.py:20
  72.6 23.8 %collective-permute-start.15 = (bf16[21,64,128]{2,1,0:T(8,128)(2,1)S(1)}, bf16[21,64,128]{2,1,0:T(8,128)(2,1)S(1)}, u32[]{:S(2)}, u32[]{:S(2)}) collective-permute-start(bf16[21,64,128]{2,1,0:T(8,128)(2,1)S(1)} %get-tuple-element.50), channel_id=1, source_target_pairs={{0,16},{8,24},{16,0},{24,8},{1,17},{9,25},{17,1},{25,9},{2,18},{10... | collective-permute-start | bytes 1032200 | tf_op jit(solution)/shard_map/ppermute | solution.py:20
  73.1 24.8 %collective-permute-start.16 = (bf16[21,64,128]{2,1,0:T(8,128)(2,1)S(1)}, bf16[21,64,128]{2,1,0:T(8,128)(2,1)S(1)}, u32[]{:S(2)}, u32[]{:S(2)}) collective-permute-start(bf16[21,64,128]{2,1,0:T(8,128)(2,1)S(1)} %get-tuple-element.51), channel_id=1, source_target_pairs={{0,24},{8,16},{16,8},{24,0},{1,25},{9,17},{17,9},{25,1},{2,26},{10... | collective-permute-start | bytes 1032200 | tf_op jit(solution)/shard_map/ppermute | solution.py:20
  74.6 17.5 %collective-permute-start.22 = (bf16[128,1024]{1,0:T(8,128)(2,1)S(1)}, bf16[128,1024]{1,0:T(8,128)(2,1)S(1)}, u32[]{:S(2)}, u32[]{:S(2)}) collective-permute-start(bf16[128,1024]{1,0:T(8,128)(2,1)S(1)} %get-tuple-element.61), channel_id=1, source_target_pairs={{0,4},{1,5},{2,6},{3,7},{4,0},{5,1},{6,2},{7,3},{8,12},{9,13},{10,... | collective-permute-start | bytes 786440 | tf_op jit(solution)/shard_map/ppermute | solution.py:20
  90.4 8.6 %collective-permute-start.34 = (bf16[128,1024]{1,0:T(8,128)(2,1)}, bf16[128,1024]{1,0:T(8,128)(2,1)S(1)}, u32[]{:S(2)}, u32[]{:S(2)}) collective-permute-start(bf16[128,1024]{1,0:T(8,128)(2,1)} %copy-done.2), channel_id=1, source_target_pairs={{0,8},{8,0},{16,24},{24,16},{1,9},{9,1},{17,25},{25,17},{2,10},{10... | collective-permute-start | bytes 786440 | tf_op jit(solution)/shard_map/ppermute | solution.py:20
  92.1 38.9 %collective-permute-start.32 = (bf16[384,1024]{1,0:T(8,128)(2,1)S(1)}, bf16[384,1024]{1,0:T(8,128)(2,1)S(1)}, u32[]{:S(2)}, u32[]{:S(2)}) collective-permute-start(bf16[384,1024]{1,0:T(8,128)(2,1)S(1)} %kj.1), channel_id=1, source_target_pairs={{0,1},{1,0},{2,3},{3,2},{4,5},{5,4},{6,7},{7,6},{8,9},{9,8},{10,11... | collective-permute-start | bytes 2359304 | tf_op jit(solution)/shard_map/ppermute | solution.py:20
  92.2 40.8 %collective-permute-start.33 = (bf16[384,1024]{1,0:T(8,128)(2,1)S(1)}, bf16[384,1024]{1,0:T(8,128)(2,1)S(1)}, u32[]{:S(2)}, u32[]{:S(2)}) collective-permute-start(bf16[384,1024]{1,0:T(8,128)(2,1)S(1)} %kj.1), channel_id=1, source_target_pairs={{0,2},{1,3},{2,0},{3,1},{4,6},{5,7},{6,4},{7,5},{8,10},{9,11},{10,... | collective-permute-start | bytes 2359304 | tf_op jit(solution)/shard_map/ppermute | solution.py:20
  96.4 33.9 %collective-permute-start.27 = (bf16[128,2048]{1,0:T(8,128)(2,1)S(1)}, bf16[128,2048]{1,0:T(8,128)(2,1)S(1)}, u32[]{:S(2)}, u32[]{:S(2)}) collective-permute-start(bf16[128,2048]{1,0:T(8,128)(2,1)S(1)} %get-tuple-element.67.refs_0_), channel_id=1, source_target_pairs={{0,16},{8,24},{16,0},{24,8},{1,17},{9,25},{17,1},{25,9},{2,18},{10... | collective-permute-start | bytes 1572872 | tf_op jit(solution)/shard_map/ppermute | solution.py:20
  97.9 16.6 %collective-permute-start.35 = (bf16[128,1024]{1,0:T(8,128)(2,1)}, bf16[128,1024]{1,0:T(8,128)(2,1)S(1)}, u32[]{:S(2)}, u32[]{:S(2)}) collective-permute-start(bf16[128,1024]{1,0:T(8,128)(2,1)} %copy-done.2), channel_id=1, source_target_pairs={{0,16},{8,24},{16,0},{24,8},{1,17},{9,25},{17,1},{25,9},{2,18},{10... | collective-permute-start | bytes 786440 | tf_op jit(solution)/shard_map/ppermute | solution.py:20
  99.0 17.1 %collective-permute-start.17 = (bf16[64,768]{1,0:T(8,128)(2,1)S(1)}, bf16[64,768]{1,0:T(8,128)(2,1)S(1)}, u32[]{:S(2)}, u32[]{:S(2)}) collective-permute-start(bf16[64,768]{1,0:T(8,128)(2,1)S(1)} %get-tuple-element.53), channel_id=1, source_target_pairs={{0,8},{8,0},{16,24},{24,16},{1,9},{9,1},{17,25},{25,17},{2,10},{10... | collective-permute-start | bytes 294920 | tf_op jit(solution)/shard_map/ppermute | solution.py:20
  114.6 15.8 %collective-permute-start.36 = (bf16[128,1024]{1,0:T(8,128)(2,1)S(1)}, bf16[128,1024]{1,0:T(8,128)(2,1)S(1)}, u32[]{:S(2)}, u32[]{:S(2)}) collective-permute-start(bf16[128,1024]{1,0:T(8,128)(2,1)S(1)} %collective-permute-done.34.refs_10_), channel_id=1, source_target_pairs={{0,16},{8,24},{16,0},{24,8},{1,17},{9,25},{17,1},{25,9},{2,18},{10... | collective-permute-start | bytes 786440 | tf_op jit(solution)/shard_map/ppermute | solution.py:20
  116.1 6.7 %collective-permute-start.18 = (bf16[64,768]{1,0:T(8,128)(2,1)S(1)}, bf16[64,768]{1,0:T(8,128)(2,1)S(1)}, u32[]{:S(2)}, u32[]{:S(2)}) collective-permute-start(bf16[64,768]{1,0:T(8,128)(2,1)S(1)} %get-tuple-element.54), channel_id=1, source_target_pairs={{0,16},{8,24},{16,0},{24,8},{1,17},{9,25},{17,1},{25,9},{2,18},{10... | collective-permute-start | bytes 294920 | tf_op jit(solution)/shard_map/ppermute | solution.py:20
  128.9 21.5 %collective-permute-start.26 = (bf16[128,2048]{1,0:T(8,128)(2,1)S(1)}, bf16[128,2048]{1,0:T(8,128)(2,1)S(1)}, u32[]{:S(2)}, u32[]{:S(2)}) collective-permute-start(bf16[128,2048]{1,0:T(8,128)(2,1)S(1)} %get-tuple-element.67.refs_0_), channel_id=1, source_target_pairs={{0,8},{8,0},{16,24},{24,16},{1,9},{9,1},{17,25},{25,17},{2,10},{10... | collective-permute-start | bytes 1572872 | tf_op jit(solution)/shard_map/ppermute | solution.py:20
  130.3 8.0 %collective-permute-start.23 = (bf16[128,1024]{1,0:T(8,128)(2,1)S(1)}, bf16[128,1024]{1,0:T(8,128)(2,1)S(1)}, u32[]{:S(2)}, u32[]{:S(2)}) collective-permute-start(bf16[128,1024]{1,0:T(8,128)(2,1)S(1)} %get-tuple-element.62), channel_id=1, source_target_pairs={{0,1},{1,0},{2,3},{3,2},{4,5},{5,4},{6,7},{7,6},{8,9},{9,8},{10,11... | collective-permute-start | bytes 786440 | tf_op jit(solution)/shard_map/ppermute | solution.py:20
  130.4 20.0 %collective-permute-start.28 = (bf16[128,2048]{1,0:T(8,128)(2,1)S(1)}, bf16[128,2048]{1,0:T(8,128)(2,1)S(1)}, u32[]{:S(2)}, u32[]{:S(2)}) collective-permute-start(bf16[128,2048]{1,0:T(8,128)(2,1)S(1)} %collective-permute-done.27.refs_2_), channel_id=1, source_target_pairs={{0,8},{8,0},{16,24},{24,16},{1,9},{9,1},{17,25},{25,17},{2,10},{10... | collective-permute-start | bytes 1572872 | tf_op jit(solution)/shard_map/ppermute | solution.py:20
  131.0 13.2 %collective-permute-start.24 = (bf16[128,1024]{1,0:T(8,128)(2,1)S(1)}, bf16[128,1024]{1,0:T(8,128)(2,1)S(1)}, u32[]{:S(2)}, u32[]{:S(2)}) collective-permute-start(bf16[128,1024]{1,0:T(8,128)(2,1)S(1)} %get-tuple-element.63), channel_id=1, source_target_pairs={{0,2},{1,3},{2,0},{3,1},{4,6},{5,7},{6,4},{7,5},{8,10},{9,11},{10,... | collective-permute-start | bytes 786440 | tf_op jit(solution)/shard_map/ppermute | solution.py:20
  133.0 14.6 %collective-permute-start.25 = (bf16[128,1024]{1,0:T(8,128)(2,1)S(1)}, bf16[128,1024]{1,0:T(8,128)(2,1)S(1)}, u32[]{:S(2)}, u32[]{:S(2)}) collective-permute-start(bf16[128,1024]{1,0:T(8,128)(2,1)S(1)} %get-tuple-element.64), channel_id=1, source_target_pairs={{0,4},{1,5},{2,6},{3,7},{4,0},{5,1},{6,2},{7,3},{8,12},{9,13},{10,... | collective-permute-start | bytes 786440 | tf_op jit(solution)/shard_map/ppermute | solution.py:20
  138.3 12.1 %collective-permute-start.37 = (bf16[256,512]{1,0:T(8,128)(2,1)S(1)}, bf16[256,512]{1,0:T(8,128)(2,1)S(1)}, u32[]{:S(2)}, u32[]{:S(2)}) collective-permute-start(bf16[256,512]{1,0:T(8,128)(2,1)S(1)} %get-tuple-element.69.refs_8_), channel_id=1, source_target_pairs={{0,1},{1,0},{2,3},{3,2},{4,5},{5,4},{6,7},{7,6},{8,9},{9,8},{10,11... | collective-permute-start | bytes 786440 | tf_op jit(solution)/shard_map/ppermute | solution.py:20
  (15 other events, 97.5 us)
